TPU v7x, 512 devices: a whole 4x4x16 slice. The times are simulated.
512 devices in a mesh: row: 16 (over z_lo, core), col: 16 (over y, x), gz: 2 (over z_hi).
Axes of the slice: x: 4, y: 4, z: 16 (z_hi: 2, z_lo: 8; z = z_hi * 8 + z_lo), core: 2. Of those that a mesh axis runs over, the one named last changes fastest.
Arguments:
- modes: bfloat16 [64, 96, 32, 3, 2048], P('row', 'col', 'gz'), may hold values from -0.109375 to 0.109375
- blocks: float32 [8, 7, 3, 3], replicated, may hold values from -6 to 6
- material: int32 [64, 96, 32], P('row', 'col', 'gz'), may hold values from 0 to 7
Outputs:
- reduced: float32 [2048, 256], P('col')
All inputs are finite; a program needn't handle non-finite values.
Results may differ from a plain program's by a relative error of at most 0.0029.
Values may be sent and summed in bfloat16 or wider, within the bound.
No kernel may reach another device: no remote copies, remote signals or barrier semaphores. Data moves between devices by JAX's collectives and lax.ppermute only.
A program may use at most 64 MiB of HBM per device.

v0:
```python
import jax
import jax.numpy as jnp
from jax import lax
from jax.sharding import PartitionSpec as P

PANEL = 256
NMAT = 8


def with_halo(value, sides, width):
    for axis, dim in sides:
        devices, length = (lax.axis_size(axis), value.shape[dim])
        up = [(i, (i + 1) % devices) for i in range(devices - 1)]
        down = [(j, i) for i, j in up]
        last = lax.slice_in_dim(value, length - width, length, axis=dim)
        first = lax.slice_in_dim(value, 0, width, axis=dim)
        before = lax.ppermute(last, axis, up)
        after = lax.ppermute(first, axis, down)
        value = jnp.concatenate([before, value, after], axis=dim)
    return value


def couplings(material, blocks):
    kinds = jnp.arange(NMAT, dtype=jnp.int32)
    onehot = (material[..., None] == kinds).astype(jnp.float32)
    table = blocks.reshape(NMAT, 63)
    flat = jnp.einsum("xyzm,mk->xyzk", onehot, table, precision=lax.Precision.HIGHEST)
    return flat.reshape(material.shape + (7, 3, 3))


def neighbours(padded):
    centre = padded[1:-1, 1:-1, 1:-1]
    return [
        centre,
        padded[2:, 1:-1, 1:-1],
        padded[:-2, 1:-1, 1:-1],
        padded[1:-1, 2:, 1:-1],
        padded[1:-1, :-2, 1:-1],
        padded[1:-1, 1:-1, 2:],
        padded[1:-1, 1:-1, :-2],
    ]


def apply_blocks(padded, coupling):
    pieces = neighbours(padded)
    result = jnp.zeros(pieces[0].shape, jnp.float32)
    for offset in range(7):
        result = result + jnp.einsum(
            "xyzij,xyzjc->xyzic",
            coupling[:, :, :, offset],
            pieces[offset],
            precision=lax.Precision.HIGHEST,
        )
    return result


def shards(modes, blocks, material):
    panel = modes[..., :PANEL]
    padded = with_halo(panel, (("row", 0), ("col", 1), ("gz", 2)), 1)
    coupling = couplings(material, blocks)
    stiff_panel = apply_blocks(padded.astype(jnp.float32), coupling).astype(jnp.bfloat16)
    flat_modes = modes.reshape(-1, modes.shape[-1])
    flat_stiff = stiff_panel.reshape(-1, PANEL)
    tile_rows = lax.psum_scatter(
        lax.dot_general(
            flat_modes, flat_stiff, (((0,), (0,)), ((), ())), preferred_element_type=jnp.float32
        ),
        "col",
        scatter_dimension=0,
        tiled=True,
    )
    shared = lax.psum_scatter(tile_rows, "row", scatter_dimension=0, tiled=True)
    summed = lax.psum(shared, "gz")
    reduced = lax.all_gather(summed, "row", axis=0, tiled=True)
    return reduced


def solution(mesh):
    return jax.shard_map(
        shards,
        mesh=mesh,
        in_specs=(P("row", "col", "gz", None, None), P(), P("row", "col", "gz")),
        out_specs=P("col", None),
        check_vma=False,
    )
```

profile of v0, /device:TPU:1, one launch (start us, length us, event | category | flops | bytes accessed | tf_op | source)
XLA Modules:
  0.0 332.2 jit_solution(4879748920144390912)
XLA Ops:
  6.5 1.0 fusion.33
  8.3 4.9 %collective-permute-start.1 = (bf16[1,6,16,3,256]{4,3,2,1,0:T(4,128)(2,1)}, bf16[1,6,16,3,256]{4,3,2,1,0:T(4,128)(2,1)S(1)}, u32[]{:S(2)}, u32[]{:S(2)}) collective-permute-start(bf16[1,6,16,3,256]{4,3,2,1,0:T(4,128)(2,1)} %copy.59), channel_id=1, source_target_pairs={{0,32},{32,64},{64,96},{96,128},{128,160},{160,192},{192,224},{224... | collective-permute-start | bytes 442376 | tf_op jit(solution)/shard_map/ppermute | solution.py:17
  13.3 0.8 copy.58
  14.0 5.1 %collective-permute-start = (bf16[1,6,16,3,256]{4,3,2,1,0:T(4,128)(2,1)}, bf16[1,6,16,3,256]{4,3,2,1,0:T(4,128)(2,1)S(1)}, u32[]{:S(2)}, u32[]{:S(2)}) collective-permute-start(bf16[1,6,16,3,256]{4,3,2,1,0:T(4,128)(2,1)} %copy.58), channel_id=1, source_target_pairs={{32,0},{64,32},{96,64},{128,96},{160,128},{192,160},{224,192},{256... | collective-permute-start | bytes 442376 | tf_op jit(solution)/shard_map/ppermute | solution.py:18
  19.2 1.1 slice.78
  21.0 1.3 fusion.35
  22.9 1.6 fusion.18
  24.4 1.4 copy.54
  25.8 2.3 copy.53
  28.1 2.3 copy.52
  30.4 2.3 copy.51
  32.7 2.3 copy.50
  34.9 1.4 copy.49
  37.4 1.3 collective-permute-start.3
  38.7 1.3 collective-permute-start.2
  40.0 1.6 fusion.10
  41.6 1.6 fusion.8
  43.2 3.9 %collective-permute-done.2 = bf16[6,1,16,3,256]{4,3,2,1,0:T(4,128)(2,1)S(1)} collective-permute-done((bf16[6,1,16,3,256]{4,3,2,1,0:T(4,128)(2,1)S(1)}, bf16[6,1,16,3,256]{4,3,2,1,0:T(4,128)(2,1)S(1)}, u32[]{:S(2)}, u32[]{:S(2)}) %collective-permute-start.2) | collective-permute-done | bytes 147488 | tf_op jit(solution)/shard_map/ppermute | solution.py:18
  47.4 1.4 collective-permute-start.4
  48.8 12.9 %collective-permute-start.5 = (bf16[6,8,1,3,256]{4,1,3,2,0:T(8,128)(2,1)S(1)}, bf16[6,8,1,3,256]{4,1,3,2,0:T(8,128)(2,1)S(1)}, u32[]{:S(2)}, u32[]{:S(2)}) collective-permute-start(bf16[6,8,1,3,256]{4,1,3,2,0:T(8,128)(2,1)S(1)} %copy.38), channel_id=1, source_target_pairs={{0,1},{2,3},{4,5},{6,7},{8,9},{10,11},{12,13},{14,15},{16,17},{18,... | collective-permute-start | bytes 221192 | tf_op jit(solution)/shard_map/ppermute | solution.py:17
  61.7 1.6 fusion.6
  63.3 1.6 fusion.4
  65.0 1.0 collective-permute-done.5
  66.1 1.6 fusion.2
  67.7 3.3 add_convert_fusion
  71.0 2.9 convolution_bitcast_fusion
  74.0 93.6 %reduce-scatter.5.cloned.1.call-done = f32[128,256]{0,1:T(8,128)} async-done(((f32[2048,256]{0,1:T(8,128)}), f32[128,256]{0,1:T(8,128)}) %reduce-scatter.5.cloned.1.call-update) | async-done | bytes 131088 | tf_op jit(solution)/shard_map/reduce_scatter | solution.py:64
  167.6 1.7 copy.55
  169.3 99.0 %reduce-scatter.7.cloned.1.call-done = f32[8,256]{1,0:T(8,128)} async-done(((f32[128,256]{1,0:T(8,128)}), f32[8,256]{1,0:T(8,128)}) %reduce-scatter.7.cloned.1.call-update) | async-done | bytes 8208
  268.3 0.8 copy.56
  269.1 24.8 %psum.7 = f32[8,256]{0,1:T(8,128)S(1)} all-reduce(f32[8,256]{0,1:T(8,128)S(1)} %copy.56), channel_id=1, replica_groups=mesh['row'=16,'col'=16,'gz'=2] {'gz'}, use_global_device_ids=true, to_apply=%region_2.0 | all-reduce | flops 2048 | bytes 16384 | tf_op jit(solution)/shard_map/psum | solution.py:73
  294.0 30.7 %all_gather.3 = f32[128,256]{1,0:T(8,128)S(1)} all-gather(f32[8,256]{1,0:T(8,128)S(1)} %copy.42), channel_id=1, replica_groups=mesh['row'=16,'col'=16,'gz'=2] {'row'}, dimensions={0}, use_global_device_ids=true | all-gather | bytes 139264 | tf_op jit(solution)/shard_map/all_gather | solution.py:74
  (45 shorter events, 4.0 us)
Async XLA Ops:
  6.5 13.8 %copy-start.6 = (s32[4,6,16]{2,0,1:T(4,128)S(1)}, s32[4,6,16]{2,0,1:T(4,128)}, u32[]{:S(2)}) copy-start(s32[4,6,16]{2,0,1:T(4,128)} %param.5) | copy-start | bytes 4612
  6.5 13.8 %copy-start.5 = (f32[8,7,3,3]{1,0,3,2:T(8,128)S(1)}, f32[8,7,3,3]{1,0,3,2:T(8,128)}, u32[]{:S(2)}) copy-start(f32[8,7,3,3]{1,0,3,2:T(8,128)} %param.4) | copy-start | bytes 6052
  6.5 161.1 %reduce-scatter.5.cloned.1.call-start = ((), (), s32[]{:S(2)}) async-start(), calls=%async_computation.2 | async-start | bytes 2228224 | tf_op jit(solution)/shard_map/reduce_scatter | solution.py:64
  8.3 28.0 %collective-permute-start.1 = (bf16[1,6,16,3,256]{4,3,2,1,0:T(4,128)(2,1)}, bf16[1,6,16,3,256]{4,3,2,1,0:T(4,128)(2,1)S(1)}, u32[]{:S(2)}, u32[]{:S(2)}) collective-permute-start(bf16[1,6,16,3,256]{4,3,2,1,0:T(4,128)(2,1)} %copy.59), channel_id=1, source_target_pairs={{0,32},{32,64},{64,96},{96,128},{128,160},{160,192},{192,224},{224... | collective-permute-start | bytes 442376 | tf_op jit(solution)/shard_map/ppermute | solution.py:17
  14.0 23.0 %collective-permute-start = (bf16[1,6,16,3,256]{4,3,2,1,0:T(4,128)(2,1)}, bf16[1,6,16,3,256]{4,3,2,1,0:T(4,128)(2,1)S(1)}, u32[]{:S(2)}, u32[]{:S(2)}) collective-permute-start(bf16[1,6,16,3,256]{4,3,2,1,0:T(4,128)(2,1)} %copy.58), channel_id=1, source_target_pairs={{32,0},{64,32},{96,64},{128,96},{160,128},{192,160},{224,192},{256... | collective-permute-start | bytes 442376 | tf_op jit(solution)/shard_map/ppermute | solution.py:18
  36.4 3.6 %copy-start.3 = (f32[4,6,16,1,3,3]{5,4,2,1,0,3:T(4,128)S(1)}, f32[4,6,16,1,3,3]{5,4,2,1,0,3:T(4,128)}, u32[]{:S(2)}) copy-start(f32[4,6,16,1,3,3]{5,4,2,1,0,3:T(4,128)} %copy.49) | copy-start | bytes 41476
  37.4 5.9 %collective-permute-start.3 = (bf16[6,1,16,3,256]{4,3,2,1,0:T(4,128)(2,1)S(1)}, bf16[6,1,16,3,256]{4,3,2,1,0:T(4,128)(2,1)S(1)}, u32[]{:S(2)}, u32[]{:S(2)}) collective-permute-start(bf16[6,1,16,3,256]{4,3,2,1,0:T(4,128)(2,1)S(1)} %get-tuple-element.9), channel_id=1, source_target_pairs={{0,2},{2,4},{4,6},{6,8},{8,10},{10,12},{12,14},{14,16},{16,18},{18... | collective-permute-start | bytes 442376 | tf_op jit(solution)/shard_map/ppermute | solution.py:17
  38.7 8.5 %collective-permute-start.2 = (bf16[6,1,16,3,256]{4,3,2,1,0:T(4,128)(2,1)S(1)}, bf16[6,1,16,3,256]{4,3,2,1,0:T(4,128)(2,1)S(1)}, u32[]{:S(2)}, u32[]{:S(2)}) collective-permute-start(bf16[6,1,16,3,256]{4,3,2,1,0:T(4,128)(2,1)S(1)} %get-tuple-element.10), channel_id=1, source_target_pairs={{2,0},{4,2},{6,4},{8,6},{10,8},{12,10},{14,12},{16,14},{18,16},{20... | collective-permute-start | bytes 442376 | tf_op jit(solution)/shard_map/ppermute | solution.py:18
  40.0 1.6 copy-start.2
  43.2 18.5 %copy-start.1 = (f32[4,6,16,1,3,3]{5,4,2,1,0,3:T(4,128)S(1)}, f32[4,6,16,1,3,3]{5,4,2,1,0,3:T(4,128)}, u32[]{:S(2)}) copy-start(f32[4,6,16,1,3,3]{5,4,2,1,0,3:T(4,128)} %copy.51) | copy-start | bytes 41476
  47.3 16.0 %copy-start = (f32[4,6,16,1,3,3]{5,4,2,1,0,3:T(4,128)S(1)}, f32[4,6,16,1,3,3]{5,4,2,1,0,3:T(4,128)}, u32[]{:S(2)}) copy-start(f32[4,6,16,1,3,3]{5,4,2,1,0,3:T(4,128)} %copy.52) | copy-start | bytes 41476
  47.4 17.6 %collective-permute-start.4 = (bf16[6,8,1,3,256]{4,1,3,2,0:T(8,128)(2,1)S(1)}, bf16[6,8,1,3,256]{4,1,3,2,0:T(8,128)(2,1)S(1)}, u32[]{:S(2)}, u32[]{:S(2)}) collective-permute-start(bf16[6,8,1,3,256]{4,1,3,2,0:T(8,128)(2,1)S(1)} %copy.34), channel_id=1, source_target_pairs={{1,0},{3,2},{5,4},{7,6},{9,8},{11,10},{13,12},{15,14},{17,16},{19,... | collective-permute-start | bytes 221192 | tf_op jit(solution)/shard_map/ppermute | solution.py:18
  48.8 17.2 %collective-permute-start.5 = (bf16[6,8,1,3,256]{4,1,3,2,0:T(8,128)(2,1)S(1)}, bf16[6,8,1,3,256]{4,1,3,2,0:T(8,128)(2,1)S(1)}, u32[]{:S(2)}, u32[]{:S(2)}) collective-permute-start(bf16[6,8,1,3,256]{4,1,3,2,0:T(8,128)(2,1)S(1)} %copy.38), channel_id=1, source_target_pairs={{0,1},{2,3},{4,5},{6,7},{8,9},{10,11},{12,13},{14,15},{16,17},{18,... | collective-permute-start | bytes 221192 | tf_op jit(solution)/shard_map/ppermute | solution.py:17
  63.3 2.7 copy-start.4
  66.1 5.0 %slice-start = ((s8[4718592]{0:T(1024)(128)(4,1)}), s8[4194304]{0:T(1024)(128)(4,1)S(1)}, s32[]{:S(2)}) async-start(s8[4718592]{0:T(1024)(128)(4,1)} %bitcast.45), calls=%async_computation.4 | async-start | bytes 8388608
  67.7 3.3 %slice-start.1 = ((s8[4718592]{0:T(1024)(128)(4,1)}), s8[524288]{0:T(1024)(128)(4,1)S(1)}, s32[]{:S(2)}) async-start(s8[4718592]{0:T(1024)(128)(4,1)} %bitcast.45), calls=%async_computation.5 | async-start | bytes 1048576
  74.0 194.4 %reduce-scatter.7.cloned.1.call-start = ((), (), s32[]{:S(2)}) async-start(), calls=%async_computation.3 | async-start | bytes 139264
Sparse Core Ops, SparseCore 0:
  74.1 93.4 reduce-scatter.4
  170.6 97.6 reduce-scatter.6
where the time goes:
time: 333 us; the launch traced here: 332 us
  waiting for transfers between devices  198 us (59%)
  blocking collectives  55.5 us (17%)
  starting transfers between devices  27 us (8%)
  local copies, waits for them, and re-layouts  21.9 us (7%)
  matrix products  16.3 us (5%)
  between operations  13.8 us (4%)
    unnamed x3, waiting for transfers between devices  99.1 us
    reduce_scatter x1, waiting for transfers between devices, shards(): lax.psum_scatter(lax.dot_general(flat_modes, flat_stiff, (((0,), (0,)), (...  93.6 us
    all_gather x1, blocking collectives, shards(): reduced = lax.all_gather(summed, 'row', axis=0, tiled=True)  30.7 us
    psum x1, blocking collectives, shards(): summed = lax.psum(shared, 'gz')  24.8 us
    ppermute x3, starting transfers between devices, with_halo(): before = lax.ppermute(last, axis, up)  19.1 us
    dot_general x7, matrix products, apply_blocks(): jnp.einsum('xyzij,xyzjc->xyzic', coupling[:, :, :, offset], pieces[offset...  12.9 us
    squeeze x7, local copies, waits for them, and re-layouts, apply_blocks(): coupling[:, :, :, offset]  12.4 us
    ppermute x3, starting transfers between devices, with_halo(): after = lax.ppermute(first, axis, down)  7.86 us
  transfers between devices with their start and end apart: 8, of which 4 were waited for; matrix products, arithmetic and copies ran while one was open for 8% of the time, Pallas kernels for 0%

commit v1 on v0

v1 whole, which is shorter than its diff:
```python
import jax
import jax.numpy as jnp
from jax import lax
from jax.experimental import pallas as pl
from jax.experimental.pallas import tpu as pltpu
from jax.sharding import Mesh, PartitionSpec as P

PANEL = 256
HALF = 128
NMAT = 8
SX, SY, SZ = 4, 6, 16
CELLS = SX * SY
GROUP = 3 * SZ
ROWS = CELLS * GROUP
ROW, COL, GZ = ("z", "core"), ("y", "x"), "gz"
Z = ("gz", "z")
f32, bf16 = jnp.float32, jnp.bfloat16


def lane(values, k):
    return jnp.broadcast_to(values[:, k : k + 1], (values.shape[0], PANEL))


def local_kernel(kind_ref, table_ref, panel_ref, coef_ref, part_ref, grid_ref):
    table = table_ref[...]
    for n in range(CELLS):
        kind = jnp.broadcast_to(kind_ref[:, n : n + 1], (SZ, 128))
        coef = jnp.zeros((SZ, 128), f32)
        for m in range(NMAT):
            coef = jnp.where(kind == m, jnp.broadcast_to(table[m : m + 1, :], (SZ, 128)), coef)
        coef_ref[n] = coef
        x, y = divmod(n, SY)
        at = (x + 1) * (SY + 2) + y + 1
        grid_ref[at] = panel_ref[n * GROUP : (n + 1) * GROUP, :].astype(f32)
    zeros = jnp.zeros((GROUP, PANEL), f32)
    for y in range(SY + 2):
        grid_ref[y] = zeros
        grid_ref[(SX + 1) * (SY + 2) + y] = zeros
    for x in range(1, SX + 1):
        grid_ref[x * (SY + 2)] = zeros
        grid_ref[x * (SY + 2) + SY + 1] = zeros
    level = lax.broadcasted_iota(jnp.int32, (SZ, PANEL), 0)

    def cell(n, carry):
        at = (n // SY + 1) * (SY + 2) + n % SY + 1
        coef = coef_ref[n]
        total = [jnp.zeros((SZ, PANEL), f32) for _ in range(3)]
        sources = ((1, at + SY + 2), (2, at - SY - 2), (3, at + 1), (4, at - 1))
        for j in range(3):
            own = grid_ref[at, j * SZ : (j + 1) * SZ, :]
            above = jnp.where(level == SZ - 1, 0.0, pltpu.roll(own, SZ - 1, 0))
            below = jnp.where(level == 0, 0.0, pltpu.roll(own, 1, 0))
            terms = [(0, own), (5, above), (6, below)]
            terms += [(o, grid_ref[s, j * SZ : (j + 1) * SZ, :]) for o, s in sources]
            for o, value in terms:
                for i in range(3):
                    total[i] = total[i] + lane(coef, o * 9 + i * 3 + j) * value
        for i in range(3):
            start = pl.multiple_of(n * GROUP + i * SZ, SZ)
            part_ref[pl.ds(start, SZ), :] = total[i]
        return carry

    lax.fori_loop(0, CELLS, cell, 0)


def finish_kernel(coef_ref, part_ref, xlo_ref, xhi_ref, ylo_ref, yhi_ref, zface_ref, modes_ref,
                  keep_ref, send_ref, work_ref, stiff_ref):
    core, gz = lax.axis_index("core"), lax.axis_index("gz")
    level = lax.broadcasted_iota(jnp.int32, (SZ, 128), 0)
    edge = jnp.where(gz == 0, SZ - 1, 0)

    def face_z(n, carry):
        coef = coef_ref[n]
        mine = jnp.where(level == edge, jnp.where(gz == 0, coef, pltpu.roll(coef, 128 - 9, 1)), 0.0)
        rows = zface_ref[n].astype(f32)
        for i in range(3):
            start = pl.multiple_of(n * GROUP + i * SZ, SZ)
            total = part_ref[pl.ds(start, SZ), :]
            for j in range(3):
                total = total + lane(mine, 45 + i * 3 + j) * jnp.broadcast_to(rows[j : j + 1, :], (SZ, PANEL))
            work_ref[pl.ds(start, SZ), :] = total
        return carry

    lax.fori_loop(0, CELLS, face_z, 0)

    def face(n, o, ref, k):
        coef = coef_ref[n]
        for i in range(3):
            start = n * GROUP + i * SZ
            total = work_ref[start : start + SZ, :]
            for j in range(3):
                value = ref[k * GROUP + j * SZ : k * GROUP + (j + 1) * SZ, :].astype(f32)
                total = total + lane(coef, o * 9 + i * 3 + j) * value
            work_ref[start : start + SZ, :] = total

    for y in range(SY):
        face((SX - 1) * SY + y, 1, xhi_ref, y)
        face(y, 2, xlo_ref, y)
    for x in range(SX):
        face(x * SY + SY - 1, 3, yhi_ref, x)
        face(x * SY, 4, ylo_ref, x)
    stiff_ref[...] = work_ref[...].astype(bf16).T
    for t in range(modes_ref.shape[1] // PANEL):
        product = jnp.dot(stiff_ref[...], modes_ref[:, t * PANEL : (t + 1) * PANEL], preferred_element_type=f32)
        low, high = product[:HALF], product[HALF:]
        keep = jnp.where(core == 0, low, high)
        send = jnp.where(core == 0, high, low)
        for u in range(2):
            keep_ref[2 * t + u] = keep[:, u * HALF : (u + 1) * HALF]
            send_ref[2 * t + u] = send[:, u * HALF : (u + 1) * HALF]


def swap(value, axis):
    return lax.ppermute(value, axis, [(0, 1), (1, 0)])


def shards(modes, blocks, material):
    full = modes.shape[-1]
    grid = modes.transpose(0, 1, 3, 2, 4)
    panel = grid[..., :PANEL]
    chain = [(i, i + 1) for i in range(15)]
    back = [(j, i) for i, j in chain]
    gz = lax.axis_index(GZ)
    zsend = jnp.where(gz == 0, panel[:, :, :, SZ - 1], panel[:, :, :, 0]).reshape(CELLS, 3, PANEL)
    zface = swap(zsend, GZ)
    ylo = lax.ppermute(panel[:, SY - 1].reshape(-1, PANEL), COL, chain)
    yhi = lax.ppermute(panel[:, 0].reshape(-1, PANEL), COL, back)
    xlo = lax.ppermute(panel[SX - 1].reshape(-1, PANEL), ROW, chain)
    xhi = lax.ppermute(panel[0].reshape(-1, PANEL), ROW, back)
    kind = material.reshape(CELLS, SZ).T
    table = jnp.pad(blocks.reshape(NMAT, 63), ((0, 0), (0, 65)))
    flat = grid.reshape(ROWS, full)
    whole = lambda *shape: pl.BlockSpec(shape, lambda i: (0,) * len(shape))
    coef, part = pl.pallas_call(
        local_kernel,
        grid=(1,),
        in_specs=[whole(SZ, CELLS), whole(NMAT, 128), whole(ROWS, PANEL)],
        out_specs=[whole(CELLS, SZ, 128), whole(ROWS, PANEL)],
        out_shape=[jax.ShapeDtypeStruct((CELLS, SZ, 128), f32), jax.ShapeDtypeStruct((ROWS, PANEL), f32)],
        scratch_shapes=[pltpu.VMEM(((SX + 2) * (SY + 2), GROUP, PANEL), f32)],
        cost_estimate=pl.CostEstimate(flops=2 * ROWS * 21 * PANEL, bytes_accessed=3 * ROWS * PANEL, transcendentals=0),
        compiler_params=pltpu.CompilerParams(vmem_limit_bytes=24 << 20),
        name="local_stencil",
    )(kind, table, flat)
    tiles = full // HALF
    vmem = pl.BlockSpec(memory_space=pltpu.VMEM)
    keep, send = pl.pallas_call(
        finish_kernel,
        in_specs=[vmem] * 8,
        out_specs=[vmem] * 2,
        out_shape=[jax.ShapeDtypeStruct((tiles, HALF, HALF), f32)] * 2,
        scratch_shapes=[pltpu.VMEM((ROWS, PANEL), f32), pltpu.VMEM((PANEL, ROWS), bf16)],
        cost_estimate=pl.CostEstimate(flops=2 * ROWS * full * PANEL, bytes_accessed=2 * ROWS * full, transcendentals=0),
        compiler_params=pltpu.CompilerParams(vmem_limit_bytes=32 << 20),
        name="faces_and_product",
    )(coef, part, xlo, xhi, ylo, yhi, zface, flat)
    mine = (keep + swap(send, "core")).astype(bf16)
    parts = lax.all_to_all(mine, COL, 0, 0, tiled=True)
    plane = jnp.sum(parts.astype(f32), axis=0).astype(bf16)
    copies = jnp.broadcast_to(plane[None], (16,) + plane.shape)
    planes = lax.all_to_all(copies, Z, 0, 0, tiled=True)
    half = jnp.sum(planes.astype(f32), axis=0)
    other = swap(half, "core")
    core = lax.axis_index("core")
    both = jnp.where(core == 0, jnp.concatenate([half, other]), jnp.concatenate([other, half]))
    return both.T


def solution(mesh):
    split = Mesh(mesh.devices.reshape(8, 2, 4, 4, 2), ("z", "core", "y", "x", "gz"))
    return jax.shard_map(
        shards,
        mesh=split,
        in_specs=(P(ROW, COL, GZ, None, None), P(), P(ROW, COL, GZ)),
        out_specs=P(COL, None),
        check_vma=False,
    )
```

time: 333 us -> 110 us (0.33)
  waiting for transfers between devices: 198 us -> 3.51 us
  matrix products: 16.3 us -> 0 us
  local copies, waits for them, and re-layouts: 21.9 us -> 7.09 us
  between operations: 13.8 us -> 0.18 us
  Pallas kernels: 0 us -> 13.4 us
  starting transfers between devices: 27 us -> 37.2 us
  blocking collectives: 55.5 us -> 46.5 us
    unnamed x3 -> x0, waiting for transfers between devices: 99.1 us -> none
    reduce_scatter x1 -> x0, waiting for transfers between devices: 93.6 us -> none  [shards(): lax.psum_scatter(lax.dot_general(flat_modes, flat_stiff, (((0,), (0,)), (...]
    all_to_all x0 -> x2, blocking collectives: none -> 46.5 us  [the longest x1 27.9 us: shards(): planes = lax.all_to_all(copies, Z, 0, 0, tiled=True)]
    all_gather x1 -> x0, blocking collectives: 30.7 us -> none  [shards(): reduced = lax.all_gather(summed, 'row', axis=0, tiled=True)]
    psum x1 -> x0, blocking collectives: 24.8 us -> none  [shards(): summed = lax.psum(shared, 'gz')]
    dot_general x9 -> x0, matrix products: 16.3 us -> none  [the longest x7 12.9 us: apply_blocks(): jnp.einsum('xyzij,xyzjc->xyzic', coupling[:, :, :, offset], pieces[offset...]
    pallas_call x0 -> x2, Pallas kernels: none -> 13.4 us  [the longest x1 6.96 us: shards(): pl.pallas_call(local_kernel, grid=(1,), in_specs=[whole(SZ, CELLS), whole...]
    squeeze x7 -> x0, local copies, waits for them, and re-layouts: 12.4 us -> none  [apply_blocks(): coupling[:, :, :, offset]]
  transfers between devices with their start and end apart: 8 -> 7, of which waited for: 4 -> 2; matrix products, arithmetic and copies ran while one was open for 8% -> 4% of each run, Pallas kernels for 0% -> 6%
where the time goes in v1:
time: 110 us; the launch traced here: 109 us
  blocking collectives  46.5 us (42%)
  starting transfers between devices  37.2 us (34%)
  Pallas kernels  13.4 us (12%)
  local copies, waits for them, and re-layouts  7.09 us (6%)
  waiting for transfers between devices  3.51 us (3%)
  other arithmetic  1.46 us (1%)
    all_to_all x1, blocking collectives, shards(): planes = lax.all_to_all(copies, Z, 0, 0, tiled=True)  27.9 us
    ppermute x3, starting transfers between devices, swap(): return lax.ppermute(value, axis, [(0, 1), (1, 0)])  24.6 us
    all_to_all x1, blocking collectives, shards(): parts = lax.all_to_all(mine, COL, 0, 0, tiled=True)  18.6 us
    pallas_call x1, Pallas kernels, shards(): pl.pallas_call(local_kernel, grid=(1,), in_specs=[whole(SZ, CELLS), whole...  6.96 us
    pallas_call x1, Pallas kernels, shards(): pl.pallas_call(finish_kernel, in_specs=[vmem] * 8, out_specs=[vmem] * 2,...  6.4 us
    ppermute x1, starting transfers between devices, shards(): xlo = lax.ppermute(panel[SX - 1].reshape(-1, PANEL), ROW, chain)  4.39 us
    ppermute x1, starting transfers between devices, shards(): ylo = lax.ppermute(panel[:, SY - 1].reshape(-1, PANEL), COL, chain)  3.95 us
    ppermute x3, waiting for transfers between devices, swap(): return lax.ppermute(value, axis, [(0, 1), (1, 0)])  3.5 us
  transfers between devices with their start and end apart: 7, of which 2 were waited for; matrix products, arithmetic and copies ran while one was open for 4% of the time, Pallas kernels for 6%

profile of v1, /device:TPU:1, one launch (start us, length us, event | category | flops | bytes accessed | tf_op | source)
XLA Modules:
  0.0 109.4 jit_solution(13442888684027275020)
XLA Ops:
  0.0 1.0 fusion.1
  1.0 4.0 %collective-permute-start.2 = (bf16[192,256]{1,0:T(8,128)(2,1)S(1)}, bf16[192,256]{1,0:T(8,128)(2,1)S(1)}, u32[]{:S(2)}, u32[]{:S(2)}) collective-permute-start(bf16[192,256]{1,0:T(8,128)(2,1)S(1)} %bitcast.24), channel_id=1, source_target_pairs={{0,2},{2,4},{4,6},{6,8},{8,10},{10,12},{12,14},{14,16},{16,18},{18... | collective-permute-start | bytes 294920 | tf_op jit(solution)/shard_map/ppermute | solution.py:126
  4.9 1.3 %collective-permute-start.3 = (bf16[192,256]{1,0:T(8,128)(2,1)S(1)}, bf16[192,256]{1,0:T(8,128)(2,1)S(1)}, u32[]{:S(2)}, u32[]{:S(2)}) collective-permute-start(bf16[192,256]{1,0:T(8,128)(2,1)S(1)} %bitcast.23), channel_id=1, source_target_pairs={{2,0},{4,2},{6,4},{8,6},{10,8},{12,10},{14,12},{16,14},{18,16},{20... | collective-permute-start | bytes 294920 | tf_op jit(solution)/shard_map/ppermute | solution.py:127
  6.2 1.0 fusion.2
  7.2 4.4 %collective-permute-start = (bf16[288,256]{1,0:T(8,128)(2,1)S(1)}, bf16[288,256]{1,0:T(8,128)(2,1)S(1)}, u32[]{:S(2)}, u32[]{:S(2)}) collective-permute-start(bf16[288,256]{1,0:T(8,128)(2,1)S(1)} %bitcast.22), channel_id=1, source_target_pairs={{0,32},{32,64},{64,96},{96,128},{128,160},{160,192},{192,224},{224... | collective-permute-start | bytes 442376 | tf_op jit(solution)/shard_map/ppermute | solution.py:128
  11.6 3.0 %collective-permute-start.1 = (bf16[288,256]{1,0:T(8,128)(2,1)S(1)}, bf16[288,256]{1,0:T(8,128)(2,1)S(1)}, u32[]{:S(2)}, u32[]{:S(2)}) collective-permute-start(bf16[288,256]{1,0:T(8,128)(2,1)S(1)} %bitcast.21), channel_id=1, source_target_pairs={{32,0},{64,32},{96,64},{128,96},{160,128},{192,160},{224,192},{256... | collective-permute-start | bytes 442376 | tf_op jit(solution)/shard_map/ppermute | solution.py:129
  14.7 1.2 %broadcast_select_fusion = bf16[4,6,3,1,256]{4,3,2,1,0:T(2,128)(2,1)S(1)} fusion(pred[]{:T(512)S(6)} %eq.7, bf16[4,6,3,16,2048]{4,3,2,1,0:T(8,128)(2,1)} %bitcast.17), kind=kLoop, calls=%fused_computation.2 | loop fusion | flops 18432 | bytes 110593 | tf_op jit(solution)/shard_map/jit(_where)/select_n | solution.py:124
  15.9 13.4 %collective-permute-start.4 = (bf16[24,3,256]{2,1,0:T(4,128)(2,1)S(1)}, bf16[24,3,256]{2,1,0:T(4,128)(2,1)S(1)}, u32[]{:S(2)}, u32[]{:S(2)}) collective-permute-start(bf16[24,3,256]{2,1,0:T(4,128)(2,1)S(1)} %bitcast.25), channel_id=1, source_target_pairs={{0,1},{1,0},{2,3},{3,2},{4,5},{5,4},{6,7},{7,6},{8,9},{9,8},{10,11... | collective-permute-start | bytes 110600 | tf_op jit(solution)/shard_map/ppermute | solution.py:114
  29.3 0.8 copy.19
  30.1 0.1 reshape.18
  30.2 0.9 copy.14
  31.2 0.1 copy.15
  31.2 2.3 %copy-done = bf16[4,6,16,3,2048]{4,2,3,1,0:T(8,128)(2,1)S(1)} copy-done((bf16[4,6,16,3,2048]{4,2,3,1,0:T(8,128)(2,1)S(1)}, bf16[4,6,16,3,2048]{4,2,3,1,0:T(8,128)(2,1)}, u32[]{:S(2)}) %copy-start) | copy-done | bytes 4718616
  33.6 7.0 %local_stencil.1 = (f32[24,16,128]{2,1,0:T(8,128)S(1)}, f32[1152,256]{1,0:T(8,128)S(1)}) custom-call(s32[16,24]{1,0:T(8,128)S(1)} %bitcast.20, f32[8,128]{1,0:T(8,128)S(1)} %pad.4.table_ref, bf16[1152,2048]{1,0:T(8,128)(2,1)S(1)} %bitcast.18), custom_call_target="tpu_custom_call" | custom-call | flops 12386304 | bytes 884736 | tf_op jit(solution)/shard_map/local_stencil/pallas_call | solution.py:134
  40.6 0.0 collective-permute-done.4.zface_ref
  40.6 0.0 collective-permute-done.2.ylo_ref
  40.6 0.0 collective-permute-done.3.yhi_ref
  40.6 0.0 collective-permute-done.xlo_ref
  40.6 0.0 collective-permute-done.1.xhi_ref
  40.6 0.0 copy-done.1
  40.6 6.4 %faces_and_product.1 = (f32[16,128,128]{2,1,0:T(8,128)S(1)}, f32[16,128,128]{2,1,0:T(8,128)S(1)}) custom-call(f32[24,16,128]{2,1,0:T(8,128)S(1)} %get-tuple-element.9.coef_ref, f32[1152,256]{1,0:T(8,128)S(1)} %get-tuple-element.10.part_ref, bf16[288,256]{1,0:T(8,128)(2,1)S(1)} %collective-permute-done.xlo_ref, ...), custom_call_target="tpu_custom_call" | custom-call | flops 1207959552 | bytes 4718592 | tf_op jit(solution)/shard_map/faces_and_product/pallas_call | solution.py:147
  47.0 1.9 %collective-permute-start.5 = (f32[16,128,128]{2,1,0:T(8,128)S(1)}, f32[16,128,128]{2,1,0:T(8,128)S(1)}, u32[]{:S(2)}, u32[]{:S(2)}) collective-permute-start(f32[16,128,128]{2,1,0:T(8,128)S(1)} %get-tuple-element.12), channel_id=1, source_target_pairs={{0,32},{32,0},{1,33},{33,1},{2,34},{34,2},{3,35},{35,3},{4,36},{36... | collective-permute-start | bytes 3145736 | tf_op jit(solution)/shard_map/ppermute | solution.py:114
  48.9 2.6 %collective-permute-done.5 = f32[16,128,128]{2,1,0:T(8,128)S(1)} collective-permute-done((f32[16,128,128]{2,1,0:T(8,128)S(1)}, f32[16,128,128]{2,1,0:T(8,128)S(1)}, u32[]{:S(2)}, u32[]{:S(2)}) %collective-permute-start.5) | collective-permute-done | bytes 1048608 | tf_op jit(solution)/shard_map/ppermute | solution.py:114
  51.6 0.1 add_convert_fusion
  51.7 18.6 %all_to_all.10 = bf16[16,128,128]{2,1,0:T(8,128)(2,1)S(1)} all-to-all(bf16[16,128,128]{2,1,0:T(8,128)(2,1)S(1)} %add_convert_fusion), channel_id=1, replica_groups=mesh['z'=8,'core'=2,'y'=4,'x'=4,'gz'=2] {'y','x'}, dimensions={0} | all-to-all | bytes 1048576 | tf_op jit(solution)/shard_map/all_to_all | solution.py:158
  70.3 0.1 reduce_sum.21
  70.4 0.1 broadcast_in_dim.2
  70.5 27.9 %all_to_all.11 = bf16[16,128,128]{2,1,0:T(8,128)(2,1)S(1)} all-to-all(bf16[16,128,128]{2,1,0:T(8,128)(2,1)S(1)} %broadcast_in_dim.2), channel_id=1, replica_groups=mesh['z'=8,'core'=2,'y'=4,'x'=4,'gz'=2] {'gz','z'}, dimensions={0} | all-to-all | bytes 1048576 | tf_op jit(solution)/shard_map/all_to_all | solution.py:161
  98.4 0.1 convert_reduce_fusion
  98.5 9.2 %collective-permute-start.6 = (f32[128,128]{1,0:T(8,128)S(1)}, f32[128,128]{1,0:T(8,128)S(1)}, u32[]{:S(2)}, u32[]{:S(2)}) collective-permute-start(f32[128,128]{1,0:T(8,128)S(1)} %convert_reduce_fusion), channel_id=1, source_target_pairs={{0,32},{32,0},{1,33},{33,1},{2,34},{34,2},{3,35},{35,3},{4,36},{36... | collective-permute-start | bytes 196616 | tf_op jit(solution)/shard_map/ppermute | solution.py:114
  107.7 0.9 collective-permute-done.6
  108.6 0.8 copy.18
  (6 shorter events, 0.1 us)
Async XLA Ops:
  1.0 39.6 %collective-permute-start.2 = (bf16[192,256]{1,0:T(8,128)(2,1)S(1)}, bf16[192,256]{1,0:T(8,128)(2,1)S(1)}, u32[]{:S(2)}, u32[]{:S(2)}) collective-permute-start(bf16[192,256]{1,0:T(8,128)(2,1)S(1)} %bitcast.24), channel_id=1, source_target_pairs={{0,2},{2,4},{4,6},{6,8},{8,10},{10,12},{12,14},{14,16},{16,18},{18... | collective-permute-start | bytes 294920 | tf_op jit(solution)/shard_map/ppermute | solution.py:126
  4.9 35.7 %collective-permute-start.3 = (bf16[192,256]{1,0:T(8,128)(2,1)S(1)}, bf16[192,256]{1,0:T(8,128)(2,1)S(1)}, u32[]{:S(2)}, u32[]{:S(2)}) collective-permute-start(bf16[192,256]{1,0:T(8,128)(2,1)S(1)} %bitcast.23), channel_id=1, source_target_pairs={{2,0},{4,2},{6,4},{8,6},{10,8},{12,10},{14,12},{16,14},{18,16},{20... | collective-permute-start | bytes 294920 | tf_op jit(solution)/shard_map/ppermute | solution.py:127
  7.2 33.4 %collective-permute-start = (bf16[288,256]{1,0:T(8,128)(2,1)S(1)}, bf16[288,256]{1,0:T(8,128)(2,1)S(1)}, u32[]{:S(2)}, u32[]{:S(2)}) collective-permute-start(bf16[288,256]{1,0:T(8,128)(2,1)S(1)} %bitcast.22), channel_id=1, source_target_pairs={{0,32},{32,64},{64,96},{96,128},{128,160},{160,192},{192,224},{224... | collective-permute-start | bytes 442376 | tf_op jit(solution)/shard_map/ppermute | solution.py:128
  11.6 29.0 %collective-permute-start.1 = (bf16[288,256]{1,0:T(8,128)(2,1)S(1)}, bf16[288,256]{1,0:T(8,128)(2,1)S(1)}, u32[]{:S(2)}, u32[]{:S(2)}) collective-permute-start(bf16[288,256]{1,0:T(8,128)(2,1)S(1)} %bitcast.21), channel_id=1, source_target_pairs={{32,0},{64,32},{96,64},{128,96},{160,128},{192,160},{224,192},{256... | collective-permute-start | bytes 442376 | tf_op jit(solution)/shard_map/ppermute | solution.py:129
  15.9 24.7 %collective-permute-start.4 = (bf16[24,3,256]{2,1,0:T(4,128)(2,1)S(1)}, bf16[24,3,256]{2,1,0:T(4,128)(2,1)S(1)}, u32[]{:S(2)}, u32[]{:S(2)}) collective-permute-start(bf16[24,3,256]{2,1,0:T(4,128)(2,1)S(1)} %bitcast.25), channel_id=1, source_target_pairs={{0,1},{1,0},{2,3},{3,2},{4,5},{5,4},{6,7},{7,6},{8,9},{9,8},{10,11... | collective-permute-start | bytes 110600 | tf_op jit(solution)/shard_map/ppermute | solution.py:114
  31.2 2.3 %copy-start = (bf16[4,6,16,3,2048]{4,2,3,1,0:T(8,128)(2,1)S(1)}, bf16[4,6,16,3,2048]{4,2,3,1,0:T(8,128)(2,1)}, u32[]{:S(2)}) copy-start(bf16[4,6,16,3,2048]{4,2,3,1,0:T(8,128)(2,1)} %param.3) | copy-start | bytes 14155780
  33.6 7.0 %copy-start.1 = (bf16[4,6,16,3,2048]{4,2,3,1,0:T(8,128)(2,1)S(1)}, bf16[4,6,16,3,2048]{4,2,3,1,0:T(8,128)(2,1)}, u32[]{:S(2)}) copy-start(bf16[4,6,16,3,2048]{4,2,3,1,0:T(8,128)(2,1)} %param.3) | copy-start | bytes 14155780
  47.0 4.6 %collective-permute-start.5 = (f32[16,128,128]{2,1,0:T(8,128)S(1)}, f32[16,128,128]{2,1,0:T(8,128)S(1)}, u32[]{:S(2)}, u32[]{:S(2)}) collective-permute-start(f32[16,128,128]{2,1,0:T(8,128)S(1)} %get-tuple-element.12), channel_id=1, source_target_pairs={{0,32},{32,0},{1,33},{33,1},{2,34},{34,2},{3,35},{35,3},{4,36},{36... | collective-permute-start | bytes 3145736 | tf_op jit(solution)/shard_map/ppermute | solution.py:114
  98.5 10.1 %collective-permute-start.6 = (f32[128,128]{1,0:T(8,128)S(1)}, f32[128,128]{1,0:T(8,128)S(1)}, u32[]{:S(2)}, u32[]{:S(2)}) collective-permute-start(f32[128,128]{1,0:T(8,128)S(1)} %convert_reduce_fusion), channel_id=1, source_target_pairs={{0,32},{32,0},{1,33},{33,1},{2,34},{34,2},{3,35},{35,3},{4,36},{36... | collective-permute-start | bytes 196616 | tf_op jit(solution)/shard_map/ppermute | solution.py:114

commit v2 on v1

v2 whole, which is shorter than its diff:
```python
import jax
import jax.numpy as jnp
from jax import lax
from jax.experimental import pallas as pl
from jax.experimental.pallas import tpu as pltpu
from jax.sharding import Mesh, PartitionSpec as P

PANEL = 256
HALF = 128
NMAT = 8
SX, SY, SZ = 4, 6, 16
CELLS = SX * SY
GROUP = 3 * SZ
ROWS = CELLS * GROUP
ROW, COL, GZ = ("zq", "zr", "core"), ("y", "x"), "gz"
Z = ("gz", "zq", "zr")
f32, bf16 = jnp.float32, jnp.bfloat16


def lane(values, o, i, j):
    k = (3 * i + j) * 7 + o
    return jnp.broadcast_to(values[:, k : k + 1], (values.shape[0], PANEL))


def collect_kernel(modes_ref, panel_ref, z_ref, xlo_ref, xhi_ref, ylo_ref, yhi_ref, raw_ref, split_ref, sem):
    copy = pltpu.make_async_copy(modes_ref.at[:, :PANEL], raw_ref, sem)
    copy.start()
    copy.wait()
    panel_ref[...] = raw_ref[...].astype(f32)
    first = jnp.where(lax.axis_index(GZ) == 0, SZ - 1, 0)
    for h in range(2):
        part = slice(h * HALF, (h + 1) * HALF)
        split_ref[h] = raw_ref[:, part].astype(f32)
        z_ref[:, part] = split_ref.at[h][pl.ds(first, 3 * CELLS, stride=SZ), :].astype(bf16)
    side = SY * GROUP
    xlo_ref[...] = raw_ref[:side, :]
    xhi_ref[...] = raw_ref[ROWS - side :, :]
    for x in range(SX):
        ylo_ref[x * GROUP : (x + 1) * GROUP, :] = raw_ref[x * side : x * side + GROUP, :]
        yhi_ref[x * GROUP : (x + 1) * GROUP, :] = raw_ref[(x + 1) * side - GROUP : (x + 1) * side, :]


def local_kernel(kind_ref, blocks_ref, panel_ref, coef_ref, part_ref, inner_ref, table_ref):
    table_ref[...] = jnp.zeros((NMAT, 128), f32)
    for i in range(3):
        for j in range(3):
            k = (3 * i + j) * 7
            table_ref[:, k : k + 7] = blocks_ref[i, j]
    table = table_ref[...]
    offset = lax.broadcasted_iota(jnp.int32, (SZ, 128), 1) % 7
    kinds = jnp.concatenate([kind_ref[y] for y in range(SY)]).astype(f32).T
    for n in range(CELLS):
        x, y = divmod(n, SY)
        kind = jnp.broadcast_to(kinds[:, y * SX + x : y * SX + x + 1], (SZ, 128))
        coef = jnp.zeros((SZ, 128), f32)
        for m in range(NMAT):
            coef = jnp.where(kind == m, jnp.broadcast_to(table[m : m + 1, :], (SZ, 128)), coef)
        coef_ref[n] = coef
        outside = [o for o, at in ((1, x == SX - 1), (2, x == 0), (3, y == SY - 1), (4, y == 0)) if at]
        for o in outside:
            coef = jnp.where(offset == o, 0.0, coef)
        inner_ref[n] = coef
    level = lax.broadcasted_iota(jnp.int32, (SZ, PANEL), 0)

    def cell(n, carry):
        coef = inner_ref[n]
        total = [jnp.zeros((SZ, PANEL), f32) for _ in range(3)]
        last = CELLS - 1
        sources = (
            (1, jnp.minimum(n + SY, last)),
            (2, jnp.maximum(n - SY, 0)),
            (3, jnp.minimum(n + 1, last)),
            (4, jnp.maximum(n - 1, 0)),
        )

        def rows(at, j):
            return panel_ref[pl.ds(pl.multiple_of(at * GROUP + j * SZ, SZ), SZ), :]

        for j in range(3):
            own = rows(n, j)
            above = jnp.where(level == SZ - 1, 0.0, pltpu.roll(own, SZ - 1, 0))
            below = jnp.where(level == 0, 0.0, pltpu.roll(own, 1, 0))
            terms = [(0, own), (5, above), (6, below)] + [(o, rows(at, j)) for o, at in sources]
            for o, value in terms:
                for i in range(3):
                    total[i] = total[i] + lane(coef, o, i, j) * value
        for i in range(3):
            part_ref[pl.ds(pl.multiple_of(n * GROUP + i * SZ, SZ), SZ), :] = total[i]
        return carry

    lax.fori_loop(0, CELLS, cell, 0)


def finish_kernel(zface_ref, ylo_ref, yhi_ref, xlo_ref, xhi_ref, coef_ref, part_ref, modes_ref,
                  keep_ref, send_ref, work_ref, stiff_ref, zrow_ref):
    zrow_ref[...] = zface_ref[...].astype(f32)
    core, gz = lax.axis_index("core"), lax.axis_index("gz")
    level = lax.broadcasted_iota(jnp.int32, (SZ, 128), 0)
    edge = jnp.where(gz == 0, SZ - 1, 0)

    def face_z(n, carry):
        coef = coef_ref[n]
        mine = jnp.where(level == edge, jnp.where(gz == 0, coef, pltpu.roll(coef, 127, 1)), 0.0)
        for i in range(3):
            start = pl.multiple_of(n * GROUP + i * SZ, SZ)
            total = part_ref[pl.ds(start, SZ), :]
            for j in range(3):
                total = total + lane(mine, 5, i, j) * jnp.broadcast_to(zrow_ref[pl.ds(3 * n + j, 1), :], (SZ, PANEL))
            work_ref[pl.ds(start, SZ), :] = total
        return carry

    lax.fori_loop(0, CELLS, face_z, 0)

    def face(n, o, ref, k):
        coef = coef_ref[n]
        for i in range(3):
            start = n * GROUP + i * SZ
            total = work_ref[start : start + SZ, :]
            for j in range(3):
                value = ref[k * GROUP + j * SZ : k * GROUP + (j + 1) * SZ, :].astype(f32)
                total = total + lane(coef, o, i, j) * value
            work_ref[start : start + SZ, :] = total

    for y in range(SY):
        face((SX - 1) * SY + y, 1, xhi_ref, y)
        face(y, 2, xlo_ref, y)
    for x in range(SX):
        face(x * SY + SY - 1, 3, yhi_ref, x)
        face(x * SY, 4, ylo_ref, x)
    stiff_ref[...] = work_ref[...].astype(bf16).T
    for t in range(modes_ref.shape[1] // PANEL):
        product = jnp.dot(stiff_ref[...], modes_ref[:, t * PANEL : (t + 1) * PANEL], preferred_element_type=f32)
        low, high = product[:HALF], product[HALF:]
        keep = jnp.where(core == 0, low, high)
        send = jnp.where(core == 0, high, low).astype(bf16)
        for u in range(2):
            keep_ref[2 * t + u] = keep[:, u * HALF : (u + 1) * HALF]
            send_ref[2 * t + u] = send[:, u * HALF : (u + 1) * HALF]


def fold_kernel(planes_ref, half_ref):
    for r in range(4):
        total = planes_ref[r]
        for q in range(1, 4):
            total = total + planes_ref[4 * q + r]
        half_ref[:, 32 * r : 32 * (r + 1)] = total.T


def swap(value, axis):
    return lax.ppermute(value, axis, [(0, 1), (1, 0)])


def shards(modes, blocks, material):
    full = modes.shape[-1]
    flat = modes.transpose(0, 1, 3, 2, 4).reshape(ROWS, full)
    chain = [(i, i + 1) for i in range(15)]
    back = [(j, i) for i, j in chain]
    vmem = pl.BlockSpec(memory_space=pltpu.VMEM)
    shape = jax.ShapeDtypeStruct
    xside, yside = SY * GROUP, SX * GROUP
    panel, zsend, xfirst, xlast, yfirst, ylast = pl.pallas_call(
        collect_kernel,
        in_specs=[pl.BlockSpec(memory_space=pl.ANY)],
        out_specs=[vmem] * 6,
        out_shape=[shape((ROWS, PANEL), f32)]
        + [shape((rows, PANEL), bf16) for rows in (3 * CELLS, xside, xside, yside, yside)],
        scratch_shapes=[pltpu.VMEM((ROWS, PANEL), bf16), pltpu.VMEM((2, ROWS, HALF), f32), pltpu.SemaphoreType.DMA],
        compiler_params=pltpu.CompilerParams(vmem_limit_bytes=57 << 20),
        name="collect_faces",
    )(flat)
    zface = swap(zsend, GZ)
    ylo = lax.ppermute(ylast, COL, chain)
    yhi = lax.ppermute(yfirst, COL, back)
    xlo = lax.ppermute(xlast, ROW, chain)
    xhi = lax.ppermute(xfirst, ROW, back)
    coef, part = pl.pallas_call(
        local_kernel,
        in_specs=[vmem] * 3,
        out_specs=[vmem] * 2,
        out_shape=[shape((CELLS, SZ, 128), f32), shape((ROWS, PANEL), f32)],
        scratch_shapes=[pltpu.VMEM((CELLS, SZ, 128), f32), pltpu.VMEM((NMAT, 128), f32)],
        cost_estimate=pl.CostEstimate(flops=2 * ROWS * 21 * PANEL, bytes_accessed=3 * ROWS * PANEL, transcendentals=0),
        compiler_params=pltpu.CompilerParams(vmem_limit_bytes=24 << 20),
        name="local_stencil",
    )(material.transpose(1, 0, 2), blocks.transpose(2, 3, 0, 1), panel)
    tiles = full // HALF
    keep, send = pl.pallas_call(
        finish_kernel,
        in_specs=[vmem] * 8,
        out_specs=[vmem] * 2,
        out_shape=[shape((tiles, HALF, HALF), dtype) for dtype in (f32, bf16)],
        scratch_shapes=[pltpu.VMEM((ROWS, PANEL), f32), pltpu.VMEM((PANEL, ROWS), bf16), pltpu.VMEM((3 * CELLS, PANEL), f32)],
        cost_estimate=pl.CostEstimate(flops=2 * ROWS * full * PANEL, bytes_accessed=2 * ROWS * full, transcendentals=0),
        compiler_params=pltpu.CompilerParams(vmem_limit_bytes=32 << 20),
        name="faces_and_product",
    )(zface, ylo, yhi, xlo, xhi, coef, part, flat)
    mine = (keep + swap(send, "core").astype(f32)).astype(bf16)
    parts = lax.all_to_all(mine, COL, 0, 0, tiled=True)
    plane = jnp.sum(parts.astype(f32), axis=0).reshape(4, 32, HALF)
    near = jnp.sum(lax.all_to_all(plane, "zr", 0, 0, tiled=True), axis=0)
    copies = jnp.broadcast_to(near[None], (16,) + near.shape)
    planes = lax.all_to_all(copies, Z, 0, 0, tiled=True)
    half = pl.pallas_call(
        fold_kernel,
        in_specs=[vmem],
        out_specs=vmem,
        out_shape=shape((HALF, HALF), f32),
        name="fold",
    )(planes)
    other = swap(half, "core")
    first = lax.axis_index("core") == 0
    return jnp.concatenate([jnp.where(first, half, other), jnp.where(first, other, half)], axis=1)


def solution(mesh):
    split = Mesh(mesh.devices.reshape(2, 4, 2, 4, 4, 2), ("zq", "zr", "core", "y", "x", "gz"))
    return jax.shard_map(
        shards,
        mesh=split,
        in_specs=(P(ROW, COL, GZ, None, None), P(), P(ROW, COL, GZ)),
        out_specs=P(COL, None),
        check_vma=False,
    )
```

time: 110 us -> 107 us (0.973)
  local copies, waits for them, and re-layouts: 7.09 us -> 2.06 us
  Pallas kernels: 13.4 us -> 17.7 us
  blocking collectives: 46.5 us -> 45.3 us
    all_to_all x1, blocking collectives: 27.9 us -> 18.3 us  [shards(): planes = lax.all_to_all(copies, Z, 0, 0, tiled=True)]
    all_to_all x0 -> x1, blocking collectives: none -> 8.68 us  [shards(): near = jnp.sum(lax.all_to_all(plane, 'zr', 0, 0, tiled=True), axis=0)]
    pallas_call x1 -> x3, Pallas kernels: 6.96 us -> 11.3 us  [the longest x1 6.93 us: shards(): pl.pallas_call(local_kernel, in_specs=[vmem] * 3, out_specs=[vmem] * 2, o...]
    slice x2 -> x0, local copies, waits for them, and re-layouts: 1.96 us -> none  [the longest x1 1.01 us: shards(): xhi = lax.ppermute(panel[0].reshape(-1, PANEL), ROW, back)]
    unnamed x6 -> x8, local copies, waits for them, and re-layouts: 3.28 us -> 2.04 us
  transfers between devices with their start and end apart: 7 -> 7, of which waited for: 2 -> 2; matrix products, arithmetic and copies ran while one was open for 4% -> 0% of each run, Pallas kernels for 6% -> 6%
where the time goes in v2:
time: 107 us
  blocking collectives  45.3 us (42%)
  starting transfers between devices  36.7 us (34%)
  Pallas kernels  17.7 us (17%)
  waiting for transfers between devices  2.97 us (3%)
  local copies, waits for them, and re-layouts  2.06 us (2%)
  other arithmetic  1.74 us (2%)
    ppermute x3, starting transfers between devices, swap(): return lax.ppermute(value, axis, [(0, 1), (1, 0)])  24 us
    all_to_all x1, blocking collectives, shards(): parts = lax.all_to_all(mine, COL, 0, 0, tiled=True)  18.3 us
    all_to_all x1, blocking collectives, shards(): planes = lax.all_to_all(copies, Z, 0, 0, tiled=True)  18.3 us
    all_to_all x1, blocking collectives, shards(): near = jnp.sum(lax.all_to_all(plane, 'zr', 0, 0, tiled=True), axis=0)  8.68 us
    pallas_call x1, Pallas kernels, shards(): pl.pallas_call(local_kernel, in_specs=[vmem] * 3, out_specs=[vmem] * 2, o...  6.93 us
    pallas_call x1, Pallas kernels, shards(): pl.pallas_call(finish_kernel, in_specs=[vmem] * 8, out_specs=[vmem] * 2,...  6.41 us
    ppermute x1, starting transfers between devices, shards(): xhi = lax.ppermute(xfirst, ROW, back)  5.15 us
    ppermute x1, starting transfers between devices, shards(): xlo = lax.ppermute(xlast, ROW, chain)  4.94 us
  transfers between devices with their start and end apart: 7, of which 2 were waited for; matrix products, arithmetic and copies ran while one was open for 0% of the time, Pallas kernels for 6%

profile of v2, /device:TPU:1, one launch (start us, length us, event | category | flops | bytes accessed | tf_op | source)
XLA Modules:
  0.0 106.7 jit_solution(1704888408041308001)
XLA Ops:
  0.0 0.0 copy-start.3
  0.0 0.0 copy-start
  0.0 2.6 %collect_faces.1 = (f32[1152,256]{1,0:T(8,128)}, bf16[72,256]{1,0:T(8,128)(2,1)}, bf16[288,256]{1,0:T(8,128)(2,1)}, bf16[288,256]{1,0:T(8,128)(2,1)}, bf16[192,2...) custom-call(bf16[1152,2048]{1,0:T(8,128)(2,1)} %bitcast.6), custom_call_target="tpu_custom_call" | custom-call | tf_op jit(solution)/shard_map/collect_faces/pallas_call | solution.py:161
  2.6 4.9 %collective-permute-start.3 = (bf16[288,256]{1,0:T(8,128)(2,1)}, bf16[288,256]{1,0:T(8,128)(2,1)S(1)}, u32[]{:S(2)}, u32[]{:S(2)}) collective-permute-start(bf16[288,256]{1,0:T(8,128)(2,1)} %get-tuple-element.18), channel_id=1, source_target_pairs={{0,32},{32,64},{64,96},{96,128},{128,160},{160,192},{192,224},{224... | collective-permute-start | bytes 442376 | tf_op jit(solution)/shard_map/ppermute | solution.py:174
  7.5 5.1 %collective-permute-start.4 = (bf16[288,256]{1,0:T(8,128)(2,1)}, bf16[288,256]{1,0:T(8,128)(2,1)S(1)}, u32[]{:S(2)}, u32[]{:S(2)}) collective-permute-start(bf16[288,256]{1,0:T(8,128)(2,1)} %get-tuple-element.19), channel_id=1, source_target_pairs={{32,0},{64,32},{96,64},{128,96},{160,128},{192,160},{224,192},{256... | collective-permute-start | bytes 442376 | tf_op jit(solution)/shard_map/ppermute | solution.py:175
  12.7 1.3 %collective-permute-start.1 = (bf16[192,256]{1,0:T(8,128)(2,1)}, bf16[192,256]{1,0:T(8,128)(2,1)S(1)}, u32[]{:S(2)}, u32[]{:S(2)}) collective-permute-start(bf16[192,256]{1,0:T(8,128)(2,1)} %get-tuple-element.16), channel_id=1, source_target_pairs={{0,2},{2,4},{4,6},{6,8},{8,10},{10,12},{12,14},{14,16},{16,18},{18... | collective-permute-start | bytes 294920 | tf_op jit(solution)/shard_map/ppermute | solution.py:172
  14.0 1.3 %collective-permute-start.2 = (bf16[192,256]{1,0:T(8,128)(2,1)}, bf16[192,256]{1,0:T(8,128)(2,1)S(1)}, u32[]{:S(2)}, u32[]{:S(2)}) collective-permute-start(bf16[192,256]{1,0:T(8,128)(2,1)} %get-tuple-element.17), channel_id=1, source_target_pairs={{2,0},{4,2},{6,4},{8,6},{10,8},{12,10},{14,12},{16,14},{18,16},{20... | collective-permute-start | bytes 294920 | tf_op jit(solution)/shard_map/ppermute | solution.py:173
  15.3 13.1 %collective-permute-start = (bf16[72,256]{1,0:T(8,128)(2,1)}, bf16[72,256]{1,0:T(8,128)(2,1)S(1)}, u32[]{:S(2)}, u32[]{:S(2)}) collective-permute-start(bf16[72,256]{1,0:T(8,128)(2,1)} %get-tuple-element.15), channel_id=1, source_target_pairs={{0,1},{1,0},{2,3},{3,2},{4,5},{5,4},{6,7},{7,6},{8,9},{9,8},{10,11... | collective-permute-start | bytes 110600 | tf_op jit(solution)/shard_map/ppermute | solution.py:150
  28.4 0.0 copy-done.3
  28.4 0.0 copy-start.1
  28.4 1.3 %copy-done.1 = f32[1152,256]{1,0:T(8,128)S(1)} copy-done((f32[1152,256]{1,0:T(8,128)S(1)}, f32[1152,256]{1,0:T(8,128)}, u32[]{:S(2)}) %copy-start.1) | copy-done | bytes 1179672
  29.7 0.8 copy-done.2
  30.5 6.9 %local_stencil.1 = (f32[24,16,128]{2,1,0:T(8,128)S(1)}, f32[1152,256]{1,0:T(8,128)S(1)}) custom-call(s32[6,4,16]{2,1,0:T(4,128)S(1)} %bitcast.9, f32[3,3,8,7]{3,2,1,0:T(8,128)S(1)} %bitcast.8, f32[1152,256]{1,0:T(8,128)S(1)} %copy-done.1), custom_call_target="tpu_custom_call" | custom-call | flops 12386304 | bytes 884736 | tf_op jit(solution)/shard_map/local_stencil/pallas_call | solution.py:176
  37.4 0.0 collective-permute-done.zface_ref
  37.4 0.0 collective-permute-done.1.ylo_ref
  37.4 0.0 collective-permute-done.2.yhi_ref
  37.4 0.0 collective-permute-done.3.xlo_ref
  37.5 0.0 collective-permute-done.4.xhi_ref
  37.5 0.0 copy-done
  37.5 6.4 %faces_and_product.1 = (f32[16,128,128]{2,1,0:T(8,128)S(1)}, bf16[16,128,128]{2,1,0:T(8,128)(2,1)S(1)}) custom-call(bf16[72,256]{1,0:T(8,128)(2,1)S(1)} %collective-permute-done.zface_ref, bf16[192,256]{1,0:T(8,128)(2,1)S(1)} %collective-permute-done.1.ylo_ref, bf16[192,256]{1,0:T(8,128)(2,1)S(1)} %collective-permute-done.2.yhi_ref, ...), custom_call_target="tpu_custom_call" | custom-call | flops 1207959552 | bytes 4718592 | tf_op jit(solution)/shard_map/faces_and_product/pallas_call | solution.py:187
  43.9 1.9 %collective-permute-start.5 = (bf16[16,128,128]{2,1,0:T(8,128)(2,1)S(1)}, bf16[16,128,128]{2,1,0:T(8,128)(2,1)S(1)}, u32[]{:S(2)}, u32[]{:S(2)}) collective-permute-start(bf16[16,128,128]{2,1,0:T(8,128)(2,1)S(1)} %get-tuple-element.24), channel_id=1, source_target_pairs={{0,32},{32,0},{1,33},{33,1},{2,34},{34,2},{3,35},{35,3},{4,36},{36... | collective-permute-start | bytes 1572872 | tf_op jit(solution)/shard_map/ppermute | solution.py:150
  45.8 1.9 %collective-permute-done.5 = bf16[16,128,128]{2,1,0:T(8,128)(2,1)S(1)} collective-permute-done((bf16[16,128,128]{2,1,0:T(8,128)(2,1)S(1)}, bf16[16,128,128]{2,1,0:T(8,128)(2,1)S(1)}, u32[]{:S(2)}, u32[]{:S(2)}) %collective-permute-start.5) | collective-permute-done | bytes 524320 | tf_op jit(solution)/shard_map/ppermute | solution.py:150
  47.7 0.1 add_convert_fusion
  47.8 18.3 %all_to_all.15 = bf16[16,128,128]{2,1,0:T(8,128)(2,1)S(1)} all-to-all(bf16[16,128,128]{2,1,0:T(8,128)(2,1)S(1)} %add_convert_fusion), channel_id=1, replica_groups=mesh['zq'=2,'zr'=4,'core'=2,'y'=4,'x'=4,'gz'=2] {'y','x'}, dimensions={0} | all-to-all | bytes 1048576 | tf_op jit(solution)/shard_map/all_to_all | solution.py:198
  66.2 0.1 convert_reduce_fusion
  66.3 8.7 %all_to_all.16 = f32[4,32,128]{2,1,0:T(8,128)S(1)} all-to-all(f32[4,32,128]{2,1,0:T(8,128)S(1)} %bitcast.10), channel_id=1, replica_groups=mesh['zq'=2,'zr'=4,'core'=2,'y'=4,'x'=4,'gz'=2] {'zr'}, dimensions={0} | all-to-all | bytes 131072 | tf_op jit(solution)/shard_map/all_to_all | solution.py:200
  75.0 18.3 %all_to_all.17.planes_ref = f32[16,32,128]{2,1,0:T(8,128)} all-to-all(f32[16,32,128]{2,1,0:T(8,128)S(1)} %broadcast_in_dim.2), channel_id=1, replica_groups=mesh['zq'=2,'zr'=4,'core'=2,'y'=4,'x'=4,'gz'=2] {'gz','zq','zr'}, dimensions={0} | all-to-all | bytes 524288 | tf_op jit(solution)/shard_map/all_to_all | solution.py:202
  93.3 1.8 %fold.1 = f32[128,128]{1,0:T(8,128)} custom-call(f32[16,32,128]{2,1,0:T(8,128)} %all_to_all.17.planes_ref), custom_call_target="tpu_custom_call" | custom-call | tf_op jit(solution)/shard_map/fold/pallas_call | solution.py:203
  95.1 9.0 %collective-permute-start.6 = (f32[128,128]{1,0:T(8,128)}, f32[128,128]{1,0:T(8,128)S(1)}, u32[]{:S(2)}, u32[]{:S(2)}) collective-permute-start(f32[128,128]{1,0:T(8,128)} %fold.1), channel_id=1, source_target_pairs={{0,32},{32,0},{1,33},{33,1},{2,34},{34,2},{3,35},{35,3},{4,36},{36... | collective-permute-start | bytes 196616 | tf_op jit(solution)/shard_map/ppermute | solution.py:150
  104.1 1.1 %collective-permute-done.6 = f32[128,128]{1,0:T(8,128)S(1)} collective-permute-done((f32[128,128]{1,0:T(8,128)}, f32[128,128]{1,0:T(8,128)S(1)}, u32[]{:S(2)}, u32[]{:S(2)}) %collective-permute-start.6) | collective-permute-done | bytes 65568 | tf_op jit(solution)/shard_map/ppermute | solution.py:150
  105.2 0.8 broadcast_select_fusion.1
  106.0 0.7 pad_maximum_fusion
  (3 shorter events, 0.0 us)
Async XLA Ops:
  0.0 28.4 %copy-start.3 = (s32[4,6,16]{2,0,1:T(4,128)S(1)}, s32[4,6,16]{2,0,1:T(4,128)}, u32[]{:S(2)}) copy-start(s32[4,6,16]{2,0,1:T(4,128)} %param.5) | copy-start | bytes 4612
  0.0 37.5 %copy-start = (bf16[4,6,16,3,2048]{4,2,3,1,0:T(8,128)(2,1)S(1)}, bf16[4,6,16,3,2048]{4,2,3,1,0:T(8,128)(2,1)}, u32[]{:S(2)}) copy-start(bf16[4,6,16,3,2048]{4,2,3,1,0:T(8,128)(2,1)} %param.3) | copy-start | bytes 14155780
  2.6 34.9 %collective-permute-start.3 = (bf16[288,256]{1,0:T(8,128)(2,1)}, bf16[288,256]{1,0:T(8,128)(2,1)S(1)}, u32[]{:S(2)}, u32[]{:S(2)}) collective-permute-start(bf16[288,256]{1,0:T(8,128)(2,1)} %get-tuple-element.18), channel_id=1, source_target_pairs={{0,32},{32,64},{64,96},{96,128},{128,160},{160,192},{192,224},{224... | collective-permute-start | bytes 442376 | tf_op jit(solution)/shard_map/ppermute | solution.py:174
  7.5 29.9 %collective-permute-start.4 = (bf16[288,256]{1,0:T(8,128)(2,1)}, bf16[288,256]{1,0:T(8,128)(2,1)S(1)}, u32[]{:S(2)}, u32[]{:S(2)}) collective-permute-start(bf16[288,256]{1,0:T(8,128)(2,1)} %get-tuple-element.19), channel_id=1, source_target_pairs={{32,0},{64,32},{96,64},{128,96},{160,128},{192,160},{224,192},{256... | collective-permute-start | bytes 442376 | tf_op jit(solution)/shard_map/ppermute | solution.py:175
  12.7 24.7 %collective-permute-start.1 = (bf16[192,256]{1,0:T(8,128)(2,1)}, bf16[192,256]{1,0:T(8,128)(2,1)S(1)}, u32[]{:S(2)}, u32[]{:S(2)}) collective-permute-start(bf16[192,256]{1,0:T(8,128)(2,1)} %get-tuple-element.16), channel_id=1, source_target_pairs={{0,2},{2,4},{4,6},{6,8},{8,10},{10,12},{12,14},{14,16},{16,18},{18... | collective-permute-start | bytes 294920 | tf_op jit(solution)/shard_map/ppermute | solution.py:172
  14.0 23.4 %collective-permute-start.2 = (bf16[192,256]{1,0:T(8,128)(2,1)}, bf16[192,256]{1,0:T(8,128)(2,1)S(1)}, u32[]{:S(2)}, u32[]{:S(2)}) collective-permute-start(bf16[192,256]{1,0:T(8,128)(2,1)} %get-tuple-element.17), channel_id=1, source_target_pairs={{2,0},{4,2},{6,4},{8,6},{10,8},{12,10},{14,12},{16,14},{18,16},{20... | collective-permute-start | bytes 294920 | tf_op jit(solution)/shard_map/ppermute | solution.py:173
  15.3 22.1 %collective-permute-start = (bf16[72,256]{1,0:T(8,128)(2,1)}, bf16[72,256]{1,0:T(8,128)(2,1)S(1)}, u32[]{:S(2)}, u32[]{:S(2)}) collective-permute-start(bf16[72,256]{1,0:T(8,128)(2,1)} %get-tuple-element.15), channel_id=1, source_target_pairs={{0,1},{1,0},{2,3},{3,2},{4,5},{5,4},{6,7},{7,6},{8,9},{9,8},{10,11... | collective-permute-start | bytes 110600 | tf_op jit(solution)/shard_map/ppermute | solution.py:150
  28.4 1.3 %copy-start.1 = (f32[1152,256]{1,0:T(8,128)S(1)}, f32[1152,256]{1,0:T(8,128)}, u32[]{:S(2)}) copy-start(f32[1152,256]{1,0:T(8,128)} %get-tuple-element.20.panel_ref) | copy-start | bytes 3538948
  29.7 0.8 copy-start.2
  43.9 3.8 %collective-permute-start.5 = (bf16[16,128,128]{2,1,0:T(8,128)(2,1)S(1)}, bf16[16,128,128]{2,1,0:T(8,128)(2,1)S(1)}, u32[]{:S(2)}, u32[]{:S(2)}) collective-permute-start(bf16[16,128,128]{2,1,0:T(8,128)(2,1)S(1)} %get-tuple-element.24), channel_id=1, source_target_pairs={{0,32},{32,0},{1,33},{33,1},{2,34},{34,2},{3,35},{35,3},{4,36},{36... | collective-permute-start | bytes 1572872 | tf_op jit(solution)/shard_map/ppermute | solution.py:150
  95.1 10.1 %collective-permute-start.6 = (f32[128,128]{1,0:T(8,128)}, f32[128,128]{1,0:T(8,128)S(1)}, u32[]{:S(2)}, u32[]{:S(2)}) collective-permute-start(f32[128,128]{1,0:T(8,128)} %fold.1), channel_id=1, source_target_pairs={{0,32},{32,0},{1,33},{33,1},{2,34},{34,2},{3,35},{35,3},{4,36},{36... | collective-permute-start | bytes 196616 | tf_op jit(solution)/shard_map/ppermute | solution.py:150

commit v3 on v2

--- a/solution.py
+++ b/solution.py
@@ -12,17 +12,19 @@
 CELLS = SX * SY
 GROUP = 3 * SZ
 ROWS = CELLS * GROUP
-ROW, COL, GZ = ("zq", "zr", "core"), ("y", "x"), "gz"
-Z = ("gz", "zq", "zr")
+EDGE = 3 * CELLS
+TALL = PANEL + 80
+ROW, COL, GZ = ("zh", "zl", "core"), ("y", "x"), "gz"
+Z = ("gz", "zh", "zl")
 f32, bf16 = jnp.float32, jnp.bfloat16
 
 
-def lane(values, o, i, j):
+def lane(values, o, i, j, width=PANEL):
     k = (3 * i + j) * 7 + o
-    return jnp.broadcast_to(values[:, k : k + 1], (values.shape[0], PANEL))
-
-
-def collect_kernel(modes_ref, panel_ref, z_ref, xlo_ref, xhi_ref, ylo_ref, yhi_ref, raw_ref, split_ref, sem):
+    return jnp.broadcast_to(values[:, k : k + 1], (values.shape[0], width))
+
+
+def collect_kernel(modes_ref, panel_ref, z_ref, xlo_ref, xhi_ref, ylo_ref, yhi_ref, raw_ref, split_ref, edge_ref, sem):
     copy = pltpu.make_async_copy(modes_ref.at[:, :PANEL], raw_ref, sem)
     copy.start()
     copy.wait()
@@ -31,7 +33,10 @@
     for h in range(2):
         part = slice(h * HALF, (h + 1) * HALF)
         split_ref[h] = raw_ref[:, part].astype(f32)
-        z_ref[:, part] = split_ref.at[h][pl.ds(first, 3 * CELLS, stride=SZ), :].astype(bf16)
+        for j in range(3):
+            rows = split_ref.at[h][pl.ds(j * SZ + first, CELLS, stride=GROUP), :]
+            edge_ref[j * CELLS : (j + 1) * CELLS, part] = rows
+    z_ref[...] = edge_ref[...].astype(bf16)
     side = SY * GROUP
     xlo_ref[...] = raw_ref[:side, :]
     xhi_ref[...] = raw_ref[ROWS - side :, :]
@@ -91,45 +96,55 @@
     lax.fori_loop(0, CELLS, cell, 0)
 
 
-def finish_kernel(zface_ref, ylo_ref, yhi_ref, xlo_ref, xhi_ref, coef_ref, part_ref, modes_ref,
-                  keep_ref, send_ref, work_ref, stiff_ref, zrow_ref):
-    zrow_ref[...] = zface_ref[...].astype(f32)
-    core, gz = lax.axis_index("core"), lax.axis_index("gz")
-    level = lax.broadcasted_iota(jnp.int32, (SZ, 128), 0)
+def product_kernel(ylo_ref, yhi_ref, xlo_ref, xhi_ref, coef_ref, part_ref, modes_ref,
+                   sum_ref, edge_ref, edge_modes_ref, edge_coef_ref, stiff_ref, left_ref):
+    gz = lax.axis_index(GZ)
     edge = jnp.where(gz == 0, SZ - 1, 0)
-
-    def face_z(n, carry):
-        coef = coef_ref[n]
-        mine = jnp.where(level == edge, jnp.where(gz == 0, coef, pltpu.roll(coef, 127, 1)), 0.0)
-        for i in range(3):
-            start = pl.multiple_of(n * GROUP + i * SZ, SZ)
-            total = part_ref[pl.ds(start, SZ), :]
-            for j in range(3):
-                total = total + lane(mine, 5, i, j) * jnp.broadcast_to(zrow_ref[pl.ds(3 * n + j, 1), :], (SZ, PANEL))
-            work_ref[pl.ds(start, SZ), :] = total
-        return carry
-
-    lax.fori_loop(0, CELLS, face_z, 0)
-
-    def face(n, o, ref, k):
-        coef = coef_ref[n]
+    level = lax.broadcasted_iota(jnp.int32, (SZ, PANEL), 0)
+    for n in range(CELLS):
+        x, y = divmod(n, SY)
+        coef = coef_ref[n * SZ : (n + 1) * SZ, :]
+        faces = [(1, xhi_ref, y)] if x == SX - 1 else []
+        faces += [(2, xlo_ref, y)] if x == 0 else []
+        faces += [(3, yhi_ref, x)] if y == SY - 1 else []
+        faces += [(4, ylo_ref, x)] if y == 0 else []
         for i in range(3):
             start = n * GROUP + i * SZ
-            total = work_ref[start : start + SZ, :]
-            for j in range(3):
-                value = ref[k * GROUP + j * SZ : k * GROUP + (j + 1) * SZ, :].astype(f32)
-                total = total + lane(coef, o, i, j) * value
-            work_ref[start : start + SZ, :] = total
-
-    for y in range(SY):
-        face((SX - 1) * SY + y, 1, xhi_ref, y)
-        face(y, 2, xlo_ref, y)
-    for x in range(SX):
-        face(x * SY + SY - 1, 3, yhi_ref, x)
-        face(x * SY, 4, ylo_ref, x)
-    stiff_ref[...] = work_ref[...].astype(bf16).T
+            total = part_ref[start : start + SZ, :]
+            for o, ref, k in faces:
+                for j in range(3):
+                    value = ref[k * GROUP + j * SZ : k * GROUP + (j + 1) * SZ, :].astype(f32)
+                    total = total + lane(coef, o, i, j) * value
+            row = i * CELLS + n
+            edge_ref[row : row + 1, :] = jnp.where(gz == 0, total[SZ - 1 :], total[:1])
+            stiff_ref[start : start + SZ, :] = jnp.where(level == edge, 0.0, total).astype(bf16)
+    left_ref[:PANEL, :] = stiff_ref[...].T
+    row = lax.broadcasted_iota(jnp.int32, (TALL - PANEL, ROWS), 0)
+    column = lax.broadcasted_iota(jnp.int32, (TALL - PANEL, ROWS), 1)
+    target = (row % CELLS) * GROUP + (row // CELLS) * SZ + edge
+    left_ref[PANEL:, :] = jnp.where((column == target) & (row < EDGE), 1.0, 0.0).astype(bf16)
+    edge_coef_ref[...] = coef_ref[pl.ds(edge, CELLS, stride=SZ), :]
     for t in range(modes_ref.shape[1] // PANEL):
-        product = jnp.dot(stiff_ref[...], modes_ref[:, t * PANEL : (t + 1) * PANEL], preferred_element_type=f32)
+        part = slice(t * PANEL, (t + 1) * PANEL)
+        product = jnp.dot(left_ref[...], modes_ref[:, part], preferred_element_type=f32)
+        sum_ref[:, part] = product[:PANEL]
+        edge_modes_ref[:, part] = product[PANEL:].astype(bf16)
+
+
+def edge_kernel(zface_ref, sum_ref, edge_ref, edge_modes_ref, edge_coef_ref, keep_ref, send_ref, stiff_ref):
+    core, gz = lax.axis_index("core"), lax.axis_index(GZ)
+    coef = edge_coef_ref[...]
+    coef = jnp.where(gz == 0, coef, pltpu.roll(coef, 127, 1))
+    stiff_ref[...] = jnp.zeros(stiff_ref.shape, f32)
+    for i in range(3):
+        total = edge_ref[i * CELLS : (i + 1) * CELLS, :]
+        for j in range(3):
+            total = total + lane(coef, 5, i, j) * zface_ref[j * CELLS : (j + 1) * CELLS, :].astype(f32)
+        stiff_ref[i * CELLS : (i + 1) * CELLS, :] = total
+    left = stiff_ref[...].T.astype(bf16)
+    for t in range(sum_ref.shape[1] // PANEL):
+        part = slice(t * PANEL, (t + 1) * PANEL)
+        product = sum_ref[:, part] + jnp.dot(left, edge_modes_ref[:, part], preferred_element_type=f32)
         low, high = product[:HALF], product[HALF:]
         keep = jnp.where(core == 0, low, high)
         send = jnp.where(core == 0, high, low).astype(bf16)
@@ -138,12 +153,21 @@
             send_ref[2 * t + u] = send[:, u * HALF : (u + 1) * HALF]
 
 
+def near_kernel(parts_ref, copies_ref):
+    total = parts_ref[0].astype(f32)
+    for k in range(1, parts_ref.shape[0]):
+        total = total + parts_ref[k].astype(f32)
+    total = total.astype(bf16)
+    for k in range(copies_ref.shape[0]):
+        copies_ref[k] = total
+
+
 def fold_kernel(planes_ref, half_ref):
-    for r in range(4):
-        total = planes_ref[r]
-        for q in range(1, 4):
-            total = total + planes_ref[4 * q + r]
-        half_ref[:, 32 * r : 32 * (r + 1)] = total.T
+    for r in range(2):
+        total = planes_ref[r].astype(f32)
+        for q in range(1, 8):
+            total = total + planes_ref[2 * q + r].astype(f32)
+        half_ref[:, 64 * r : 64 * (r + 1)] = total.T
 
 
 def swap(value, axis):
@@ -164,7 +188,7 @@
         out_specs=[vmem] * 6,
         out_shape=[shape((ROWS, PANEL), f32)]
         + [shape((rows, PANEL), bf16) for rows in (3 * CELLS, xside, xside, yside, yside)],
-        scratch_shapes=[pltpu.VMEM((ROWS, PANEL), bf16), pltpu.VMEM((2, ROWS, HALF), f32), pltpu.SemaphoreType.DMA],
+        scratch_shapes=[pltpu.VMEM((ROWS, PANEL), bf16), pltpu.VMEM((2, ROWS, HALF), f32), pltpu.VMEM((EDGE, PANEL), f32), pltpu.SemaphoreType.DMA],
         compiler_params=pltpu.CompilerParams(vmem_limit_bytes=57 << 20),
         name="collect_faces",
     )(flat)
@@ -184,27 +208,48 @@
         name="local_stencil",
     )(material.transpose(1, 0, 2), blocks.transpose(2, 3, 0, 1), panel)
     tiles = full // HALF
+    total, edge, edge_modes, edge_coef = pl.pallas_call(
+        product_kernel,
+        in_specs=[vmem] * 7,
+        out_specs=[vmem] * 4,
+        out_shape=[
+            shape((PANEL, full), f32),
+            shape((EDGE, PANEL), f32),
+            shape((TALL - PANEL, full), bf16),
+            shape((CELLS, 128), f32),
+        ],
+        scratch_shapes=[pltpu.VMEM((ROWS, PANEL), bf16), pltpu.VMEM((TALL, ROWS), bf16)],
+        cost_estimate=pl.CostEstimate(flops=2 * ROWS * full * TALL, bytes_accessed=2 * ROWS * full, transcendentals=0),
+        compiler_params=pltpu.CompilerParams(vmem_limit_bytes=32 << 20),
+        name="faces_and_product",
+    )(ylo, yhi, xlo, xhi, coef.reshape(CELLS * SZ, 128), part, flat)
     keep, send = pl.pallas_call(
-        finish_kernel,
-        in_specs=[vmem] * 8,
+        edge_kernel,
+        in_specs=[vmem] * 5,
         out_specs=[vmem] * 2,
         out_shape=[shape((tiles, HALF, HALF), dtype) for dtype in (f32, bf16)],
-        scratch_shapes=[pltpu.VMEM((ROWS, PANEL), f32), pltpu.VMEM((PANEL, ROWS), bf16), pltpu.VMEM((3 * CELLS, PANEL), f32)],
-        cost_estimate=pl.CostEstimate(flops=2 * ROWS * full * PANEL, bytes_accessed=2 * ROWS * full, transcendentals=0),
-        compiler_params=pltpu.CompilerParams(vmem_limit_bytes=32 << 20),
-        name="faces_and_product",
-    )(zface, ylo, yhi, xlo, xhi, coef, part, flat)
+        scratch_shapes=[pltpu.VMEM((TALL - PANEL, PANEL), f32)],
+        cost_estimate=pl.CostEstimate(flops=2 * EDGE * full * PANEL, bytes_accessed=4 * PANEL * full, transcendentals=0),
+        compiler_params=pltpu.CompilerParams(vmem_limit_bytes=24 << 20),
+        name="edge_rows",
+    )(zface, total, edge, edge_modes, edge_coef)
     mine = (keep + swap(send, "core").astype(f32)).astype(bf16)
-    parts = lax.all_to_all(mine, COL, 0, 0, tiled=True)
-    plane = jnp.sum(parts.astype(f32), axis=0).reshape(4, 32, HALF)
-    near = jnp.sum(lax.all_to_all(plane, "zr", 0, 0, tiled=True), axis=0)
-    copies = jnp.broadcast_to(near[None], (16,) + near.shape)
+    parts = lax.all_to_all(mine.reshape(2 * tiles, HALF // 2, HALF), COL + ("zl",), 0, 0, tiled=True)
+    copies = pl.pallas_call(
+        near_kernel,
+        in_specs=[vmem],
+        out_specs=vmem,
+        out_shape=shape((16, HALF // 2, HALF), bf16),
+        compiler_params=pltpu.CompilerParams(vmem_limit_bytes=4 << 20),
+        name="near_sum",
+    )(parts)
     planes = lax.all_to_all(copies, Z, 0, 0, tiled=True)
     half = pl.pallas_call(
         fold_kernel,
         in_specs=[vmem],
         out_specs=vmem,
         out_shape=shape((HALF, HALF), f32),
+        compiler_params=pltpu.CompilerParams(vmem_limit_bytes=4 << 20),
         name="fold",
     )(planes)
     other = swap(half, "core")
@@ -213,7 +258,7 @@
 
 
 def solution(mesh):
-    split = Mesh(mesh.devices.reshape(2, 4, 2, 4, 4, 2), ("zq", "zr", "core", "y", "x", "gz"))
+    split = Mesh(mesh.devices.reshape(4, 2, 2, 4, 4, 2), ("zh", "zl", "core", "y", "x", "gz"))
     return jax.shard_map(
         shards,
         mesh=split,

time: 107 us -> 93.9 us (0.88)
  blocking collectives: 45.3 us -> 38.1 us
  Pallas kernels: 17.7 us -> 13.2 us
    all_to_all x2 -> x1, blocking collectives: 27 us -> 21.1 us  [shards(): lax.all_to_all(mine.reshape(2 * tiles, HALF // 2, HALF), COL + ('zl',), 0...]
    pallas_call x1 -> x3, Pallas kernels: 6.41 us -> 3.47 us  [the longest x1 2.73 us: shards(): pl.pallas_call(product_kernel, in_specs=[vmem] * 7, out_specs=[vmem] * 4,...]
    pallas_call x1, Pallas kernels: 1.8 us -> 0.18 us  [shards(): pl.pallas_call(fold_kernel, in_specs=[vmem], out_specs=vmem, out_shape=sh...]
    all_to_all x1, blocking collectives: 18.3 us -> 17 us  [shards(): planes = lax.all_to_all(copies, Z, 0, 0, tiled=True)]
  transfers between devices with their start and end apart: 7 -> 7, of which waited for: 2 -> 2; matrix products, arithmetic and copies ran while one was open for 0% -> 0% of each run, Pallas kernels for 6% -> 10%
where the time goes in v3:
time: 93.9 us; the launch traced here: 93.5 us
  blocking collectives  38.1 us (41%)
  starting transfers between devices  36.4 us (39%)
  Pallas kernels  13.2 us (14%)
  waiting for transfers between devices  2.76 us (3%)
  local copies, waits for them, and re-layouts  2.04 us (2%)
    ppermute x3, starting transfers between devices, swap(): return lax.ppermute(value, axis, [(0, 1), (1, 0)])  23.7 us
    all_to_all x1, blocking collectives, shards(): lax.all_to_all(mine.reshape(2 * tiles, HALF // 2, HALF), COL + ('zl',), 0...  21.1 us
    all_to_all x1, blocking collectives, shards(): planes = lax.all_to_all(copies, Z, 0, 0, tiled=True)  17 us
    pallas_call x1, Pallas kernels, shards(): pl.pallas_call(local_kernel, in_specs=[vmem] * 3, out_specs=[vmem] * 2, o...  6.93 us
    ppermute x1, starting transfers between devices, shards(): xhi = lax.ppermute(xfirst, ROW, back)  5.15 us
    ppermute x1, starting transfers between devices, shards(): xlo = lax.ppermute(xlast, ROW, chain)  4.94 us
    ppermute x3, waiting for transfers between devices, swap(): return lax.ppermute(value, axis, [(0, 1), (1, 0)])  2.75 us
    pallas_call x1, Pallas kernels, shards(): pl.pallas_call(product_kernel, in_specs=[vmem] * 7, out_specs=[vmem] * 4,...  2.73 us
  transfers between devices with their start and end apart: 7, of which 2 were waited for; matrix products, arithmetic and copies ran while one was open for 0% of the time, Pallas kernels for 10%

profile of v3, /device:TPU:1, one launch (start us, length us, event | category | flops | bytes accessed | tf_op | source)
XLA Modules:
  0.0 93.5 jit_solution(629516015923021968)
XLA Ops:
  0.0 0.0 copy-start.3
  0.0 0.0 copy-start
  0.0 2.6 %collect_faces.1 = (f32[1152,256]{1,0:T(8,128)}, bf16[72,256]{1,0:T(8,128)(2,1)}, bf16[288,256]{1,0:T(8,128)(2,1)}, bf16[288,256]{1,0:T(8,128)(2,1)}, bf16[192,2...) custom-call(bf16[1152,2048]{1,0:T(8,128)(2,1)} %bitcast.7), custom_call_target="tpu_custom_call" | custom-call | tf_op jit(solution)/shard_map/collect_faces/pallas_call | solution.py:185
  2.6 4.9 %collective-permute-start.3 = (bf16[288,256]{1,0:T(8,128)(2,1)}, bf16[288,256]{1,0:T(8,128)(2,1)S(1)}, u32[]{:S(2)}, u32[]{:S(2)}) collective-permute-start(bf16[288,256]{1,0:T(8,128)(2,1)} %get-tuple-element.22), channel_id=1, source_target_pairs={{0,32},{32,64},{64,96},{96,128},{128,160},{160,192},{192,224},{224... | collective-permute-start | bytes 442376 | tf_op jit(solution)/shard_map/ppermute | solution.py:198
  7.5 5.1 %collective-permute-start.4 = (bf16[288,256]{1,0:T(8,128)(2,1)}, bf16[288,256]{1,0:T(8,128)(2,1)S(1)}, u32[]{:S(2)}, u32[]{:S(2)}) collective-permute-start(bf16[288,256]{1,0:T(8,128)(2,1)} %get-tuple-element.23), channel_id=1, source_target_pairs={{32,0},{64,32},{96,64},{128,96},{160,128},{192,160},{224,192},{256... | collective-permute-start | bytes 442376 | tf_op jit(solution)/shard_map/ppermute | solution.py:199
  12.7 1.3 %collective-permute-start.1 = (bf16[192,256]{1,0:T(8,128)(2,1)}, bf16[192,256]{1,0:T(8,128)(2,1)S(1)}, u32[]{:S(2)}, u32[]{:S(2)}) collective-permute-start(bf16[192,256]{1,0:T(8,128)(2,1)} %get-tuple-element.20), channel_id=1, source_target_pairs={{0,2},{2,4},{4,6},{6,8},{8,10},{10,12},{12,14},{14,16},{16,18},{18... | collective-permute-start | bytes 294920 | tf_op jit(solution)/shard_map/ppermute | solution.py:196
  14.0 1.3 %collective-permute-start.2 = (bf16[192,256]{1,0:T(8,128)(2,1)}, bf16[192,256]{1,0:T(8,128)(2,1)S(1)}, u32[]{:S(2)}, u32[]{:S(2)}) collective-permute-start(bf16[192,256]{1,0:T(8,128)(2,1)} %get-tuple-element.21), channel_id=1, source_target_pairs={{2,0},{4,2},{6,4},{8,6},{10,8},{12,10},{14,12},{16,14},{18,16},{20... | collective-permute-start | bytes 294920 | tf_op jit(solution)/shard_map/ppermute | solution.py:197
  15.3 13.1 %collective-permute-start = (bf16[72,256]{1,0:T(8,128)(2,1)}, bf16[72,256]{1,0:T(8,128)(2,1)S(1)}, u32[]{:S(2)}, u32[]{:S(2)}) collective-permute-start(bf16[72,256]{1,0:T(8,128)(2,1)} %get-tuple-element.19), channel_id=1, source_target_pairs={{0,1},{1,0},{2,3},{3,2},{4,5},{5,4},{6,7},{7,6},{8,9},{9,8},{10,11... | collective-permute-start | bytes 110600 | tf_op jit(solution)/shard_map/ppermute | solution.py:174
  28.4 0.0 copy-done.3
  28.4 0.0 copy-start.1
  28.5 1.3 %copy-done.1 = f32[1152,256]{1,0:T(8,128)S(1)} copy-done((f32[1152,256]{1,0:T(8,128)S(1)}, f32[1152,256]{1,0:T(8,128)}, u32[]{:S(2)}) %copy-start.1) | copy-done | bytes 1179672
  29.7 0.0 copy-start.2
  29.7 0.8 copy-done.2
  30.5 6.9 %local_stencil.1 = (f32[24,16,128]{2,1,0:T(8,128)S(1)}, f32[1152,256]{1,0:T(8,128)S(1)}) custom-call(s32[6,4,16]{2,1,0:T(4,128)S(1)} %bitcast.11, f32[3,3,8,7]{3,2,1,0:T(8,128)S(1)} %bitcast.10, f32[1152,256]{1,0:T(8,128)S(1)} %copy-done.1), custom_call_target="tpu_custom_call" | custom-call | flops 12386304 | bytes 884736 | tf_op jit(solution)/shard_map/local_stencil/pallas_call | solution.py:200
  37.4 0.0 collective-permute-done.1.ylo_ref
  37.4 0.0 collective-permute-done.2.yhi_ref
  37.4 0.0 collective-permute-done.3.xlo_ref
  37.5 0.0 collective-permute-done.4.xhi_ref
  37.5 0.0 copy-done
  37.5 2.7 %faces_and_product.1 = (f32[256,2048]{1,0:T(8,128)S(1)}, f32[72,256]{1,0:T(8,128)S(1)}, bf16[80,2048]{1,0:T(8,128)(2,1)S(1)}, f32[24,128]{1,0:T(8,128)S(1)}) custom-call(bf16[192,256]{1,0:T(8,128)(2,1)S(1)} %collective-permute-done.1.ylo_ref, bf16[192,256]{1,0:T(8,128)(2,1)S(1)} %collective-permute-done.2.yhi_ref, ...), custom_call_target="tpu_custom_call" | custom-call | flops 1585446912 | bytes 4718592 | tf_op jit(solution)/shard_map/faces_and_product/pallas_call | solution.py:211
  40.2 0.0 collective-permute-done.zface_ref
  40.2 0.7 edge_rows.1
  40.9 1.9 %collective-permute-start.5 = (bf16[16,128,128]{2,1,0:T(8,128)(2,1)S(1)}, bf16[16,128,128]{2,1,0:T(8,128)(2,1)S(1)}, u32[]{:S(2)}, u32[]{:S(2)}) collective-permute-start(bf16[16,128,128]{2,1,0:T(8,128)(2,1)S(1)} %get-tuple-element.32), channel_id=1, source_target_pairs={{0,32},{32,0},{1,33},{33,1},{2,34},{34,2},{3,35},{35,3},{4,36},{36... | collective-permute-start | bytes 1572872 | tf_op jit(solution)/shard_map/ppermute | solution.py:174
  42.8 1.9 %collective-permute-done.5 = bf16[16,128,128]{2,1,0:T(8,128)(2,1)S(1)} collective-permute-done((bf16[16,128,128]{2,1,0:T(8,128)(2,1)S(1)}, bf16[16,128,128]{2,1,0:T(8,128)(2,1)S(1)}, u32[]{:S(2)}, u32[]{:S(2)}) %collective-permute-start.5) | collective-permute-done | bytes 524320 | tf_op jit(solution)/shard_map/ppermute | solution.py:174
  44.7 0.1 add_convert_fusion
  44.8 21.1 %all_to_all.10.parts_ref = bf16[32,64,128]{2,1,0:T(8,128)(2,1)S(1)} all-to-all(bf16[32,64,128]{2,1,0:T(8,128)(2,1)S(1)} %bitcast.12), channel_id=1, replica_groups=mesh['zh'=4,'zl'=2,'core'=2,'y'=4,'x'=4,'gz'=2] {'y','x','zl'}, dimensions={0} | all-to-all | bytes 1048576 | tf_op jit(solution)/shard_map/all_to_all | solution.py:237
  66.0 0.1 near_sum.1
  66.1 17.0 %all_to_all.11.planes_ref = bf16[16,64,128]{2,1,0:T(8,128)(2,1)S(1)} all-to-all(bf16[16,64,128]{2,1,0:T(8,128)(2,1)S(1)} %near_sum.1), channel_id=1, replica_groups=mesh['zh'=4,'zl'=2,'core'=2,'y'=4,'x'=4,'gz'=2] {'gz','zh','zl'}, dimensions={0} | all-to-all | bytes 524288 | tf_op jit(solution)/shard_map/all_to_all | solution.py:246
  83.0 0.2 fold.1
  83.2 8.7 %collective-permute-start.6 = (f32[128,128]{1,0:T(8,128)S(1)}, f32[128,128]{1,0:T(8,128)S(1)}, u32[]{:S(2)}, u32[]{:S(2)}) collective-permute-start(f32[128,128]{1,0:T(8,128)S(1)} %fold.1), channel_id=1, source_target_pairs={{0,32},{32,0},{1,33},{33,1},{2,34},{34,2},{3,35},{35,3},{4,36},{36... | collective-permute-start | bytes 196616 | tf_op jit(solution)/shard_map/ppermute | solution.py:174
  91.9 0.9 collective-permute-done.6
  92.8 0.7 pad_maximum_fusion
  (1 shorter events, 0.0 us)
Async XLA Ops:
  0.0 28.4 %copy-start.3 = (s32[4,6,16]{2,0,1:T(4,128)S(1)}, s32[4,6,16]{2,0,1:T(4,128)}, u32[]{:S(2)}) copy-start(s32[4,6,16]{2,0,1:T(4,128)} %param.5) | copy-start | bytes 4612
  0.0 37.5 %copy-start = (bf16[4,6,16,3,2048]{4,2,3,1,0:T(8,128)(2,1)S(1)}, bf16[4,6,16,3,2048]{4,2,3,1,0:T(8,128)(2,1)}, u32[]{:S(2)}) copy-start(bf16[4,6,16,3,2048]{4,2,3,1,0:T(8,128)(2,1)} %param.3) | copy-start | bytes 14155780
  2.6 34.8 %collective-permute-start.3 = (bf16[288,256]{1,0:T(8,128)(2,1)}, bf16[288,256]{1,0:T(8,128)(2,1)S(1)}, u32[]{:S(2)}, u32[]{:S(2)}) collective-permute-start(bf16[288,256]{1,0:T(8,128)(2,1)} %get-tuple-element.22), channel_id=1, source_target_pairs={{0,32},{32,64},{64,96},{96,128},{128,160},{160,192},{192,224},{224... | collective-permute-start | bytes 442376 | tf_op jit(solution)/shard_map/ppermute | solution.py:198
  7.5 29.9 %collective-permute-start.4 = (bf16[288,256]{1,0:T(8,128)(2,1)}, bf16[288,256]{1,0:T(8,128)(2,1)S(1)}, u32[]{:S(2)}, u32[]{:S(2)}) collective-permute-start(bf16[288,256]{1,0:T(8,128)(2,1)} %get-tuple-element.23), channel_id=1, source_target_pairs={{32,0},{64,32},{96,64},{128,96},{160,128},{192,160},{224,192},{256... | collective-permute-start | bytes 442376 | tf_op jit(solution)/shard_map/ppermute | solution.py:199
  12.7 24.7 %collective-permute-start.1 = (bf16[192,256]{1,0:T(8,128)(2,1)}, bf16[192,256]{1,0:T(8,128)(2,1)S(1)}, u32[]{:S(2)}, u32[]{:S(2)}) collective-permute-start(bf16[192,256]{1,0:T(8,128)(2,1)} %get-tuple-element.20), channel_id=1, source_target_pairs={{0,2},{2,4},{4,6},{6,8},{8,10},{10,12},{12,14},{14,16},{16,18},{18... | collective-permute-start | bytes 294920 | tf_op jit(solution)/shard_map/ppermute | solution.py:196
  14.0 23.4 %collective-permute-start.2 = (bf16[192,256]{1,0:T(8,128)(2,1)}, bf16[192,256]{1,0:T(8,128)(2,1)S(1)}, u32[]{:S(2)}, u32[]{:S(2)}) collective-permute-start(bf16[192,256]{1,0:T(8,128)(2,1)} %get-tuple-element.21), channel_id=1, source_target_pairs={{2,0},{4,2},{6,4},{8,6},{10,8},{12,10},{14,12},{16,14},{18,16},{20... | collective-permute-start | bytes 294920 | tf_op jit(solution)/shard_map/ppermute | solution.py:197
  15.3 24.9 %collective-permute-start = (bf16[72,256]{1,0:T(8,128)(2,1)}, bf16[72,256]{1,0:T(8,128)(2,1)S(1)}, u32[]{:S(2)}, u32[]{:S(2)}) collective-permute-start(bf16[72,256]{1,0:T(8,128)(2,1)} %get-tuple-element.19), channel_id=1, source_target_pairs={{0,1},{1,0},{2,3},{3,2},{4,5},{5,4},{6,7},{7,6},{8,9},{9,8},{10,11... | collective-permute-start | bytes 110600 | tf_op jit(solution)/shard_map/ppermute | solution.py:174
  28.4 1.3 %copy-start.1 = (f32[1152,256]{1,0:T(8,128)S(1)}, f32[1152,256]{1,0:T(8,128)}, u32[]{:S(2)}) copy-start(f32[1152,256]{1,0:T(8,128)} %get-tuple-element.24.panel_ref) | copy-start | bytes 3538948
  29.7 0.8 copy-start.2
  40.9 3.8 %collective-permute-start.5 = (bf16[16,128,128]{2,1,0:T(8,128)(2,1)S(1)}, bf16[16,128,128]{2,1,0:T(8,128)(2,1)S(1)}, u32[]{:S(2)}, u32[]{:S(2)}) collective-permute-start(bf16[16,128,128]{2,1,0:T(8,128)(2,1)S(1)} %get-tuple-element.32), channel_id=1, source_target_pairs={{0,32},{32,0},{1,33},{33,1},{2,34},{34,2},{3,35},{35,3},{4,36},{36... | collective-permute-start | bytes 1572872 | tf_op jit(solution)/shard_map/ppermute | solution.py:174
  83.2 9.6 %collective-permute-start.6 = (f32[128,128]{1,0:T(8,128)S(1)}, f32[128,128]{1,0:T(8,128)S(1)}, u32[]{:S(2)}, u32[]{:S(2)}) collective-permute-start(f32[128,128]{1,0:T(8,128)S(1)} %fold.1), channel_id=1, source_target_pairs={{0,32},{32,0},{1,33},{33,1},{2,34},{34,2},{3,35},{35,3},{4,36},{36... | collective-permute-start | bytes 196616 | tf_op jit(solution)/shard_map/ppermute | solution.py:174

commit v4 on v3

v4 whole, which is shorter than its diff:
```python
import jax
import jax.numpy as jnp
from jax import lax
from jax.experimental import pallas as pl
from jax.experimental.pallas import tpu as pltpu
from jax.sharding import Mesh, PartitionSpec as P

PANEL = 256
HALF = 128
NMAT = 8
SX, SY, SZ = 4, 6, 16
CELLS = SX * SY
GROUP = 3 * SZ
ROWS = CELLS * GROUP
EDGE = 3 * CELLS
ROW, COL, GZ = ("zh", "zl", "core"), ("y", "x"), "gz"
Z = ("gz", "zh", "zl")
f32, bf16 = jnp.float32, jnp.bfloat16


def lane(values, o, i, j, width=PANEL):
    k = (3 * i + j) * 7 + o
    return jnp.broadcast_to(values[:, k : k + 1], (values.shape[0], width))


def collect_kernel(modes_ref, panel_ref, z_ref, xlo_ref, xhi_ref, ylo_ref, yhi_ref, raw_ref, edge_ref, sem):
    copy = pltpu.make_async_copy(modes_ref.at[:, :PANEL], raw_ref, sem)
    copy.start()
    copy.wait()
    first = jnp.where(lax.axis_index(GZ) == 0, SZ - 1, 0)
    for h in range(2):
        part = slice(h * HALF, (h + 1) * HALF)
        panel_ref[h] = raw_ref[:, part].astype(f32)
        for j in range(3):
            rows = panel_ref.at[h][pl.ds(j * SZ + first, CELLS, stride=GROUP), :]
            edge_ref[j * CELLS : (j + 1) * CELLS, part] = rows
    z_ref[...] = edge_ref[...].astype(bf16)
    side = SY * GROUP
    xlo_ref[...] = raw_ref[:side, :]
    xhi_ref[...] = raw_ref[ROWS - side :, :]
    for x in range(SX):
        ylo_ref[x * GROUP : (x + 1) * GROUP, :] = raw_ref[x * side : x * side + GROUP, :]
        yhi_ref[x * GROUP : (x + 1) * GROUP, :] = raw_ref[(x + 1) * side - GROUP : (x + 1) * side, :]


def local_kernel(kind_ref, blocks_ref, panel_ref, modes_ref, coef_ref, part_ref, near_ref, inner_ref, table_ref, sem):
    copy = pltpu.make_async_copy(modes_ref, near_ref, sem)
    copy.start()
    table_ref[...] = jnp.zeros((NMAT, 128), f32)
    for i in range(3):
        for j in range(3):
            k = (3 * i + j) * 7
            table_ref[:, k : k + 7] = blocks_ref[i, j]
    table = table_ref[...]
    offset = lax.broadcasted_iota(jnp.int32, (SZ, 128), 1) % 7
    kinds = jnp.concatenate([kind_ref[y] for y in range(SY)]).astype(f32).T
    for n in range(CELLS):
        x, y = divmod(n, SY)
        kind = jnp.broadcast_to(kinds[:, y * SX + x : y * SX + x + 1], (SZ, 128))
        coef = jnp.zeros((SZ, 128), f32)
        for m in range(NMAT):
            coef = jnp.where(kind == m, jnp.broadcast_to(table[m : m + 1, :], (SZ, 128)), coef)
        coef_ref[n] = coef
        outside = [o for o, at in ((1, x == SX - 1), (2, x == 0), (3, y == SY - 1), (4, y == 0)) if at]
        for o in outside:
            coef = jnp.where(offset == o, 0.0, coef)
        inner_ref[n] = coef
    level = lax.broadcasted_iota(jnp.int32, (SZ, PANEL), 0)

    def cell(n, carry):
        coef = inner_ref[n]
        total = [jnp.zeros((SZ, PANEL), f32) for _ in range(3)]
        last = CELLS - 1
        sources = (
            (1, jnp.minimum(n + SY, last)),
            (2, jnp.maximum(n - SY, 0)),
            (3, jnp.minimum(n + 1, last)),
            (4, jnp.maximum(n - 1, 0)),
        )

        def rows(at, j):
            start = pl.multiple_of(at * GROUP + j * SZ, SZ)
            return jnp.concatenate([panel_ref[h, pl.ds(start, SZ), :] for h in range(2)], axis=1)

        for j in range(3):
            own = rows(n, j)
            above = jnp.where(level == SZ - 1, 0.0, pltpu.roll(own, SZ - 1, 0))
            below = jnp.where(level == 0, 0.0, pltpu.roll(own, 1, 0))
            terms = [(0, own), (5, above), (6, below)] + [(o, rows(at, j)) for o, at in sources]
            for o, value in terms:
                for i in range(3):
                    total[i] = total[i] + lane(coef, o, i, j) * value
        for i in range(3):
            part_ref[pl.ds(pl.multiple_of(n * GROUP + i * SZ, SZ), SZ), :] = total[i]
        return carry

    lax.fori_loop(0, CELLS, cell, 0)
    copy.wait()


def edge_kernel(zface_ref, coef_ref, term_ref):
    gz = lax.axis_index(GZ)
    coef = coef_ref[pl.ds(jnp.where(gz == 0, SZ - 1, 0), CELLS, stride=SZ), :]
    coef = jnp.where(gz == 0, coef, pltpu.roll(coef, 127, 1))
    for i in range(3):
        total = jnp.zeros((CELLS, PANEL), f32)
        for j in range(3):
            total = total + lane(coef, 5, i, j) * zface_ref[j * CELLS : (j + 1) * CELLS, :].astype(f32)
        term_ref[i * CELLS : (i + 1) * CELLS, :] = total


def product_kernel(ylo_ref, yhi_ref, xlo_ref, xhi_ref, coef_ref, part_ref, term_ref, modes_ref,
                   keep_ref, send_ref, stiff_ref, left_ref):
    core, gz = lax.axis_index("core"), lax.axis_index(GZ)
    level = lax.broadcasted_iota(jnp.int32, (SZ, PANEL), 0)
    at_edge = level == jnp.where(gz == 0, SZ - 1, 0)
    for n in range(CELLS):
        x, y = divmod(n, SY)
        coef = coef_ref[n * SZ : (n + 1) * SZ, :]
        faces = [(1, xhi_ref, y)] if x == SX - 1 else []
        faces += [(2, xlo_ref, y)] if x == 0 else []
        faces += [(3, yhi_ref, x)] if y == SY - 1 else []
        faces += [(4, ylo_ref, x)] if y == 0 else []
        for i in range(3):
            start = n * GROUP + i * SZ
            row = i * CELLS + n
            term = jnp.broadcast_to(term_ref[row : row + 1, :], (SZ, PANEL))
            total = part_ref[start : start + SZ, :] + jnp.where(at_edge, term, 0.0)
            for o, ref, k in faces:
                for j in range(3):
                    value = ref[k * GROUP + j * SZ : k * GROUP + (j + 1) * SZ, :].astype(f32)
                    total = total + lane(coef, o, i, j) * value
            stiff_ref[start : start + SZ, :] = total.astype(bf16)
    left_ref[...] = stiff_ref[...].T
    for t in range(modes_ref.shape[1] // PANEL):
        part = slice(t * PANEL, (t + 1) * PANEL)
        product = jnp.dot(left_ref[...], modes_ref[:, part], preferred_element_type=f32)
        low, high = product[:HALF], product[HALF:]
        keep = jnp.where(core == 0, low, high)
        send = jnp.where(core == 0, high, low).astype(bf16)
        for u in range(2):
            keep_ref[2 * t + u] = keep[:, u * HALF : (u + 1) * HALF]
            send_ref[2 * t + u] = send[:, u * HALF : (u + 1) * HALF]


def near_kernel(parts_ref, copies_ref):
    total = parts_ref[0].astype(f32)
    for k in range(1, parts_ref.shape[0]):
        total = total + parts_ref[k].astype(f32)
    total = total.astype(bf16)
    for k in range(copies_ref.shape[0]):
        copies_ref[k] = total


def fold_kernel(planes_ref, half_ref):
    for r in range(2):
        total = planes_ref[r].astype(f32)
        for q in range(1, 8):
            total = total + planes_ref[2 * q + r].astype(f32)
        half_ref[:, 64 * r : 64 * (r + 1)] = total.T


def swap(value, axis):
    return lax.ppermute(value, axis, [(0, 1), (1, 0)])


def shards(modes, blocks, material):
    full = modes.shape[-1]
    flat = modes.transpose(0, 1, 3, 2, 4).reshape(ROWS, full)
    chain = [(i, i + 1) for i in range(15)]
    back = [(j, i) for i, j in chain]
    vmem = pl.BlockSpec(memory_space=pltpu.VMEM)
    shape = jax.ShapeDtypeStruct
    xside, yside = SY * GROUP, SX * GROUP
    panel, zsend, xfirst, xlast, yfirst, ylast = pl.pallas_call(
        collect_kernel,
        in_specs=[pl.BlockSpec(memory_space=pl.ANY)],
        out_specs=[vmem] * 6,
        out_shape=[shape((2, ROWS, HALF), f32)]
        + [shape((rows, PANEL), bf16) for rows in (3 * CELLS, xside, xside, yside, yside)],
        scratch_shapes=[pltpu.VMEM((ROWS, PANEL), bf16), pltpu.VMEM((EDGE, PANEL), f32), pltpu.SemaphoreType.DMA],
        compiler_params=pltpu.CompilerParams(vmem_limit_bytes=50 << 20),
        name="collect_faces",
    )(flat)
    zface = swap(zsend, GZ)
    ylo = lax.ppermute(ylast, COL, chain)
    yhi = lax.ppermute(yfirst, COL, back)
    xlo = lax.ppermute(xlast, ROW, chain)
    xhi = lax.ppermute(xfirst, ROW, back)
    coef, part, near = pl.pallas_call(
        local_kernel,
        in_specs=[vmem] * 3 + [pl.BlockSpec(memory_space=pl.ANY)],
        out_specs=[vmem] * 3,
        out_shape=[shape((CELLS, SZ, 128), f32), shape((ROWS, PANEL), f32), shape((ROWS, full), bf16)],
        scratch_shapes=[pltpu.VMEM((CELLS, SZ, 128), f32), pltpu.VMEM((NMAT, 128), f32), pltpu.SemaphoreType.DMA],
        cost_estimate=pl.CostEstimate(flops=2 * ROWS * 21 * PANEL, bytes_accessed=3 * ROWS * PANEL, transcendentals=0),
        compiler_params=pltpu.CompilerParams(vmem_limit_bytes=46 << 20),
        name="local_stencil",
    )(material.transpose(1, 0, 2), blocks.transpose(2, 3, 0, 1), panel, flat)
    tiles = full // HALF
    coef = coef.reshape(CELLS * SZ, 128)
    term = pl.pallas_call(
        edge_kernel,
        in_specs=[vmem] * 2,
        out_specs=vmem,
        out_shape=shape((EDGE, PANEL), f32),
        cost_estimate=pl.CostEstimate(flops=4 * 10**9, bytes_accessed=EDGE * PANEL * 6, transcendentals=0),
        compiler_params=pltpu.CompilerParams(vmem_limit_bytes=8 << 20),
        name="edge_terms",
    )(zface, coef)
    keep, send = pl.pallas_call(
        product_kernel,
        in_specs=[vmem] * 8,
        out_specs=[vmem] * 2,
        out_shape=[shape((tiles, HALF, HALF), dtype) for dtype in (f32, bf16)],
        scratch_shapes=[pltpu.VMEM((ROWS, PANEL), bf16), pltpu.VMEM((PANEL, ROWS), bf16)],
        cost_estimate=pl.CostEstimate(flops=2 * ROWS * full * PANEL, bytes_accessed=2 * ROWS * full, transcendentals=0),
        compiler_params=pltpu.CompilerParams(vmem_limit_bytes=32 << 20),
        name="faces_and_product",
    )(ylo, yhi, xlo, xhi, coef, part, term, near)
    mine = (keep + swap(send, "core").astype(f32)).astype(bf16)
    parts = lax.all_to_all(mine.reshape(2 * tiles, HALF // 2, HALF), COL + ("zl",), 0, 0, tiled=True)
    copies = pl.pallas_call(
        near_kernel,
        in_specs=[vmem],
        out_specs=vmem,
        out_shape=shape((16, HALF // 2, HALF), bf16),
        compiler_params=pltpu.CompilerParams(vmem_limit_bytes=4 << 20),
        name="near_sum",
    )(parts)
    planes = lax.all_to_all(copies, Z, 0, 0, tiled=True)
    half = pl.pallas_call(
        fold_kernel,
        in_specs=[vmem],
        out_specs=vmem,
        out_shape=shape((HALF, HALF), f32),
        compiler_params=pltpu.CompilerParams(vmem_limit_bytes=4 << 20),
        name="fold",
    )(planes)
    other = swap(half, "core")
    first = lax.axis_index("core") == 0
    return jnp.concatenate([jnp.where(first, half, other), jnp.where(first, other, half)], axis=1)


def solution(mesh):
    split = Mesh(mesh.devices.reshape(4, 2, 2, 4, 4, 2), ("zh", "zl", "core", "y", "x", "gz"))
    return jax.shard_map(
        shards,
        mesh=split,
        in_specs=(P(ROW, COL, GZ, None, None), P(), P(ROW, COL, GZ)),
        out_specs=P(COL, None),
        check_vma=False,
    )
```

time: 93.9 us -> 89.6 us (0.954)
  Pallas kernels: 13.2 us -> 11 us
  local copies, waits for them, and re-layouts: 2.04 us -> 0.01 us
    ppermute x1, starting transfers between devices: 5.15 us -> 1.92 us  [shards(): xhi = lax.ppermute(xfirst, ROW, back)]
    ppermute x3, starting transfers between devices: 23.7 us -> 26.9 us  [swap(): return lax.ppermute(value, axis, [(0, 1), (1, 0)])]
    unnamed x8 -> x4, local copies, waits for them, and re-layouts: 2.04 us -> 0.01 us
    ppermute x1, starting transfers between devices: 1.29 us -> 3.12 us  [shards(): ylo = lax.ppermute(ylast, COL, chain)]
    ppermute x1, starting transfers between devices: 4.94 us -> 3.49 us  [shards(): xlo = lax.ppermute(xlast, ROW, chain)]
    pallas_call x1, Pallas kernels: 2.58 us -> 1.24 us  [shards(): pl.pallas_call(collect_kernel, in_specs=[pl.BlockSpec(memory_space=pl.ANY...]
  transfers between devices with their start and end apart: 7 -> 7, of which waited for: 2 -> 2; matrix products, arithmetic and copies ran while one was open for 0% -> 0% of each run, Pallas kernels for 10% -> 8%
where the time goes in v4:
time: 89.6 us; the launch traced here: 89.3 us
  blocking collectives  37.8 us (42%)
  starting transfers between devices  36.7 us (41%)
  Pallas kernels  11 us (12%)
  waiting for transfers between devices  2.76 us (3%)
    ppermute x3, starting transfers between devices, swap(): return lax.ppermute(value, axis, [(0, 1), (1, 0)])  26.9 us
    all_to_all x1, blocking collectives, shards(): lax.all_to_all(mine.reshape(2 * tiles, HALF // 2, HALF), COL + ('zl',), 0...  20.8 us
    all_to_all x1, blocking collectives, shards(): planes = lax.all_to_all(copies, Z, 0, 0, tiled=True)  17 us
    pallas_call x1, Pallas kernels, shards(): pl.pallas_call(local_kernel, in_specs=[vmem] * 3 + [pl.BlockSpec(memory_s...  6.95 us
    ppermute x1, starting transfers between devices, shards(): xlo = lax.ppermute(xlast, ROW, chain)  3.49 us
    ppermute x1, starting transfers between devices, shards(): ylo = lax.ppermute(ylast, COL, chain)  3.12 us
    ppermute x3, waiting for transfers between devices, swap(): return lax.ppermute(value, axis, [(0, 1), (1, 0)])  2.75 us
    pallas_call x1, Pallas kernels, shards(): pl.pallas_call(product_kernel, in_specs=[vmem] * 8, out_specs=[vmem] * 2,...  2.4 us
  transfers between devices with their start and end apart: 7, of which 2 were waited for; matrix products, arithmetic and copies ran while one was open for 0% of the time, Pallas kernels for 8%

profile of v4, /device:TPU:1, one launch (start us, length us, event | category | flops | bytes accessed | tf_op | source)
XLA Modules:
  0.0 89.3 jit_solution(8205532530660560944)
XLA Ops:
  0.0 0.0 copy-start.1
  0.0 0.0 copy-start
  0.0 1.2 %collect_faces.1 = (f32[2,1152,128]{2,1,0:T(8,128)S(1)}, bf16[72,256]{1,0:T(8,128)(2,1)S(1)}, bf16[288,256]{1,0:T(8,128)(2,1)S(1)}, bf16[288,256]{1,0:T(8,128)(2...) custom-call(bf16[1152,2048]{1,0:T(8,128)(2,1)} %bitcast.11), custom_call_target="tpu_custom_call" | custom-call | tf_op jit(solution)/shard_map/collect_faces/pallas_call | solution.py:175
  1.3 16.3 %collective-permute-start.4 = (bf16[72,256]{1,0:T(8,128)(2,1)S(1)}, bf16[72,256]{1,0:T(8,128)(2,1)S(1)}, u32[]{:S(2)}, u32[]{:S(2)}) collective-permute-start(bf16[72,256]{1,0:T(8,128)(2,1)S(1)} %get-tuple-element.23), channel_id=1, source_target_pairs={{0,1},{1,0},{2,3},{3,2},{4,5},{5,4},{6,7},{7,6},{8,9},{9,8},{10,11... | collective-permute-start | bytes 110600 | tf_op jit(solution)/shard_map/ppermute | solution.py:164
  17.5 3.5 %collective-permute-start.2 = (bf16[288,256]{1,0:T(8,128)(2,1)S(1)}, bf16[288,256]{1,0:T(8,128)(2,1)S(1)}, u32[]{:S(2)}, u32[]{:S(2)}) collective-permute-start(bf16[288,256]{1,0:T(8,128)(2,1)S(1)} %get-tuple-element.18), channel_id=1, source_target_pairs={{0,32},{32,64},{64,96},{96,128},{128,160},{160,192},{192,224},{224... | collective-permute-start | bytes 442376 | tf_op jit(solution)/shard_map/ppermute | solution.py:188
  21.0 1.9 %collective-permute-start.3 = (bf16[288,256]{1,0:T(8,128)(2,1)S(1)}, bf16[288,256]{1,0:T(8,128)(2,1)S(1)}, u32[]{:S(2)}, u32[]{:S(2)}) collective-permute-start(bf16[288,256]{1,0:T(8,128)(2,1)S(1)} %get-tuple-element.19), channel_id=1, source_target_pairs={{32,0},{64,32},{96,64},{128,96},{160,128},{192,160},{224,192},{256... | collective-permute-start | bytes 442376 | tf_op jit(solution)/shard_map/ppermute | solution.py:189
  22.9 3.1 %collective-permute-start = (bf16[192,256]{1,0:T(8,128)(2,1)S(1)}, bf16[192,256]{1,0:T(8,128)(2,1)S(1)}, u32[]{:S(2)}, u32[]{:S(2)}) collective-permute-start(bf16[192,256]{1,0:T(8,128)(2,1)S(1)} %get-tuple-element.16), channel_id=1, source_target_pairs={{0,2},{2,4},{4,6},{6,8},{8,10},{10,12},{12,14},{14,16},{16,18},{18... | collective-permute-start | bytes 294920 | tf_op jit(solution)/shard_map/ppermute | solution.py:186
  26.1 1.3 %collective-permute-start.1 = (bf16[192,256]{1,0:T(8,128)(2,1)S(1)}, bf16[192,256]{1,0:T(8,128)(2,1)S(1)}, u32[]{:S(2)}, u32[]{:S(2)}) collective-permute-start(bf16[192,256]{1,0:T(8,128)(2,1)S(1)} %get-tuple-element.17), channel_id=1, source_target_pairs={{2,0},{4,2},{6,4},{8,6},{10,8},{12,10},{14,12},{16,14},{18,16},{20... | collective-permute-start | bytes 294920 | tf_op jit(solution)/shard_map/ppermute | solution.py:187
  27.4 0.0 copy-done.1
  27.4 0.0 copy-done
  27.4 7.0 %local_stencil.1 = (f32[24,16,128]{2,1,0:T(8,128)S(1)}, f32[1152,256]{1,0:T(8,128)S(1)}, bf16[1152,2048]{1,0:T(8,128)(2,1)S(1)}) custom-call(s32[6,4,16]{2,1,0:T(4,128)S(1)} %bitcast.10, f32[3,3,8,7]{3,2,1,0:T(8,128)S(1)} %bitcast.9, f32[2,1152,128]{2,1,0:T(8,128)S(1)} %get-tuple-element.20.panel_ref, bf16[1152,2048]{1,0:T(8,128)(2,1)} %bitcast.12), custom_call_target="tpu_custom_call" | custom-call | flops 12386304 | bytes 884736 | tf_op jit(solution)/shard_map/local_stencil/pallas_call | solution.py:190
  34.4 0.0 collective-permute-done.4.zface_ref
  34.4 0.2 edge_terms.1.term_ref
  34.6 0.0 collective-permute-done.ylo_ref
  34.6 0.0 collective-permute-done.1.yhi_ref
  34.6 0.0 collective-permute-done.2.xlo_ref
  34.6 0.0 collective-permute-done.3.xhi_ref
  34.6 2.4 %faces_and_product.1 = (f32[16,128,128]{2,1,0:T(8,128)S(1)}, bf16[16,128,128]{2,1,0:T(8,128)(2,1)S(1)}) custom-call(bf16[192,256]{1,0:T(8,128)(2,1)S(1)} %collective-permute-done.ylo_ref, bf16[192,256]{1,0:T(8,128)(2,1)S(1)} %collective-permute-done.1.yhi_ref, bf16[288,256]{1,0:T(8,128)(2,1)S(1)} %collective-permute-done.2.xlo_ref, ...), custom_call_target="tpu_custom_call" | custom-call | flops 1207959552 | bytes 4718592 | tf_op jit(solution)/shard_map/faces_and_product/pallas_call | solution.py:211
  37.0 1.9 %collective-permute-start.5 = (bf16[16,128,128]{2,1,0:T(8,128)(2,1)S(1)}, bf16[16,128,128]{2,1,0:T(8,128)(2,1)S(1)}, u32[]{:S(2)}, u32[]{:S(2)}) collective-permute-start(bf16[16,128,128]{2,1,0:T(8,128)(2,1)S(1)} %get-tuple-element.26), channel_id=1, source_target_pairs={{0,32},{32,0},{1,33},{33,1},{2,34},{34,2},{3,35},{35,3},{4,36},{36... | collective-permute-start | bytes 1572872 | tf_op jit(solution)/shard_map/ppermute | solution.py:164
  38.9 1.9 %collective-permute-done.5 = bf16[16,128,128]{2,1,0:T(8,128)(2,1)S(1)} collective-permute-done((bf16[16,128,128]{2,1,0:T(8,128)(2,1)S(1)}, bf16[16,128,128]{2,1,0:T(8,128)(2,1)S(1)}, u32[]{:S(2)}, u32[]{:S(2)}) %collective-permute-start.5) | collective-permute-done | bytes 524320 | tf_op jit(solution)/shard_map/ppermute | solution.py:164
  40.8 0.1 add_convert_fusion
  40.9 20.8 %all_to_all.10.parts_ref = bf16[32,64,128]{2,1,0:T(8,128)(2,1)S(1)} all-to-all(bf16[32,64,128]{2,1,0:T(8,128)(2,1)S(1)} %bitcast.13), channel_id=1, replica_groups=mesh['zh'=4,'zl'=2,'core'=2,'y'=4,'x'=4,'gz'=2] {'y','x','zl'}, dimensions={0} | all-to-all | bytes 1048576 | tf_op jit(solution)/shard_map/all_to_all | solution.py:222
  61.8 0.1 near_sum.1
  61.9 17.0 %all_to_all.11.planes_ref = bf16[16,64,128]{2,1,0:T(8,128)(2,1)S(1)} all-to-all(bf16[16,64,128]{2,1,0:T(8,128)(2,1)S(1)} %near_sum.1), channel_id=1, replica_groups=mesh['zh'=4,'zl'=2,'core'=2,'y'=4,'x'=4,'gz'=2] {'gz','zh','zl'}, dimensions={0} | all-to-all | bytes 524288 | tf_op jit(solution)/shard_map/all_to_all | solution.py:231
  78.9 0.2 fold.1
  79.0 8.7 %collective-permute-start.6 = (f32[128,128]{1,0:T(8,128)S(1)}, f32[128,128]{1,0:T(8,128)S(1)}, u32[]{:S(2)}, u32[]{:S(2)}) collective-permute-start(f32[128,128]{1,0:T(8,128)S(1)} %fold.1), channel_id=1, source_target_pairs={{0,32},{32,0},{1,33},{33,1},{2,34},{34,2},{3,35},{35,3},{4,36},{36... | collective-permute-start | bytes 196616 | tf_op jit(solution)/shard_map/ppermute | solution.py:164
  87.7 0.9 collective-permute-done.6
  88.6 0.7 pad_maximum_fusion
  (1 shorter events, 0.0 us)
Async XLA Ops:
  0.0 27.4 %copy-start.1 = (s32[4,6,16]{2,0,1:T(4,128)S(1)}, s32[4,6,16]{2,0,1:T(4,128)}, u32[]{:S(2)}) copy-start(s32[4,6,16]{2,0,1:T(4,128)} %param.5) | copy-start | bytes 4612
  0.0 27.4 %copy-start = (f32[8,7,3,3]{1,0,3,2:T(8,128)S(1)}, f32[8,7,3,3]{1,0,3,2:T(8,128)}, u32[]{:S(2)}) copy-start(f32[8,7,3,3]{1,0,3,2:T(8,128)} %param.4) | copy-start | bytes 6052
  1.3 33.1 %collective-permute-start.4 = (bf16[72,256]{1,0:T(8,128)(2,1)S(1)}, bf16[72,256]{1,0:T(8,128)(2,1)S(1)}, u32[]{:S(2)}, u32[]{:S(2)}) collective-permute-start(bf16[72,256]{1,0:T(8,128)(2,1)S(1)} %get-tuple-element.23), channel_id=1, source_target_pairs={{0,1},{1,0},{2,3},{3,2},{4,5},{5,4},{6,7},{7,6},{8,9},{9,8},{10,11... | collective-permute-start | bytes 110600 | tf_op jit(solution)/shard_map/ppermute | solution.py:164
  17.5 17.1 %collective-permute-start.2 = (bf16[288,256]{1,0:T(8,128)(2,1)S(1)}, bf16[288,256]{1,0:T(8,128)(2,1)S(1)}, u32[]{:S(2)}, u32[]{:S(2)}) collective-permute-start(bf16[288,256]{1,0:T(8,128)(2,1)S(1)} %get-tuple-element.18), channel_id=1, source_target_pairs={{0,32},{32,64},{64,96},{96,128},{128,160},{160,192},{192,224},{224... | collective-permute-start | bytes 442376 | tf_op jit(solution)/shard_map/ppermute | solution.py:188
  21.0 13.6 %collective-permute-start.3 = (bf16[288,256]{1,0:T(8,128)(2,1)S(1)}, bf16[288,256]{1,0:T(8,128)(2,1)S(1)}, u32[]{:S(2)}, u32[]{:S(2)}) collective-permute-start(bf16[288,256]{1,0:T(8,128)(2,1)S(1)} %get-tuple-element.19), channel_id=1, source_target_pairs={{32,0},{64,32},{96,64},{128,96},{160,128},{192,160},{224,192},{256... | collective-permute-start | bytes 442376 | tf_op jit(solution)/shard_map/ppermute | solution.py:189
  22.9 11.6 %collective-permute-start = (bf16[192,256]{1,0:T(8,128)(2,1)S(1)}, bf16[192,256]{1,0:T(8,128)(2,1)S(1)}, u32[]{:S(2)}, u32[]{:S(2)}) collective-permute-start(bf16[192,256]{1,0:T(8,128)(2,1)S(1)} %get-tuple-element.16), channel_id=1, source_target_pairs={{0,2},{2,4},{4,6},{6,8},{8,10},{10,12},{12,14},{14,16},{16,18},{18... | collective-permute-start | bytes 294920 | tf_op jit(solution)/shard_map/ppermute | solution.py:186
  26.1 8.5 %collective-permute-start.1 = (bf16[192,256]{1,0:T(8,128)(2,1)S(1)}, bf16[192,256]{1,0:T(8,128)(2,1)S(1)}, u32[]{:S(2)}, u32[]{:S(2)}) collective-permute-start(bf16[192,256]{1,0:T(8,128)(2,1)S(1)} %get-tuple-element.17), channel_id=1, source_target_pairs={{2,0},{4,2},{6,4},{8,6},{10,8},{12,10},{14,12},{16,14},{18,16},{20... | collective-permute-start | bytes 294920 | tf_op jit(solution)/shard_map/ppermute | solution.py:187
  37.0 3.8 %collective-permute-start.5 = (bf16[16,128,128]{2,1,0:T(8,128)(2,1)S(1)}, bf16[16,128,128]{2,1,0:T(8,128)(2,1)S(1)}, u32[]{:S(2)}, u32[]{:S(2)}) collective-permute-start(bf16[16,128,128]{2,1,0:T(8,128)(2,1)S(1)} %get-tuple-element.26), channel_id=1, source_target_pairs={{0,32},{32,0},{1,33},{33,1},{2,34},{34,2},{3,35},{35,3},{4,36},{36... | collective-permute-start | bytes 1572872 | tf_op jit(solution)/shard_map/ppermute | solution.py:164
  79.0 9.6 %collective-permute-start.6 = (f32[128,128]{1,0:T(8,128)S(1)}, f32[128,128]{1,0:T(8,128)S(1)}, u32[]{:S(2)}, u32[]{:S(2)}) collective-permute-start(f32[128,128]{1,0:T(8,128)S(1)} %fold.1), channel_id=1, source_target_pairs={{0,32},{32,0},{1,33},{33,1},{2,34},{34,2},{3,35},{35,3},{4,36},{36... | collective-permute-start | bytes 196616 | tf_op jit(solution)/shard_map/ppermute | solution.py:164

commit v5 on v4

--- a/solution.py
+++ b/solution.py
@@ -23,7 +23,7 @@
     return jnp.broadcast_to(values[:, k : k + 1], (values.shape[0], width))
 
 
-def collect_kernel(modes_ref, panel_ref, z_ref, xlo_ref, xhi_ref, ylo_ref, yhi_ref, raw_ref, edge_ref, sem):
+def collect_kernel(modes_ref, panel_ref, z_ref, xin_ref, xout_ref, ylo_ref, yhi_ref, raw_ref, edge_ref, sem):
     copy = pltpu.make_async_copy(modes_ref.at[:, :PANEL], raw_ref, sem)
     copy.start()
     copy.wait()
@@ -36,40 +36,52 @@
             edge_ref[j * CELLS : (j + 1) * CELLS, part] = rows
     z_ref[...] = edge_ref[...].astype(bf16)
     side = SY * GROUP
-    xlo_ref[...] = raw_ref[:side, :]
-    xhi_ref[...] = raw_ref[ROWS - side :, :]
+    low = lax.axis_index("core") == 0
+    xin_ref[...] = jnp.where(low, raw_ref[ROWS - side :, :], raw_ref[:side, :])
+    xout_ref[...] = jnp.where(low, raw_ref[:side, :], raw_ref[ROWS - side :, :])
     for x in range(SX):
         ylo_ref[x * GROUP : (x + 1) * GROUP, :] = raw_ref[x * side : x * side + GROUP, :]
         yhi_ref[x * GROUP : (x + 1) * GROUP, :] = raw_ref[(x + 1) * side - GROUP : (x + 1) * side, :]
 
 
-def local_kernel(kind_ref, blocks_ref, panel_ref, modes_ref, coef_ref, part_ref, near_ref, inner_ref, table_ref, sem):
+def split3(value):
+    high = value.astype(bf16).astype(f32)
+    mid = (value - high).astype(bf16).astype(f32)
+    low = value - high - mid
+    return jnp.concatenate([high, mid, low, jnp.zeros_like(value)]).astype(bf16)
+
+
+def local_kernel(kind_ref, blocks_ref, panel_ref, modes_ref,
+                 coef_ref, part_ref, near_ref, table_ref, wide_ref, hot_ref, plane_ref, sem):
     copy = pltpu.make_async_copy(modes_ref, near_ref, sem)
     copy.start()
     table_ref[...] = jnp.zeros((NMAT, 128), f32)
     for i in range(3):
         for j in range(3):
-            k = (3 * i + j) * 7
-            table_ref[:, k : k + 7] = blocks_ref[i, j]
-    table = table_ref[...]
-    offset = lax.broadcasted_iota(jnp.int32, (SZ, 128), 1) % 7
+            k = 3 * i + j
+            values = blocks_ref[i, j]
+            table_ref[:, 7 * k : 7 * k + 7] = values
+            for o in range(7):
+                column = jnp.broadcast_to(values[:, o : o + 1], (NMAT, HALF))
+                wide_ref[o, :, k * HALF : (k + 1) * HALF] = split3(column)
     kinds = jnp.concatenate([kind_ref[y] for y in range(SY)]).astype(f32).T
+    slot = lax.broadcasted_iota(jnp.int32, (SZ, 4 * NMAT), 1)
+    slot = jnp.where(slot < 3 * NMAT, slot % NMAT, -1).astype(f32)
+    none = jnp.zeros((SZ, 4 * NMAT), bf16)
     for n in range(CELLS):
         x, y = divmod(n, SY)
-        kind = jnp.broadcast_to(kinds[:, y * SX + x : y * SX + x + 1], (SZ, 128))
-        coef = jnp.zeros((SZ, 128), f32)
-        for m in range(NMAT):
-            coef = jnp.where(kind == m, jnp.broadcast_to(table[m : m + 1, :], (SZ, 128)), coef)
-        coef_ref[n] = coef
-        outside = [o for o, at in ((1, x == SX - 1), (2, x == 0), (3, y == SY - 1), (4, y == 0)) if at]
-        for o in outside:
-            coef = jnp.where(offset == o, 0.0, coef)
-        inner_ref[n] = coef
-    level = lax.broadcasted_iota(jnp.int32, (SZ, PANEL), 0)
+        kind = jnp.broadcast_to(kinds[:, y * SX + x : y * SX + x + 1], (SZ, 4 * NMAT))
+        hot = jnp.where(kind == slot, 1.0, 0.0).astype(bf16)
+        outside = (False, x == SX - 1, x == 0, y == SY - 1, y == 0)
+        for o in range(5):
+            hot_ref[o, n * SZ : (n + 1) * SZ, :] = none if outside[o] else hot
+    coef_ref[...] = jnp.dot(hot_ref[0], split3(table_ref[...]), preferred_element_type=f32)
+    for o in range(7):
+        plane_ref[o] = jnp.dot(hot_ref[o if o < 5 else 0], wide_ref[o], preferred_element_type=f32)
+    level = lax.broadcasted_iota(jnp.int32, (SZ, HALF), 0)
+    top, bottom = level == SZ - 1, level == 0
 
     def cell(n, carry):
-        coef = inner_ref[n]
-        total = [jnp.zeros((SZ, PANEL), f32) for _ in range(3)]
         last = CELLS - 1
         sources = (
             (1, jnp.minimum(n + SY, last)),
@@ -77,24 +89,31 @@
             (3, jnp.minimum(n + 1, last)),
             (4, jnp.maximum(n - 1, 0)),
         )
+        here = pl.ds(pl.multiple_of(n * SZ, SZ), SZ)
+        total = [[jnp.zeros((SZ, HALF), f32) for _ in range(2)] for _ in range(3)]
 
         def rows(at, j):
             start = pl.multiple_of(at * GROUP + j * SZ, SZ)
-            return jnp.concatenate([panel_ref[h, pl.ds(start, SZ), :] for h in range(2)], axis=1)
+            return [panel_ref[h, pl.ds(start, SZ), :] for h in range(2)]
 
         for j in range(3):
             own = rows(n, j)
-            above = jnp.where(level == SZ - 1, 0.0, pltpu.roll(own, SZ - 1, 0))
-            below = jnp.where(level == 0, 0.0, pltpu.roll(own, 1, 0))
+            above = [jnp.where(top, 0.0, pltpu.roll(v, SZ - 1, 0)) for v in own]
+            below = [jnp.where(bottom, 0.0, pltpu.roll(v, 1, 0)) for v in own]
             terms = [(0, own), (5, above), (6, below)] + [(o, rows(at, j)) for o, at in sources]
-            for o, value in terms:
+            for o, values in terms:
                 for i in range(3):
-                    total[i] = total[i] + lane(coef, o, i, j) * value
+                    k = 3 * i + j
+                    factor = plane_ref[o, here, k * HALF : (k + 1) * HALF]
+                    for h in range(2):
+                        total[i][h] = total[i][h] + factor * values[h]
         for i in range(3):
-            part_ref[pl.ds(pl.multiple_of(n * GROUP + i * SZ, SZ), SZ), :] = total[i]
+            start = pl.multiple_of(n * GROUP + i * SZ, SZ)
+            for h in range(2):
+                part_ref[pl.ds(start, SZ), h * HALF : (h + 1) * HALF] = total[i][h]
         return carry
 
-    lax.fori_loop(0, CELLS, cell, 0)
+    lax.fori_loop(0, CELLS, cell, 0, unroll=2)
     copy.wait()
 
 
@@ -109,26 +128,30 @@
         term_ref[i * CELLS : (i + 1) * CELLS, :] = total
 
 
-def product_kernel(ylo_ref, yhi_ref, xlo_ref, xhi_ref, coef_ref, part_ref, term_ref, modes_ref,
+def product_kernel(ylo_ref, yhi_ref, chip_ref, beside_ref, coef_ref, part_ref, term_ref, modes_ref,
                    keep_ref, send_ref, stiff_ref, left_ref):
     core, gz = lax.axis_index("core"), lax.axis_index(GZ)
     level = lax.broadcasted_iota(jnp.int32, (SZ, PANEL), 0)
     at_edge = level == jnp.where(gz == 0, SZ - 1, 0)
+    low = core == 0
     for n in range(CELLS):
         x, y = divmod(n, SY)
         coef = coef_ref[n * SZ : (n + 1) * SZ, :]
-        faces = [(1, xhi_ref, y)] if x == SX - 1 else []
-        faces += [(2, xlo_ref, y)] if x == 0 else []
-        faces += [(3, yhi_ref, x)] if y == SY - 1 else []
-        faces += [(4, ylo_ref, x)] if y == 0 else []
+        faces = [(1, (chip_ref, beside_ref), y)] if x == SX - 1 else []
+        faces += [(2, (beside_ref, chip_ref), y)] if x == 0 else []
+        faces += [(3, (yhi_ref,), x)] if y == SY - 1 else []
+        faces += [(4, (ylo_ref,), x)] if y == 0 else []
         for i in range(3):
             start = n * GROUP + i * SZ
             row = i * CELLS + n
             term = jnp.broadcast_to(term_ref[row : row + 1, :], (SZ, PANEL))
             total = part_ref[start : start + SZ, :] + jnp.where(at_edge, term, 0.0)
-            for o, ref, k in faces:
+            for o, refs, k in faces:
                 for j in range(3):
-                    value = ref[k * GROUP + j * SZ : k * GROUP + (j + 1) * SZ, :].astype(f32)
+                    at = slice(k * GROUP + j * SZ, k * GROUP + (j + 1) * SZ)
+                    value = refs[0][at, :].astype(f32)
+                    if len(refs) == 2:
+                        value = jnp.where(low, value, refs[1][at, :].astype(f32))
                     total = total + lane(coef, o, i, j) * value
             stiff_ref[start : start + SZ, :] = total.astype(bf16)
     left_ref[...] = stiff_ref[...].T
@@ -157,7 +180,11 @@
         total = planes_ref[r].astype(f32)
         for q in range(1, 8):
             total = total + planes_ref[2 * q + r].astype(f32)
-        half_ref[:, 64 * r : 64 * (r + 1)] = total.T
+        half_ref[64 * r : 64 * (r + 1), :] = total
+
+
+def flip_kernel(both_ref, out_ref):
+    out_ref[...] = both_ref[...].T
 
 
 def swap(value, axis):
@@ -172,7 +199,7 @@
     vmem = pl.BlockSpec(memory_space=pltpu.VMEM)
     shape = jax.ShapeDtypeStruct
     xside, yside = SY * GROUP, SX * GROUP
-    panel, zsend, xfirst, xlast, yfirst, ylast = pl.pallas_call(
+    panel, zsend, xinner, xouter, yfirst, ylast = pl.pallas_call(
         collect_kernel,
         in_specs=[pl.BlockSpec(memory_space=pl.ANY)],
         out_specs=[vmem] * 6,
@@ -185,20 +212,26 @@
     zface = swap(zsend, GZ)
     ylo = lax.ppermute(ylast, COL, chain)
     yhi = lax.ppermute(yfirst, COL, back)
-    xlo = lax.ppermute(xlast, ROW, chain)
-    xhi = lax.ppermute(xfirst, ROW, back)
+    chip = swap(xinner, "core")
+    pairs = [(i, i + 1) for i in range(1, 15, 2)]
+    beside = lax.ppermute(xouter, ROW, pairs + [(j, i) for i, j in pairs])
     coef, part, near = pl.pallas_call(
         local_kernel,
         in_specs=[vmem] * 3 + [pl.BlockSpec(memory_space=pl.ANY)],
         out_specs=[vmem] * 3,
-        out_shape=[shape((CELLS, SZ, 128), f32), shape((ROWS, PANEL), f32), shape((ROWS, full), bf16)],
-        scratch_shapes=[pltpu.VMEM((CELLS, SZ, 128), f32), pltpu.VMEM((NMAT, 128), f32), pltpu.SemaphoreType.DMA],
+        out_shape=[shape((CELLS * SZ, 128), f32), shape((ROWS, PANEL), f32), shape((ROWS, full), bf16)],
+        scratch_shapes=[
+            pltpu.VMEM((NMAT, 128), f32),
+            pltpu.VMEM((7, 4 * NMAT, 9 * HALF), bf16),
+            pltpu.VMEM((5, CELLS * SZ, 4 * NMAT), bf16),
+            pltpu.VMEM((7, CELLS * SZ, 9 * HALF), f32),
+            pltpu.SemaphoreType.DMA,
+        ],
         cost_estimate=pl.CostEstimate(flops=2 * ROWS * 21 * PANEL, bytes_accessed=3 * ROWS * PANEL, transcendentals=0),
         compiler_params=pltpu.CompilerParams(vmem_limit_bytes=46 << 20),
         name="local_stencil",
     )(material.transpose(1, 0, 2), blocks.transpose(2, 3, 0, 1), panel, flat)
     tiles = full // HALF
-    coef = coef.reshape(CELLS * SZ, 128)
     term = pl.pallas_call(
         edge_kernel,
         in_specs=[vmem] * 2,
@@ -217,7 +250,7 @@
         cost_estimate=pl.CostEstimate(flops=2 * ROWS * full * PANEL, bytes_accessed=2 * ROWS * full, transcendentals=0),
         compiler_params=pltpu.CompilerParams(vmem_limit_bytes=32 << 20),
         name="faces_and_product",
-    )(ylo, yhi, xlo, xhi, coef, part, term, near)
+    )(ylo, yhi, chip, beside, coef, part, term, near)
     mine = (keep + swap(send, "core").astype(f32)).astype(bf16)
     parts = lax.all_to_all(mine.reshape(2 * tiles, HALF // 2, HALF), COL + ("zl",), 0, 0, tiled=True)
     copies = pl.pallas_call(
@@ -237,9 +270,15 @@
         compiler_params=pltpu.CompilerParams(vmem_limit_bytes=4 << 20),
         name="fold",
     )(planes)
-    other = swap(half, "core")
-    first = lax.axis_index("core") == 0
-    return jnp.concatenate([jnp.where(first, half, other), jnp.where(first, other, half)], axis=1)
+    both = lax.all_gather(half, "core", axis=0, tiled=True)
+    return pl.pallas_call(
+        flip_kernel,
+        in_specs=[vmem],
+        out_specs=vmem,
+        out_shape=shape((HALF, PANEL), f32),
+        compiler_params=pltpu.CompilerParams(vmem_limit_bytes=4 << 20),
+        name="flip",
+    )(both)
 
 
 def solution(mesh):

time: 89.6 us -> 84.9 us (0.948)
  starting transfers between devices: 36.7 us -> 28.3 us
  blocking collectives: 37.8 us -> 45.2 us
  Pallas kernels: 11 us -> 8.87 us
    all_gather x0 -> x1, blocking collectives: none -> 8.34 us  [shards(): both = lax.all_gather(half, 'core', axis=0, tiled=True)]
    ppermute x3, starting transfers between devices: 26.9 us -> 21.3 us  [swap(): return lax.ppermute(value, axis, [(0, 1), (1, 0)])]
    ppermute x2 -> x1, starting transfers between devices: 5.41 us -> 2.54 us  [shards(): beside = lax.ppermute(xouter, ROW, pairs + [(j, i) for i, j in pairs])]
    pallas_call x1, Pallas kernels: 6.95 us -> 4.16 us  [shards(): pl.pallas_call(local_kernel, in_specs=[vmem] * 3 + [pl.BlockSpec(memory_s...]
    all_to_all x1, blocking collectives: 20.8 us -> 19.9 us  [shards(): lax.all_to_all(mine.reshape(2 * tiles, HALF // 2, HALF), COL + ('zl',), 0...]
  transfers between devices with their start and end apart: 7 -> 6, of which waited for: 2 -> 1; matrix products, arithmetic and copies ran while one was open for 0% -> 0% of each run, Pallas kernels for 8% -> 5%
where the time goes in v5:
time: 84.9 us; the launch traced here: 84.6 us
  blocking collectives  45.2 us (53%)
  starting transfers between devices  28.3 us (33%)
  Pallas kernels  8.87 us (10%)
  waiting for transfers between devices  1.89 us (2%)
    ppermute x3, starting transfers between devices, swap(): return lax.ppermute(value, axis, [(0, 1), (1, 0)])  21.3 us
    all_to_all x1, blocking collectives, shards(): lax.all_to_all(mine.reshape(2 * tiles, HALF // 2, HALF), COL + ('zl',), 0...  19.9 us
    all_to_all x1, blocking collectives, shards(): planes = lax.all_to_all(copies, Z, 0, 0, tiled=True)  17 us
    all_gather x1, blocking collectives, shards(): both = lax.all_gather(half, 'core', axis=0, tiled=True)  8.34 us
    pallas_call x1, Pallas kernels, shards(): pl.pallas_call(local_kernel, in_specs=[vmem] * 3 + [pl.BlockSpec(memory_s...  4.16 us
    ppermute x1, starting transfers between devices, shards(): ylo = lax.ppermute(ylast, COL, chain)  3.12 us
    ppermute x1, starting transfers between devices, shards(): beside = lax.ppermute(xouter, ROW, pairs + [(j, i) for i, j in pairs])  2.54 us
    pallas_call x1, Pallas kernels, shards(): pl.pallas_call(product_kernel, in_specs=[vmem] * 8, out_specs=[vmem] * 2,...  2.4 us
  transfers between devices with their start and end apart: 6, of which 1 were waited for; matrix products, arithmetic and copies ran while one was open for 0% of the time, Pallas kernels for 5%

profile of v5, /device:TPU:1, one launch (start us, length us, event | category | flops | bytes accessed | tf_op | source)
XLA Modules:
  0.0 84.6 jit_solution(4224258459952493659)
XLA Ops:
  0.0 0.0 copy-start.1
  0.0 0.0 copy-start
  0.0 1.2 %collect_faces.1 = (f32[2,1152,128]{2,1,0:T(8,128)S(1)}, bf16[72,256]{1,0:T(8,128)(2,1)S(1)}, bf16[288,256]{1,0:T(8,128)(2,1)S(1)}, bf16[288,256]{1,0:T(8,128)(2...) custom-call(bf16[1152,2048]{1,0:T(8,128)(2,1)} %bitcast.8), custom_call_target="tpu_custom_call" | custom-call | tf_op jit(solution)/shard_map/collect_faces/pallas_call | solution.py:202
  1.3 16.3 %collective-permute-start.4 = (bf16[72,256]{1,0:T(8,128)(2,1)S(1)}, bf16[72,256]{1,0:T(8,128)(2,1)S(1)}, u32[]{:S(2)}, u32[]{:S(2)}) collective-permute-start(bf16[72,256]{1,0:T(8,128)(2,1)S(1)} %get-tuple-element.23), channel_id=1, source_target_pairs={{0,1},{1,0},{2,3},{3,2},{4,5},{5,4},{6,7},{7,6},{8,9},{9,8},{10,11... | collective-permute-start | bytes 110600 | tf_op jit(solution)/shard_map/ppermute | solution.py:191
  17.5 3.1 %collective-permute-start = (bf16[192,256]{1,0:T(8,128)(2,1)S(1)}, bf16[192,256]{1,0:T(8,128)(2,1)S(1)}, u32[]{:S(2)}, u32[]{:S(2)}) collective-permute-start(bf16[192,256]{1,0:T(8,128)(2,1)S(1)} %get-tuple-element.16), channel_id=1, source_target_pairs={{0,2},{2,4},{4,6},{6,8},{8,10},{10,12},{12,14},{14,16},{16,18},{18... | collective-permute-start | bytes 294920 | tf_op jit(solution)/shard_map/ppermute | solution.py:213
  20.7 1.3 %collective-permute-start.1 = (bf16[192,256]{1,0:T(8,128)(2,1)S(1)}, bf16[192,256]{1,0:T(8,128)(2,1)S(1)}, u32[]{:S(2)}, u32[]{:S(2)}) collective-permute-start(bf16[192,256]{1,0:T(8,128)(2,1)S(1)} %get-tuple-element.17), channel_id=1, source_target_pairs={{2,0},{4,2},{6,4},{8,6},{10,8},{12,10},{14,12},{16,14},{18,16},{20... | collective-permute-start | bytes 294920 | tf_op jit(solution)/shard_map/ppermute | solution.py:214
  22.0 3.1 %collective-permute-start.2 = (bf16[288,256]{1,0:T(8,128)(2,1)S(1)}, bf16[288,256]{1,0:T(8,128)(2,1)S(1)}, u32[]{:S(2)}, u32[]{:S(2)}) collective-permute-start(bf16[288,256]{1,0:T(8,128)(2,1)S(1)} %get-tuple-element.18), channel_id=1, source_target_pairs={{0,32},{32,0},{1,33},{33,1},{2,34},{34,2},{3,35},{35,3},{4,36},{36... | collective-permute-start | bytes 442376 | tf_op jit(solution)/shard_map/ppermute | solution.py:191
  25.1 2.5 %collective-permute-start.3 = (bf16[288,256]{1,0:T(8,128)(2,1)S(1)}, bf16[288,256]{1,0:T(8,128)(2,1)S(1)}, u32[]{:S(2)}, u32[]{:S(2)}) collective-permute-start(bf16[288,256]{1,0:T(8,128)(2,1)S(1)} %get-tuple-element.19), channel_id=1, source_target_pairs={{32,64},{96,128},{160,192},{224,256},{288,320},{352,384},{416,448}... | collective-permute-start | bytes 442376 | tf_op jit(solution)/shard_map/ppermute | solution.py:217
  27.7 0.0 copy-done.1
  27.7 0.0 copy-done
  27.7 4.2 %local_stencil.1 = (f32[384,128]{1,0:T(8,128)S(1)}, f32[1152,256]{1,0:T(8,128)S(1)}, bf16[1152,2048]{1,0:T(8,128)(2,1)S(1)}) custom-call(s32[6,4,16]{2,1,0:T(4,128)S(1)} %bitcast.7, f32[3,3,8,7]{3,2,1,0:T(8,128)S(1)} %bitcast.6, f32[2,1152,128]{2,1,0:T(8,128)S(1)} %get-tuple-element.20.panel_ref, bf16[1152,2048]{1,0:T(8,128)(2,1)} %bitcast.9), custom_call_target="tpu_custom_call" | custom-call | flops 12386304 | bytes 884736 | tf_op jit(solution)/shard_map/local_stencil/pallas_call | solution.py:218
  31.8 0.0 collective-permute-done.4.zface_ref
  31.9 0.2 edge_terms.1.term_ref
  32.1 0.0 collective-permute-done.ylo_ref
  32.1 0.0 collective-permute-done.1.yhi_ref
  32.1 0.0 collective-permute-done.2.chip_ref
  32.1 0.0 collective-permute-done.3.beside_ref
  32.1 2.4 %faces_and_product.1 = (f32[16,128,128]{2,1,0:T(8,128)S(1)}, bf16[16,128,128]{2,1,0:T(8,128)(2,1)S(1)}) custom-call(bf16[192,256]{1,0:T(8,128)(2,1)S(1)} %collective-permute-done.ylo_ref, bf16[192,256]{1,0:T(8,128)(2,1)S(1)} %collective-permute-done.1.yhi_ref, bf16[288,256]{1,0:T(8,128)(2,1)S(1)} %collective-permute-done.2.chip_ref, ...), custom_call_target="tpu_custom_call" | custom-call | flops 1207959552 | bytes 4718592 | tf_op jit(solution)/shard_map/faces_and_product/pallas_call | solution.py:244
  34.5 1.9 %collective-permute-start.5 = (bf16[16,128,128]{2,1,0:T(8,128)(2,1)S(1)}, bf16[16,128,128]{2,1,0:T(8,128)(2,1)S(1)}, u32[]{:S(2)}, u32[]{:S(2)}) collective-permute-start(bf16[16,128,128]{2,1,0:T(8,128)(2,1)S(1)} %get-tuple-element.26), channel_id=1, source_target_pairs={{0,32},{32,0},{1,33},{33,1},{2,34},{34,2},{3,35},{35,3},{4,36},{36... | collective-permute-start | bytes 1572872 | tf_op jit(solution)/shard_map/ppermute | solution.py:191
  36.4 1.9 %collective-permute-done.5 = bf16[16,128,128]{2,1,0:T(8,128)(2,1)S(1)} collective-permute-done((bf16[16,128,128]{2,1,0:T(8,128)(2,1)S(1)}, bf16[16,128,128]{2,1,0:T(8,128)(2,1)S(1)}, u32[]{:S(2)}, u32[]{:S(2)}) %collective-permute-start.5) | collective-permute-done | bytes 524320 | tf_op jit(solution)/shard_map/ppermute | solution.py:191
  38.3 0.1 add_convert_fusion
  38.4 19.9 %all_to_all.10.parts_ref = bf16[32,64,128]{2,1,0:T(8,128)(2,1)S(1)} all-to-all(bf16[32,64,128]{2,1,0:T(8,128)(2,1)S(1)} %bitcast.10), channel_id=1, replica_groups=mesh['zh'=4,'zl'=2,'core'=2,'y'=4,'x'=4,'gz'=2] {'y','x','zl'}, dimensions={0} | all-to-all | bytes 1048576 | tf_op jit(solution)/shard_map/all_to_all | solution.py:255
  58.4 0.1 near_sum.1
  58.5 17.0 %all_to_all.11.planes_ref = bf16[16,64,128]{2,1,0:T(8,128)(2,1)S(1)} all-to-all(bf16[16,64,128]{2,1,0:T(8,128)(2,1)S(1)} %near_sum.1), channel_id=1, replica_groups=mesh['zh'=4,'zl'=2,'core'=2,'y'=4,'x'=4,'gz'=2] {'gz','zh','zl'}, dimensions={0} | all-to-all | bytes 524288 | tf_op jit(solution)/shard_map/all_to_all | solution.py:264
  75.5 8.3 %all_gather.3.both_ref = f32[256,128]{1,0:T(8,128)S(1)} all-gather(f32[128,128]{1,0:T(8,128)S(1)} %fold.1), channel_id=1, replica_groups=mesh['zh'=4,'zl'=2,'core'=2,'y'=4,'x'=4,'gz'=2] {'core'}, dimensions={0}, use_global_device_ids=true | all-gather | bytes 196608 | tf_op jit(solution)/shard_map/all_gather | solution.py:273
  83.8 0.8 flip.1
  (1 shorter events, 0.0 us)
Async XLA Ops:
  0.0 27.7 %copy-start.1 = (s32[4,6,16]{2,0,1:T(4,128)S(1)}, s32[4,6,16]{2,0,1:T(4,128)}, u32[]{:S(2)}) copy-start(s32[4,6,16]{2,0,1:T(4,128)} %param.5) | copy-start | bytes 4612
  0.0 27.7 %copy-start = (f32[8,7,3,3]{1,0,3,2:T(8,128)S(1)}, f32[8,7,3,3]{1,0,3,2:T(8,128)}, u32[]{:S(2)}) copy-start(f32[8,7,3,3]{1,0,3,2:T(8,128)} %param.4) | copy-start | bytes 6052
  1.3 30.6 %collective-permute-start.4 = (bf16[72,256]{1,0:T(8,128)(2,1)S(1)}, bf16[72,256]{1,0:T(8,128)(2,1)S(1)}, u32[]{:S(2)}, u32[]{:S(2)}) collective-permute-start(bf16[72,256]{1,0:T(8,128)(2,1)S(1)} %get-tuple-element.23), channel_id=1, source_target_pairs={{0,1},{1,0},{2,3},{3,2},{4,5},{5,4},{6,7},{7,6},{8,9},{9,8},{10,11... | collective-permute-start | bytes 110600 | tf_op jit(solution)/shard_map/ppermute | solution.py:191
  17.5 14.5 %collective-permute-start = (bf16[192,256]{1,0:T(8,128)(2,1)S(1)}, bf16[192,256]{1,0:T(8,128)(2,1)S(1)}, u32[]{:S(2)}, u32[]{:S(2)}) collective-permute-start(bf16[192,256]{1,0:T(8,128)(2,1)S(1)} %get-tuple-element.16), channel_id=1, source_target_pairs={{0,2},{2,4},{4,6},{6,8},{8,10},{10,12},{12,14},{14,16},{16,18},{18... | collective-permute-start | bytes 294920 | tf_op jit(solution)/shard_map/ppermute | solution.py:213
  20.7 11.4 %collective-permute-start.1 = (bf16[192,256]{1,0:T(8,128)(2,1)S(1)}, bf16[192,256]{1,0:T(8,128)(2,1)S(1)}, u32[]{:S(2)}, u32[]{:S(2)}) collective-permute-start(bf16[192,256]{1,0:T(8,128)(2,1)S(1)} %get-tuple-element.17), channel_id=1, source_target_pairs={{2,0},{4,2},{6,4},{8,6},{10,8},{12,10},{14,12},{16,14},{18,16},{20... | collective-permute-start | bytes 294920 | tf_op jit(solution)/shard_map/ppermute | solution.py:214
  22.0 10.1 %collective-permute-start.2 = (bf16[288,256]{1,0:T(8,128)(2,1)S(1)}, bf16[288,256]{1,0:T(8,128)(2,1)S(1)}, u32[]{:S(2)}, u32[]{:S(2)}) collective-permute-start(bf16[288,256]{1,0:T(8,128)(2,1)S(1)} %get-tuple-element.18), channel_id=1, source_target_pairs={{0,32},{32,0},{1,33},{33,1},{2,34},{34,2},{3,35},{35,3},{4,36},{36... | collective-permute-start | bytes 442376 | tf_op jit(solution)/shard_map/ppermute | solution.py:191
  25.1 7.0 %collective-permute-start.3 = (bf16[288,256]{1,0:T(8,128)(2,1)S(1)}, bf16[288,256]{1,0:T(8,128)(2,1)S(1)}, u32[]{:S(2)}, u32[]{:S(2)}) collective-permute-start(bf16[288,256]{1,0:T(8,128)(2,1)S(1)} %get-tuple-element.19), channel_id=1, source_target_pairs={{32,64},{96,128},{160,192},{224,256},{288,320},{352,384},{416,448}... | collective-permute-start | bytes 442376 | tf_op jit(solution)/shard_map/ppermute | solution.py:217
  34.5 3.8 %collective-permute-start.5 = (bf16[16,128,128]{2,1,0:T(8,128)(2,1)S(1)}, bf16[16,128,128]{2,1,0:T(8,128)(2,1)S(1)}, u32[]{:S(2)}, u32[]{:S(2)}) collective-permute-start(bf16[16,128,128]{2,1,0:T(8,128)(2,1)S(1)} %get-tuple-element.26), channel_id=1, source_target_pairs={{0,32},{32,0},{1,33},{33,1},{2,34},{34,2},{3,35},{35,3},{4,36},{36... | collective-permute-start | bytes 1572872 | tf_op jit(solution)/shard_map/ppermute | solution.py:191

commit v6 on v5

--- a/solution.py
+++ b/solution.py
@@ -23,7 +23,7 @@
     return jnp.broadcast_to(values[:, k : k + 1], (values.shape[0], width))
 
 
-def collect_kernel(modes_ref, panel_ref, z_ref, xin_ref, xout_ref, ylo_ref, yhi_ref, raw_ref, edge_ref, sem):
+def collect_kernel(modes_ref, panel_ref, z_ref, xin_ref, xout_ref, yin_ref, yout_ref, raw_ref, edge_ref, sem):
     copy = pltpu.make_async_copy(modes_ref.at[:, :PANEL], raw_ref, sem)
     copy.start()
     copy.wait()
@@ -39,9 +39,12 @@
     low = lax.axis_index("core") == 0
     xin_ref[...] = jnp.where(low, raw_ref[ROWS - side :, :], raw_ref[:side, :])
     xout_ref[...] = jnp.where(low, raw_ref[:side, :], raw_ref[ROWS - side :, :])
+    even = lax.axis_index("x") % 2 == 0
     for x in range(SX):
-        ylo_ref[x * GROUP : (x + 1) * GROUP, :] = raw_ref[x * side : x * side + GROUP, :]
-        yhi_ref[x * GROUP : (x + 1) * GROUP, :] = raw_ref[(x + 1) * side - GROUP : (x + 1) * side, :]
+        near = raw_ref[x * side : x * side + GROUP, :]
+        far = raw_ref[(x + 1) * side - GROUP : (x + 1) * side, :]
+        yin_ref[x * GROUP : (x + 1) * GROUP, :] = jnp.where(even, far, near)
+        yout_ref[x * GROUP : (x + 1) * GROUP, :] = jnp.where(even, near, far)
 
 
 def split3(value):
@@ -52,7 +55,7 @@
 
 
 def local_kernel(kind_ref, blocks_ref, panel_ref, modes_ref,
-                 coef_ref, part_ref, near_ref, table_ref, wide_ref, hot_ref, plane_ref, sem):
+                 coef_ref, wall_ref, part_ref, near_ref, table_ref, wide_ref, hot_ref, plane_ref, sem):
     copy = pltpu.make_async_copy(modes_ref, near_ref, sem)
     copy.start()
     table_ref[...] = jnp.zeros((NMAT, 128), f32)
@@ -78,6 +81,16 @@
     coef_ref[...] = jnp.dot(hot_ref[0], split3(table_ref[...]), preferred_element_type=f32)
     for o in range(7):
         plane_ref[o] = jnp.dot(hot_ref[o if o < 5 else 0], wide_ref[o], preferred_element_type=f32)
+    whole = hot_ref[0]
+    walls = (
+        [(SX - 1) * SY + y for y in range(SY)],
+        [y for y in range(SY)],
+        [x * SY + SY - 1 for x in range(SX)],
+        [x * SY for x in range(SX)],
+    )
+    for o, cells in enumerate(walls):
+        rows = jnp.concatenate([whole[n * SZ : (n + 1) * SZ] for n in cells])
+        wall_ref[o, : len(cells) * SZ, :] = jnp.dot(rows, wide_ref[o + 1], preferred_element_type=f32)
     level = lax.broadcasted_iota(jnp.int32, (SZ, HALF), 0)
     top, bottom = level == SZ - 1, level == 0
 
@@ -128,31 +141,31 @@
         term_ref[i * CELLS : (i + 1) * CELLS, :] = total
 
 
-def product_kernel(ylo_ref, yhi_ref, chip_ref, beside_ref, coef_ref, part_ref, term_ref, modes_ref,
+def product_kernel(yin_ref, yout_ref, chip_ref, beside_ref, wall_ref, part_ref, term_ref, modes_ref,
                    keep_ref, send_ref, stiff_ref, left_ref):
     core, gz = lax.axis_index("core"), lax.axis_index(GZ)
     level = lax.broadcasted_iota(jnp.int32, (SZ, PANEL), 0)
     at_edge = level == jnp.where(gz == 0, SZ - 1, 0)
     low = core == 0
+    even = lax.axis_index("x") % 2 == 0
     for n in range(CELLS):
         x, y = divmod(n, SY)
-        coef = coef_ref[n * SZ : (n + 1) * SZ, :]
-        faces = [(1, (chip_ref, beside_ref), y)] if x == SX - 1 else []
-        faces += [(2, (beside_ref, chip_ref), y)] if x == 0 else []
-        faces += [(3, (yhi_ref,), x)] if y == SY - 1 else []
-        faces += [(4, (ylo_ref,), x)] if y == 0 else []
+        faces = [(1, low, chip_ref, beside_ref, y)] if x == SX - 1 else []
+        faces += [(2, low, beside_ref, chip_ref, y)] if x == 0 else []
+        faces += [(3, even, yin_ref, yout_ref, x)] if y == SY - 1 else []
+        faces += [(4, even, yout_ref, yin_ref, x)] if y == 0 else []
         for i in range(3):
             start = n * GROUP + i * SZ
             row = i * CELLS + n
             term = jnp.broadcast_to(term_ref[row : row + 1, :], (SZ, PANEL))
             total = part_ref[start : start + SZ, :] + jnp.where(at_edge, term, 0.0)
-            for o, refs, k in faces:
+            for o, pick, one, two, cell in faces:
                 for j in range(3):
-                    at = slice(k * GROUP + j * SZ, k * GROUP + (j + 1) * SZ)
-                    value = refs[0][at, :].astype(f32)
-                    if len(refs) == 2:
-                        value = jnp.where(low, value, refs[1][at, :].astype(f32))
-                    total = total + lane(coef, o, i, j) * value
+                    at = slice(cell * GROUP + j * SZ, cell * GROUP + (j + 1) * SZ)
+                    value = jnp.where(pick, one[at, :].astype(f32), two[at, :].astype(f32))
+                    k = 3 * i + j
+                    factor = wall_ref[o - 1, cell * SZ : (cell + 1) * SZ, k * HALF : (k + 1) * HALF]
+                    total = total + jnp.concatenate([factor, factor], axis=1) * value
             stiff_ref[start : start + SZ, :] = total.astype(bf16)
     left_ref[...] = stiff_ref[...].T
     for t in range(modes_ref.shape[1] // PANEL):
@@ -194,12 +207,10 @@
 def shards(modes, blocks, material):
     full = modes.shape[-1]
     flat = modes.transpose(0, 1, 3, 2, 4).reshape(ROWS, full)
-    chain = [(i, i + 1) for i in range(15)]
-    back = [(j, i) for i, j in chain]
     vmem = pl.BlockSpec(memory_space=pltpu.VMEM)
     shape = jax.ShapeDtypeStruct
     xside, yside = SY * GROUP, SX * GROUP
-    panel, zsend, xinner, xouter, yfirst, ylast = pl.pallas_call(
+    panel, zsend, xinner, xouter, yinner, youter = pl.pallas_call(
         collect_kernel,
         in_specs=[pl.BlockSpec(memory_space=pl.ANY)],
         out_specs=[vmem] * 6,
@@ -210,16 +221,20 @@
         name="collect_faces",
     )(flat)
     zface = swap(zsend, GZ)
-    ylo = lax.ppermute(ylast, COL, chain)
-    yhi = lax.ppermute(yfirst, COL, back)
+
+    def pairs(start):
+        ends = [(i, i + 1) for i in range(start, 15, 2)]
+        return ends + [(j, i) for i, j in ends]
+
+    yin = lax.ppermute(yinner, COL, pairs(0))
+    yout = lax.ppermute(youter, COL, pairs(1))
     chip = swap(xinner, "core")
-    pairs = [(i, i + 1) for i in range(1, 15, 2)]
-    beside = lax.ppermute(xouter, ROW, pairs + [(j, i) for i, j in pairs])
-    coef, part, near = pl.pallas_call(
+    beside = lax.ppermute(xouter, ROW, pairs(1))
+    coef, wall, part, near = pl.pallas_call(
         local_kernel,
         in_specs=[vmem] * 3 + [pl.BlockSpec(memory_space=pl.ANY)],
-        out_specs=[vmem] * 3,
-        out_shape=[shape((CELLS * SZ, 128), f32), shape((ROWS, PANEL), f32), shape((ROWS, full), bf16)],
+        out_specs=[vmem] * 4,
+        out_shape=[shape((CELLS * SZ, 128), f32), shape((4, SY * SZ, 9 * HALF), f32), shape((ROWS, PANEL), f32), shape((ROWS, full), bf16)],
         scratch_shapes=[
             pltpu.VMEM((NMAT, 128), f32),
             pltpu.VMEM((7, 4 * NMAT, 9 * HALF), bf16),
@@ -228,7 +243,7 @@
             pltpu.SemaphoreType.DMA,
         ],
         cost_estimate=pl.CostEstimate(flops=2 * ROWS * 21 * PANEL, bytes_accessed=3 * ROWS * PANEL, transcendentals=0),
-        compiler_params=pltpu.CompilerParams(vmem_limit_bytes=46 << 20),
+        compiler_params=pltpu.CompilerParams(vmem_limit_bytes=44 << 20),
         name="local_stencil",
     )(material.transpose(1, 0, 2), blocks.transpose(2, 3, 0, 1), panel, flat)
     tiles = full // HALF
@@ -250,7 +265,7 @@
         cost_estimate=pl.CostEstimate(flops=2 * ROWS * full * PANEL, bytes_accessed=2 * ROWS * full, transcendentals=0),
         compiler_params=pltpu.CompilerParams(vmem_limit_bytes=32 << 20),
         name="faces_and_product",
-    )(ylo, yhi, chip, beside, coef, part, term, near)
+    )(yin, yout, chip, beside, wall, part, term, near)
     mine = (keep + swap(send, "core").astype(f32)).astype(bf16)
     parts = lax.all_to_all(mine.reshape(2 * tiles, HALF // 2, HALF), COL + ("zl",), 0, 0, tiled=True)
     copies = pl.pallas_call(

time: 84.9 us -> 84.9 us (level)
  blocking collectives: 45.2 us -> 46.3 us
    all_to_all x1, blocking collectives: 19.9 us -> 21 us  [shards(): lax.all_to_all(mine.reshape(2 * tiles, HALF // 2, HALF), COL + ('zl',), 0...]
where the time goes in v6:
time: 84.9 us; the launch traced here: 84.5 us
  blocking collectives  46.3 us (55%)
  starting transfers between devices  27.7 us (33%)
  Pallas kernels  8.44 us (10%)
  waiting for transfers between devices  1.89 us (2%)
    ppermute x3, starting transfers between devices, swap(): return lax.ppermute(value, axis, [(0, 1), (1, 0)])  21.3 us
    all_to_all x1, blocking collectives, shards(): lax.all_to_all(mine.reshape(2 * tiles, HALF // 2, HALF), COL + ('zl',), 0...  21 us
    all_to_all x1, blocking collectives, shards(): planes = lax.all_to_all(copies, Z, 0, 0, tiled=True)  17 us
    all_gather x1, blocking collectives, shards(): both = lax.all_gather(half, 'core', axis=0, tiled=True)  8.34 us
    pallas_call x1, Pallas kernels, shards(): pl.pallas_call(local_kernel, in_specs=[vmem] * 3 + [pl.BlockSpec(memory_s...  4.35 us
    ppermute x1, starting transfers between devices, shards(): yin = lax.ppermute(yinner, COL, pairs(0))  3.12 us
    ppermute x1, starting transfers between devices, shards(): beside = lax.ppermute(xouter, ROW, pairs(1))  2.54 us
    ppermute x3, waiting for transfers between devices, swap(): return lax.ppermute(value, axis, [(0, 1), (1, 0)])  1.88 us
  transfers between devices with their start and end apart: 6, of which 1 were waited for; matrix products, arithmetic and copies ran while one was open for 0% of the time, Pallas kernels for 5%

profile of v6, /device:TPU:1, one launch (start us, length us, event | category | flops | bytes accessed | tf_op | source)
XLA Modules:
  0.0 84.5 jit_solution(8977063237846639172)
XLA Ops:
  0.0 0.0 copy-start
  0.0 0.0 copy-start.1
  0.0 1.2 %collect_faces.1 = (f32[2,1152,128]{2,1,0:T(8,128)S(1)}, bf16[72,256]{1,0:T(8,128)(2,1)S(1)}, bf16[288,256]{1,0:T(8,128)(2,1)S(1)}, bf16[288,256]{1,0:T(8,128)(2...) custom-call(bf16[1152,2048]{1,0:T(8,128)(2,1)} %bitcast.8), custom_call_target="tpu_custom_call" | custom-call | tf_op jit(solution)/shard_map/collect_faces/pallas_call | solution.py:213
  1.3 16.3 %collective-permute-start.4 = (bf16[72,256]{1,0:T(8,128)(2,1)S(1)}, bf16[72,256]{1,0:T(8,128)(2,1)S(1)}, u32[]{:S(2)}, u32[]{:S(2)}) collective-permute-start(bf16[72,256]{1,0:T(8,128)(2,1)S(1)} %get-tuple-element.24), channel_id=1, source_target_pairs={{0,1},{1,0},{2,3},{3,2},{4,5},{5,4},{6,7},{7,6},{8,9},{9,8},{10,11... | collective-permute-start | bytes 110600 | tf_op jit(solution)/shard_map/ppermute | solution.py:204
  17.5 3.1 %collective-permute-start = (bf16[192,256]{1,0:T(8,128)(2,1)S(1)}, bf16[192,256]{1,0:T(8,128)(2,1)S(1)}, u32[]{:S(2)}, u32[]{:S(2)}) collective-permute-start(bf16[192,256]{1,0:T(8,128)(2,1)S(1)} %get-tuple-element.17), channel_id=1, source_target_pairs={{0,2},{4,6},{8,10},{12,14},{16,18},{20,22},{24,26},{28,30},{2,0},{... | collective-permute-start | bytes 294920 | tf_op jit(solution)/shard_map/ppermute | solution.py:229
  20.7 0.7 collective-permute-start.1
  21.3 3.1 %collective-permute-start.2 = (bf16[288,256]{1,0:T(8,128)(2,1)S(1)}, bf16[288,256]{1,0:T(8,128)(2,1)S(1)}, u32[]{:S(2)}, u32[]{:S(2)}) collective-permute-start(bf16[288,256]{1,0:T(8,128)(2,1)S(1)} %get-tuple-element.19), channel_id=1, source_target_pairs={{0,32},{32,0},{1,33},{33,1},{2,34},{34,2},{3,35},{35,3},{4,36},{36... | collective-permute-start | bytes 442376 | tf_op jit(solution)/shard_map/ppermute | solution.py:204
  24.5 2.5 %collective-permute-start.3 = (bf16[288,256]{1,0:T(8,128)(2,1)S(1)}, bf16[288,256]{1,0:T(8,128)(2,1)S(1)}, u32[]{:S(2)}, u32[]{:S(2)}) collective-permute-start(bf16[288,256]{1,0:T(8,128)(2,1)S(1)} %get-tuple-element.20), channel_id=1, source_target_pairs={{32,64},{96,128},{160,192},{224,256},{288,320},{352,384},{416,448}... | collective-permute-start | bytes 442376 | tf_op jit(solution)/shard_map/ppermute | solution.py:232
  27.0 0.0 copy-done
  27.0 0.0 copy-done.1
  27.0 4.4 %local_stencil.1 = (f32[384,128]{1,0:T(8,128)S(1)}, f32[4,96,1152]{2,1,0:T(8,128)S(1)}, f32[1152,256]{1,0:T(8,128)S(1)}, bf16[1152,2048]{1,0:T(8,128)(2,1)S(1)}) custom-call(s32[6,4,16]{2,1,0:T(4,128)S(1)} %bitcast.7, f32[3,3,8,7]{3,2,1,0:T(8,128)S(1)} %bitcast.6, f32[2,1152,128]{2,1,0:T(8,128)S(1)} %get-tuple-element.21.panel_ref, bf16[1152,2048]{1,0:T(8,128)(2,1)} %bitcast.9), custom_call_target="tpu_custom_call" | custom-call | flops 12386304 | bytes 884736 | tf_op jit(solution)/shard_map/local_stencil/pallas_call | solution.py:233
  31.4 0.0 collective-permute-done.4.zface_ref
  31.4 0.2 edge_terms.1.term_ref
  31.6 0.0 collective-permute-done.yin_ref
  31.6 0.0 collective-permute-done.1.yout_ref
  31.6 0.0 collective-permute-done.2.chip_ref
  31.6 0.0 collective-permute-done.3.beside_ref
  31.7 1.8 %faces_and_product.1 = (f32[16,128,128]{2,1,0:T(8,128)S(1)}, bf16[16,128,128]{2,1,0:T(8,128)(2,1)S(1)}) custom-call(bf16[192,256]{1,0:T(8,128)(2,1)S(1)} %collective-permute-done.yin_ref, bf16[192,256]{1,0:T(8,128)(2,1)S(1)} %collective-permute-done.1.yout_ref, bf16[288,256]{1,0:T(8,128)(2,1)S(1)} %collective-permute-done.2.chip_ref, ...), custom_call_target="tpu_custom_call" | custom-call | flops 1207959552 | bytes 4718592 | tf_op jit(solution)/shard_map/faces_and_product/pallas_call | solution.py:259
  33.4 1.9 %collective-permute-start.5 = (bf16[16,128,128]{2,1,0:T(8,128)(2,1)S(1)}, bf16[16,128,128]{2,1,0:T(8,128)(2,1)S(1)}, u32[]{:S(2)}, u32[]{:S(2)}) collective-permute-start(bf16[16,128,128]{2,1,0:T(8,128)(2,1)S(1)} %get-tuple-element.28), channel_id=1, source_target_pairs={{0,32},{32,0},{1,33},{33,1},{2,34},{34,2},{3,35},{35,3},{4,36},{36... | collective-permute-start | bytes 1572872 | tf_op jit(solution)/shard_map/ppermute | solution.py:204
  35.4 1.9 %collective-permute-done.5 = bf16[16,128,128]{2,1,0:T(8,128)(2,1)S(1)} collective-permute-done((bf16[16,128,128]{2,1,0:T(8,128)(2,1)S(1)}, bf16[16,128,128]{2,1,0:T(8,128)(2,1)S(1)}, u32[]{:S(2)}, u32[]{:S(2)}) %collective-permute-start.5) | collective-permute-done | bytes 524320 | tf_op jit(solution)/shard_map/ppermute | solution.py:204
  37.3 0.1 add_convert_fusion
  37.4 21.0 %all_to_all.10.parts_ref = bf16[32,64,128]{2,1,0:T(8,128)(2,1)S(1)} all-to-all(bf16[32,64,128]{2,1,0:T(8,128)(2,1)S(1)} %bitcast.10), channel_id=1, replica_groups=mesh['zh'=4,'zl'=2,'core'=2,'y'=4,'x'=4,'gz'=2] {'y','x','zl'}, dimensions={0} | all-to-all | bytes 1048576 | tf_op jit(solution)/shard_map/all_to_all | solution.py:270
  58.4 0.1 near_sum.1
  58.4 17.0 %all_to_all.11.planes_ref = bf16[16,64,128]{2,1,0:T(8,128)(2,1)S(1)} all-to-all(bf16[16,64,128]{2,1,0:T(8,128)(2,1)S(1)} %near_sum.1), channel_id=1, replica_groups=mesh['zh'=4,'zl'=2,'core'=2,'y'=4,'x'=4,'gz'=2] {'gz','zh','zl'}, dimensions={0} | all-to-all | bytes 524288 | tf_op jit(solution)/shard_map/all_to_all | solution.py:279
  75.5 8.3 %all_gather.3.both_ref = f32[256,128]{1,0:T(8,128)S(1)} all-gather(f32[128,128]{1,0:T(8,128)S(1)} %fold.1), channel_id=1, replica_groups=mesh['zh'=4,'zl'=2,'core'=2,'y'=4,'x'=4,'gz'=2] {'core'}, dimensions={0}, use_global_device_ids=true | all-gather | bytes 196608 | tf_op jit(solution)/shard_map/all_gather | solution.py:288
  83.8 0.8 flip.1
  (1 shorter events, 0.0 us)
Async XLA Ops:
  0.0 27.0 %copy-start = (f32[8,7,3,3]{1,0,3,2:T(8,128)S(1)}, f32[8,7,3,3]{1,0,3,2:T(8,128)}, u32[]{:S(2)}) copy-start(f32[8,7,3,3]{1,0,3,2:T(8,128)} %param.4) | copy-start | bytes 6052
  0.0 27.0 %copy-start.1 = (s32[4,6,16]{2,0,1:T(4,128)S(1)}, s32[4,6,16]{2,0,1:T(4,128)}, u32[]{:S(2)}) copy-start(s32[4,6,16]{2,0,1:T(4,128)} %param.5) | copy-start | bytes 4612
  1.3 30.2 %collective-permute-start.4 = (bf16[72,256]{1,0:T(8,128)(2,1)S(1)}, bf16[72,256]{1,0:T(8,128)(2,1)S(1)}, u32[]{:S(2)}, u32[]{:S(2)}) collective-permute-start(bf16[72,256]{1,0:T(8,128)(2,1)S(1)} %get-tuple-element.24), channel_id=1, source_target_pairs={{0,1},{1,0},{2,3},{3,2},{4,5},{5,4},{6,7},{7,6},{8,9},{9,8},{10,11... | collective-permute-start | bytes 110600 | tf_op jit(solution)/shard_map/ppermute | solution.py:204
  17.5 14.1 %collective-permute-start = (bf16[192,256]{1,0:T(8,128)(2,1)S(1)}, bf16[192,256]{1,0:T(8,128)(2,1)S(1)}, u32[]{:S(2)}, u32[]{:S(2)}) collective-permute-start(bf16[192,256]{1,0:T(8,128)(2,1)S(1)} %get-tuple-element.17), channel_id=1, source_target_pairs={{0,2},{4,6},{8,10},{12,14},{16,18},{20,22},{24,26},{28,30},{2,0},{... | collective-permute-start | bytes 294920 | tf_op jit(solution)/shard_map/ppermute | solution.py:229
  20.7 11.0 %collective-permute-start.1 = (bf16[192,256]{1,0:T(8,128)(2,1)S(1)}, bf16[192,256]{1,0:T(8,128)(2,1)S(1)}, u32[]{:S(2)}, u32[]{:S(2)}) collective-permute-start(bf16[192,256]{1,0:T(8,128)(2,1)S(1)} %get-tuple-element.18), channel_id=1, source_target_pairs={{2,4},{6,8},{10,12},{14,16},{18,20},{22,24},{26,28},{4,2},{8,6},{1... | collective-permute-start | bytes 294920 | tf_op jit(solution)/shard_map/ppermute | solution.py:230
  21.3 10.3 %collective-permute-start.2 = (bf16[288,256]{1,0:T(8,128)(2,1)S(1)}, bf16[288,256]{1,0:T(8,128)(2,1)S(1)}, u32[]{:S(2)}, u32[]{:S(2)}) collective-permute-start(bf16[288,256]{1,0:T(8,128)(2,1)S(1)} %get-tuple-element.19), channel_id=1, source_target_pairs={{0,32},{32,0},{1,33},{33,1},{2,34},{34,2},{3,35},{35,3},{4,36},{36... | collective-permute-start | bytes 442376 | tf_op jit(solution)/shard_map/ppermute | solution.py:204
  24.5 7.2 %collective-permute-start.3 = (bf16[288,256]{1,0:T(8,128)(2,1)S(1)}, bf16[288,256]{1,0:T(8,128)(2,1)S(1)}, u32[]{:S(2)}, u32[]{:S(2)}) collective-permute-start(bf16[288,256]{1,0:T(8,128)(2,1)S(1)} %get-tuple-element.20), channel_id=1, source_target_pairs={{32,64},{96,128},{160,192},{224,256},{288,320},{352,384},{416,448}... | collective-permute-start | bytes 442376 | tf_op jit(solution)/shard_map/ppermute | solution.py:232
  33.4 3.8 %collective-permute-start.5 = (bf16[16,128,128]{2,1,0:T(8,128)(2,1)S(1)}, bf16[16,128,128]{2,1,0:T(8,128)(2,1)S(1)}, u32[]{:S(2)}, u32[]{:S(2)}) collective-permute-start(bf16[16,128,128]{2,1,0:T(8,128)(2,1)S(1)} %get-tuple-element.28), channel_id=1, source_target_pairs={{0,32},{32,0},{1,33},{33,1},{2,34},{34,2},{3,35},{35,3},{4,36},{36... | collective-permute-start | bytes 1572872 | tf_op jit(solution)/shard_map/ppermute | solution.py:204

commit v7 on v6

--- a/solution.py
+++ b/solution.py
@@ -252,7 +252,7 @@
         in_specs=[vmem] * 2,
         out_specs=vmem,
         out_shape=shape((EDGE, PANEL), f32),
-        cost_estimate=pl.CostEstimate(flops=4 * 10**9, bytes_accessed=EDGE * PANEL * 6, transcendentals=0),
+        cost_estimate=pl.CostEstimate(flops=95 * 10**7, bytes_accessed=EDGE * PANEL * 6, transcendentals=0),
         compiler_params=pltpu.CompilerParams(vmem_limit_bytes=8 << 20),
         name="edge_terms",
     )(zface, coef)

time: 84.9 us -> 85.5 us (level)
  blocking collectives: 46.3 us -> 47.4 us
where the time goes in v7:
time: 85.5 us; the launch traced here: 85.1 us
  blocking collectives  47.4 us (55%)
  starting transfers between devices  27.1 us (32%)
  Pallas kernels  8.44 us (10%)
  waiting for transfers between devices  1.89 us (2%)
    all_to_all x1, blocking collectives, shards(): lax.all_to_all(mine.reshape(2 * tiles, HALF // 2, HALF), COL + ('zl',), 0...  21.8 us
    ppermute x3, starting transfers between devices, swap(): return lax.ppermute(value, axis, [(0, 1), (1, 0)])  21.4 us
    all_to_all x1, blocking collectives, shards(): planes = lax.all_to_all(copies, Z, 0, 0, tiled=True)  17.3 us
    all_gather x1, blocking collectives, shards(): both = lax.all_gather(half, 'core', axis=0, tiled=True)  8.34 us
    pallas_call x1, Pallas kernels, shards(): pl.pallas_call(local_kernel, in_specs=[vmem] * 3 + [pl.BlockSpec(memory_s...  4.35 us
    ppermute x1, starting transfers between devices, shards(): yin = lax.ppermute(yinner, COL, pairs(0))  3.12 us
    ppermute x1, starting transfers between devices, shards(): beside = lax.ppermute(xouter, ROW, pairs(1))  1.92 us
    ppermute x3, waiting for transfers between devices, swap(): return lax.ppermute(value, axis, [(0, 1), (1, 0)])  1.88 us
  transfers between devices with their start and end apart: 6, of which 1 were waited for; matrix products, arithmetic and copies ran while one was open for 0% of the time, Pallas kernels for 5%

profile of v7, /device:TPU:1, one launch (start us, length us, event | category | flops | bytes accessed | tf_op | source)
XLA Modules:
  0.0 85.1 jit_solution(6937245583951954160)
XLA Ops:
  0.0 0.0 copy-start
  0.0 0.0 copy-start.1
  0.0 1.2 %collect_faces.1 = (f32[2,1152,128]{2,1,0:T(8,128)S(1)}, bf16[72,256]{1,0:T(8,128)(2,1)S(1)}, bf16[288,256]{1,0:T(8,128)(2,1)S(1)}, bf16[288,256]{1,0:T(8,128)(2...) custom-call(bf16[1152,2048]{1,0:T(8,128)(2,1)} %bitcast.8), custom_call_target="tpu_custom_call" | custom-call | tf_op jit(solution)/shard_map/collect_faces/pallas_call | solution.py:213
  1.3 8.8 %collective-permute-start.2 = (bf16[288,256]{1,0:T(8,128)(2,1)S(1)}, bf16[288,256]{1,0:T(8,128)(2,1)S(1)}, u32[]{:S(2)}, u32[]{:S(2)}) collective-permute-start(bf16[288,256]{1,0:T(8,128)(2,1)S(1)} %get-tuple-element.19), channel_id=1, source_target_pairs={{0,32},{32,0},{1,33},{33,1},{2,34},{34,2},{3,35},{35,3},{4,36},{36... | collective-permute-start | bytes 442376 | tf_op jit(solution)/shard_map/ppermute | solution.py:204
  10.0 1.9 %collective-permute-start.3 = (bf16[288,256]{1,0:T(8,128)(2,1)S(1)}, bf16[288,256]{1,0:T(8,128)(2,1)S(1)}, u32[]{:S(2)}, u32[]{:S(2)}) collective-permute-start(bf16[288,256]{1,0:T(8,128)(2,1)S(1)} %get-tuple-element.20), channel_id=1, source_target_pairs={{32,64},{96,128},{160,192},{224,256},{288,320},{352,384},{416,448}... | collective-permute-start | bytes 442376 | tf_op jit(solution)/shard_map/ppermute | solution.py:232
  12.0 10.7 %collective-permute-start.4 = (bf16[72,256]{1,0:T(8,128)(2,1)S(1)}, bf16[72,256]{1,0:T(8,128)(2,1)S(1)}, u32[]{:S(2)}, u32[]{:S(2)}) collective-permute-start(bf16[72,256]{1,0:T(8,128)(2,1)S(1)} %get-tuple-element.24), channel_id=1, source_target_pairs={{0,1},{1,0},{2,3},{3,2},{4,5},{5,4},{6,7},{7,6},{8,9},{9,8},{10,11... | collective-permute-start | bytes 110600 | tf_op jit(solution)/shard_map/ppermute | solution.py:204
  22.7 3.1 %collective-permute-start = (bf16[192,256]{1,0:T(8,128)(2,1)S(1)}, bf16[192,256]{1,0:T(8,128)(2,1)S(1)}, u32[]{:S(2)}, u32[]{:S(2)}) collective-permute-start(bf16[192,256]{1,0:T(8,128)(2,1)S(1)} %get-tuple-element.17), channel_id=1, source_target_pairs={{0,2},{4,6},{8,10},{12,14},{16,18},{20,22},{24,26},{28,30},{2,0},{... | collective-permute-start | bytes 294920 | tf_op jit(solution)/shard_map/ppermute | solution.py:229
  25.8 0.7 collective-permute-start.1
  26.5 0.0 copy-done
  26.5 0.0 copy-done.1
  26.5 4.4 %local_stencil.1 = (f32[384,128]{1,0:T(8,128)S(1)}, f32[4,96,1152]{2,1,0:T(8,128)S(1)}, f32[1152,256]{1,0:T(8,128)S(1)}, bf16[1152,2048]{1,0:T(8,128)(2,1)S(1)}) custom-call(s32[6,4,16]{2,1,0:T(4,128)S(1)} %bitcast.7, f32[3,3,8,7]{3,2,1,0:T(8,128)S(1)} %bitcast.6, f32[2,1152,128]{2,1,0:T(8,128)S(1)} %get-tuple-element.21.panel_ref, bf16[1152,2048]{1,0:T(8,128)(2,1)} %bitcast.9), custom_call_target="tpu_custom_call" | custom-call | flops 12386304 | bytes 884736 | tf_op jit(solution)/shard_map/local_stencil/pallas_call | solution.py:233
  30.8 0.0 collective-permute-done.4.zface_ref
  30.9 0.2 edge_terms.1.term_ref
  31.1 0.0 collective-permute-done.yin_ref
  31.1 0.0 collective-permute-done.1.yout_ref
  31.1 0.0 collective-permute-done.2.chip_ref
  31.1 0.0 collective-permute-done.3.beside_ref
  31.1 1.8 %faces_and_product.1 = (f32[16,128,128]{2,1,0:T(8,128)S(1)}, bf16[16,128,128]{2,1,0:T(8,128)(2,1)S(1)}) custom-call(bf16[192,256]{1,0:T(8,128)(2,1)S(1)} %collective-permute-done.yin_ref, bf16[192,256]{1,0:T(8,128)(2,1)S(1)} %collective-permute-done.1.yout_ref, bf16[288,256]{1,0:T(8,128)(2,1)S(1)} %collective-permute-done.2.chip_ref, ...), custom_call_target="tpu_custom_call" | custom-call | flops 1207959552 | bytes 4718592 | tf_op jit(solution)/shard_map/faces_and_product/pallas_call | solution.py:259
  32.9 1.9 %collective-permute-start.5 = (bf16[16,128,128]{2,1,0:T(8,128)(2,1)S(1)}, bf16[16,128,128]{2,1,0:T(8,128)(2,1)S(1)}, u32[]{:S(2)}, u32[]{:S(2)}) collective-permute-start(bf16[16,128,128]{2,1,0:T(8,128)(2,1)S(1)} %get-tuple-element.28), channel_id=1, source_target_pairs={{0,32},{32,0},{1,33},{33,1},{2,34},{34,2},{3,35},{35,3},{4,36},{36... | collective-permute-start | bytes 1572872 | tf_op jit(solution)/shard_map/ppermute | solution.py:204
  34.8 1.9 %collective-permute-done.5 = bf16[16,128,128]{2,1,0:T(8,128)(2,1)S(1)} collective-permute-done((bf16[16,128,128]{2,1,0:T(8,128)(2,1)S(1)}, bf16[16,128,128]{2,1,0:T(8,128)(2,1)S(1)}, u32[]{:S(2)}, u32[]{:S(2)}) %collective-permute-start.5) | collective-permute-done | bytes 524320 | tf_op jit(solution)/shard_map/ppermute | solution.py:204
  36.7 0.1 add_convert_fusion
  36.8 21.8 %all_to_all.10.parts_ref = bf16[32,64,128]{2,1,0:T(8,128)(2,1)S(1)} all-to-all(bf16[32,64,128]{2,1,0:T(8,128)(2,1)S(1)} %bitcast.10), channel_id=1, replica_groups=mesh['zh'=4,'zl'=2,'core'=2,'y'=4,'x'=4,'gz'=2] {'y','x','zl'}, dimensions={0} | all-to-all | bytes 1048576 | tf_op jit(solution)/shard_map/all_to_all | solution.py:270
  58.6 0.1 near_sum.1
  58.7 17.3 %all_to_all.11.planes_ref = bf16[16,64,128]{2,1,0:T(8,128)(2,1)S(1)} all-to-all(bf16[16,64,128]{2,1,0:T(8,128)(2,1)S(1)} %near_sum.1), channel_id=1, replica_groups=mesh['zh'=4,'zl'=2,'core'=2,'y'=4,'x'=4,'gz'=2] {'gz','zh','zl'}, dimensions={0} | all-to-all | bytes 524288 | tf_op jit(solution)/shard_map/all_to_all | solution.py:279
  76.0 8.3 %all_gather.3.both_ref = f32[256,128]{1,0:T(8,128)S(1)} all-gather(f32[128,128]{1,0:T(8,128)S(1)} %fold.1), channel_id=1, replica_groups=mesh['zh'=4,'zl'=2,'core'=2,'y'=4,'x'=4,'gz'=2] {'core'}, dimensions={0}, use_global_device_ids=true | all-gather | bytes 196608 | tf_op jit(solution)/shard_map/all_gather | solution.py:288
  84.4 0.8 flip.1
  (1 shorter events, 0.0 us)
Async XLA Ops:
  0.0 26.5 %copy-start = (f32[8,7,3,3]{1,0,3,2:T(8,128)S(1)}, f32[8,7,3,3]{1,0,3,2:T(8,128)}, u32[]{:S(2)}) copy-start(f32[8,7,3,3]{1,0,3,2:T(8,128)} %param.4) | copy-start | bytes 6052
  0.0 26.5 %copy-start.1 = (s32[4,6,16]{2,0,1:T(4,128)S(1)}, s32[4,6,16]{2,0,1:T(4,128)}, u32[]{:S(2)}) copy-start(s32[4,6,16]{2,0,1:T(4,128)} %param.5) | copy-start | bytes 4612
  1.3 29.8 %collective-permute-start.2 = (bf16[288,256]{1,0:T(8,128)(2,1)S(1)}, bf16[288,256]{1,0:T(8,128)(2,1)S(1)}, u32[]{:S(2)}, u32[]{:S(2)}) collective-permute-start(bf16[288,256]{1,0:T(8,128)(2,1)S(1)} %get-tuple-element.19), channel_id=1, source_target_pairs={{0,32},{32,0},{1,33},{33,1},{2,34},{34,2},{3,35},{35,3},{4,36},{36... | collective-permute-start | bytes 442376 | tf_op jit(solution)/shard_map/ppermute | solution.py:204
  10.0 21.0 %collective-permute-start.3 = (bf16[288,256]{1,0:T(8,128)(2,1)S(1)}, bf16[288,256]{1,0:T(8,128)(2,1)S(1)}, u32[]{:S(2)}, u32[]{:S(2)}) collective-permute-start(bf16[288,256]{1,0:T(8,128)(2,1)S(1)} %get-tuple-element.20), channel_id=1, source_target_pairs={{32,64},{96,128},{160,192},{224,256},{288,320},{352,384},{416,448}... | collective-permute-start | bytes 442376 | tf_op jit(solution)/shard_map/ppermute | solution.py:232
  12.0 18.9 %collective-permute-start.4 = (bf16[72,256]{1,0:T(8,128)(2,1)S(1)}, bf16[72,256]{1,0:T(8,128)(2,1)S(1)}, u32[]{:S(2)}, u32[]{:S(2)}) collective-permute-start(bf16[72,256]{1,0:T(8,128)(2,1)S(1)} %get-tuple-element.24), channel_id=1, source_target_pairs={{0,1},{1,0},{2,3},{3,2},{4,5},{5,4},{6,7},{7,6},{8,9},{9,8},{10,11... | collective-permute-start | bytes 110600 | tf_op jit(solution)/shard_map/ppermute | solution.py:204
  22.7 8.4 %collective-permute-start = (bf16[192,256]{1,0:T(8,128)(2,1)S(1)}, bf16[192,256]{1,0:T(8,128)(2,1)S(1)}, u32[]{:S(2)}, u32[]{:S(2)}) collective-permute-start(bf16[192,256]{1,0:T(8,128)(2,1)S(1)} %get-tuple-element.17), channel_id=1, source_target_pairs={{0,2},{4,6},{8,10},{12,14},{16,18},{20,22},{24,26},{28,30},{2,0},{... | collective-permute-start | bytes 294920 | tf_op jit(solution)/shard_map/ppermute | solution.py:229
  25.8 5.3 %collective-permute-start.1 = (bf16[192,256]{1,0:T(8,128)(2,1)S(1)}, bf16[192,256]{1,0:T(8,128)(2,1)S(1)}, u32[]{:S(2)}, u32[]{:S(2)}) collective-permute-start(bf16[192,256]{1,0:T(8,128)(2,1)S(1)} %get-tuple-element.18), channel_id=1, source_target_pairs={{2,4},{6,8},{10,12},{14,16},{18,20},{22,24},{26,28},{4,2},{8,6},{1... | collective-permute-start | bytes 294920 | tf_op jit(solution)/shard_map/ppermute | solution.py:230
  32.9 3.8 %collective-permute-start.5 = (bf16[16,128,128]{2,1,0:T(8,128)(2,1)S(1)}, bf16[16,128,128]{2,1,0:T(8,128)(2,1)S(1)}, u32[]{:S(2)}, u32[]{:S(2)}) collective-permute-start(bf16[16,128,128]{2,1,0:T(8,128)(2,1)S(1)} %get-tuple-element.28), channel_id=1, source_target_pairs={{0,32},{32,0},{1,33},{33,1},{2,34},{34,2},{3,35},{35,3},{4,36},{36... | collective-permute-start | bytes 1572872 | tf_op jit(solution)/shard_map/ppermute | solution.py:204

commit v8 on v6

--- a/solution.py
+++ b/solution.py
@@ -50,15 +50,20 @@
 def split3(value):
     high = value.astype(bf16).astype(f32)
     mid = (value - high).astype(bf16).astype(f32)
-    low = value - high - mid
-    return jnp.concatenate([high, mid, low, jnp.zeros_like(value)]).astype(bf16)
+    return high, mid, value - high - mid
+
+
+def stack3(value):
+    return jnp.concatenate([*split3(value), jnp.zeros_like(value)]).astype(bf16)
 
 
 def local_kernel(kind_ref, blocks_ref, panel_ref, modes_ref,
-                 coef_ref, wall_ref, part_ref, near_ref, table_ref, wide_ref, hot_ref, plane_ref, sem):
+                 coef_ref, wall_ref, part_ref, near_ref,
+                 table_ref, wide_ref, hot_ref, text_ref, weight_ref, place_ref, matrix_ref, grid_ref, sem):
     copy = pltpu.make_async_copy(modes_ref, near_ref, sem)
     copy.start()
     table_ref[...] = jnp.zeros((NMAT, 128), f32)
+    text_ref[...] = jnp.zeros(text_ref.shape, f32)
     for i in range(3):
         for j in range(3):
             k = 3 * i + j
@@ -66,22 +71,43 @@
             table_ref[:, 7 * k : 7 * k + 7] = values
             for o in range(7):
                 column = jnp.broadcast_to(values[:, o : o + 1], (NMAT, HALF))
-                wide_ref[o, :, k * HALF : (k + 1) * HALF] = split3(column)
+                own, at = (0, o * GROUP) if o < 5 else (o - 4, 0)
+                at += j * SZ
+                text_ref[own, i, :, at : at + SZ] = column[:, :SZ]
+                if 1 <= o <= 4:
+                    wide_ref[o - 1, :, k * HALF : (k + 1) * HALF] = stack3(column)
+    row = lax.broadcasted_iota(jnp.int32, (SZ, PANEL), 0)
+    column = lax.broadcasted_iota(jnp.int32, (SZ, PANEL), 1)
+    same = column % SZ == row
+    above = (column % SZ == row + 1) & (column < GROUP)
+    below = (column % SZ == row - 1) & (column < GROUP)
+    for i in range(3):
+        for m in range(NMAT):
+            here, up, down = [jnp.broadcast_to(text_ref[own, i, m : m + 1, :], (SZ, PANEL)) for own in range(3)]
+            value = jnp.where(same, here, jnp.where(above, up, jnp.where(below, down, 0.0)))
+            for part, piece in enumerate(split3(value)):
+                weight_ref[part, i, m * SZ : (m + 1) * SZ, :] = piece.astype(bf16)
     kinds = jnp.concatenate([kind_ref[y] for y in range(SY)]).astype(f32).T
     slot = lax.broadcasted_iota(jnp.int32, (SZ, 4 * NMAT), 1)
     slot = jnp.where(slot < 3 * NMAT, slot % NMAT, -1).astype(f32)
-    none = jnp.zeros((SZ, 4 * NMAT), bf16)
+    spot = column[:, :128]
+    spot = jnp.where(spot % SZ == row[:, :128], spot // SZ, -1).astype(f32)
+    none = jnp.zeros((GROUP, PANEL), bf16)
     for n in range(CELLS):
         x, y = divmod(n, SY)
-        kind = jnp.broadcast_to(kinds[:, y * SX + x : y * SX + x + 1], (SZ, 4 * NMAT))
-        hot = jnp.where(kind == slot, 1.0, 0.0).astype(bf16)
-        outside = (False, x == SX - 1, x == 0, y == SY - 1, y == 0)
-        for o in range(5):
-            hot_ref[o, n * SZ : (n + 1) * SZ, :] = none if outside[o] else hot
-    coef_ref[...] = jnp.dot(hot_ref[0], split3(table_ref[...]), preferred_element_type=f32)
-    for o in range(7):
-        plane_ref[o] = jnp.dot(hot_ref[o if o < 5 else 0], wide_ref[o], preferred_element_type=f32)
-    whole = hot_ref[0]
+        kind = jnp.broadcast_to(kinds[:, y * SX + x : y * SX + x + 1], (SZ, 128))
+        here = slice(n * SZ, (n + 1) * SZ)
+        hot_ref[here, :] = jnp.where(kind[:, : 4 * NMAT] == slot, 1.0, 0.0).astype(bf16)
+        place_ref[here, :] = jnp.where(kind == spot, 1.0, 0.0).astype(bf16)
+        rows = [panel_ref[h, n * GROUP : (n + 1) * GROUP, :] for h in range(2)]
+        grid_ref[(x + 1) * (SY + 2) + y + 1] = jnp.concatenate(rows, axis=1).astype(bf16)
+    for y in range(SY + 2):
+        grid_ref[y] = none
+        grid_ref[(SX + 1) * (SY + 2) + y] = none
+    for x in range(1, SX + 1):
+        grid_ref[x * (SY + 2)] = none
+        grid_ref[x * (SY + 2) + SY + 1] = none
+    coef_ref[...] = jnp.dot(hot_ref[...], stack3(table_ref[...]), preferred_element_type=f32)
     walls = (
         [(SX - 1) * SY + y for y in range(SY)],
         [y for y in range(SY)],
@@ -89,44 +115,20 @@
         [x * SY for x in range(SX)],
     )
     for o, cells in enumerate(walls):
-        rows = jnp.concatenate([whole[n * SZ : (n + 1) * SZ] for n in cells])
-        wall_ref[o, : len(cells) * SZ, :] = jnp.dot(rows, wide_ref[o + 1], preferred_element_type=f32)
-    level = lax.broadcasted_iota(jnp.int32, (SZ, HALF), 0)
-    top, bottom = level == SZ - 1, level == 0
-
-    def cell(n, carry):
-        last = CELLS - 1
-        sources = (
-            (1, jnp.minimum(n + SY, last)),
-            (2, jnp.maximum(n - SY, 0)),
-            (3, jnp.minimum(n + 1, last)),
-            (4, jnp.maximum(n - 1, 0)),
-        )
-        here = pl.ds(pl.multiple_of(n * SZ, SZ), SZ)
-        total = [[jnp.zeros((SZ, HALF), f32) for _ in range(2)] for _ in range(3)]
-
-        def rows(at, j):
-            start = pl.multiple_of(at * GROUP + j * SZ, SZ)
-            return [panel_ref[h, pl.ds(start, SZ), :] for h in range(2)]
-
-        for j in range(3):
-            own = rows(n, j)
-            above = [jnp.where(top, 0.0, pltpu.roll(v, SZ - 1, 0)) for v in own]
-            below = [jnp.where(bottom, 0.0, pltpu.roll(v, 1, 0)) for v in own]
-            terms = [(0, own), (5, above), (6, below)] + [(o, rows(at, j)) for o, at in sources]
-            for o, values in terms:
-                for i in range(3):
-                    k = 3 * i + j
-                    factor = plane_ref[o, here, k * HALF : (k + 1) * HALF]
-                    for h in range(2):
-                        total[i][h] = total[i][h] + factor * values[h]
-        for i in range(3):
-            start = pl.multiple_of(n * GROUP + i * SZ, SZ)
-            for h in range(2):
-                part_ref[pl.ds(start, SZ), h * HALF : (h + 1) * HALF] = total[i][h]
-        return carry
-
-    lax.fori_loop(0, CELLS, cell, 0, unroll=2)
+        rows = jnp.concatenate([hot_ref[n * SZ : (n + 1) * SZ, :] for n in cells])
+        wall_ref[o, : len(cells) * SZ, :] = jnp.dot(rows, wide_ref[o], preferred_element_type=f32)
+    for i in range(3):
+        for part in range(3):
+            product = jnp.dot(place_ref[...], weight_ref[part, i], preferred_element_type=f32)
+            matrix_ref[part, i] = product.astype(bf16)
+    pad = jnp.zeros((SZ, PANEL), bf16)
+    for n in range(CELLS):
+        at = (n // SY + 1) * (SY + 2) + n % SY + 1
+        here = slice(n * SZ, (n + 1) * SZ)
+        left = jnp.concatenate([matrix_ref[part, i, here, :] for part in range(3) for i in range(3)])
+        right = jnp.concatenate([grid_ref[k] for k in (at, at + SY + 2, at - SY - 2, at + 1, at - 1)] + [pad])
+        out = jnp.dot(left, right, preferred_element_type=f32)
+        part_ref[n * GROUP : (n + 1) * GROUP, :] = (out[2 * GROUP :] + out[GROUP : 2 * GROUP]) + out[:GROUP]
     copy.wait()
 
 
@@ -237,9 +239,13 @@
         out_shape=[shape((CELLS * SZ, 128), f32), shape((4, SY * SZ, 9 * HALF), f32), shape((ROWS, PANEL), f32), shape((ROWS, full), bf16)],
         scratch_shapes=[
             pltpu.VMEM((NMAT, 128), f32),
-            pltpu.VMEM((7, 4 * NMAT, 9 * HALF), bf16),
-            pltpu.VMEM((5, CELLS * SZ, 4 * NMAT), bf16),
-            pltpu.VMEM((7, CELLS * SZ, 9 * HALF), f32),
+            pltpu.VMEM((4, 4 * NMAT, 9 * HALF), bf16),
+            pltpu.VMEM((CELLS * SZ, 4 * NMAT), bf16),
+            pltpu.VMEM((3, 3, NMAT, PANEL), f32),
+            pltpu.VMEM((3, 3, NMAT * SZ, PANEL), bf16),
+            pltpu.VMEM((CELLS * SZ, NMAT * SZ), bf16),
+            pltpu.VMEM((3, 3, CELLS * SZ, PANEL), bf16),
+            pltpu.VMEM(((SX + 2) * (SY + 2), GROUP, PANEL), bf16),
             pltpu.SemaphoreType.DMA,
         ],
         cost_estimate=pl.CostEstimate(flops=2 * ROWS * 21 * PANEL, bytes_accessed=3 * ROWS * PANEL, transcendentals=0),

time: 84.9 us -> 83.7 us (0.986)
  Pallas kernels: 8.44 us -> 6.44 us
  waiting for transfers between devices: 1.89 us -> 3.18 us
    pallas_call x1, Pallas kernels: 4.35 us -> 2.35 us  [shards(): pl.pallas_call(local_kernel, in_specs=[vmem] * 3 + [pl.BlockSpec(memory_s...]
    ppermute x1, waiting for transfers between devices: 0.01 us -> 1.29 us  [shards(): beside = lax.ppermute(xouter, ROW, pairs(1))]
  transfers between devices with their start and end apart: 6 -> 6, of which waited for: 1 -> 2; matrix products, arithmetic and copies ran while one was open for 0% -> 0% of each run, Pallas kernels for 5% -> 3%
where the time goes in v8:
time: 83.7 us; the launch traced here: 83.4 us
  blocking collectives  45.8 us (55%)
  starting transfers between devices  27.7 us (33%)
  Pallas kernels  6.44 us (8%)
  waiting for transfers between devices  3.18 us (4%)
    ppermute x3, starting transfers between devices, swap(): return lax.ppermute(value, axis, [(0, 1), (1, 0)])  21.3 us
    all_to_all x1, blocking collectives, shards(): lax.all_to_all(mine.reshape(2 * tiles, HALF // 2, HALF), COL + ('zl',), 0...  21.1 us
    all_to_all x1, blocking collectives, shards(): planes = lax.all_to_all(copies, Z, 0, 0, tiled=True)  16.4 us
    all_gather x1, blocking collectives, shards(): both = lax.all_gather(half, 'core', axis=0, tiled=True)  8.34 us
    ppermute x1, starting transfers between devices, shards(): yin = lax.ppermute(yinner, COL, pairs(0))  3.12 us
    ppermute x1, starting transfers between devices, shards(): beside = lax.ppermute(xouter, ROW, pairs(1))  2.54 us
    pallas_call x1, Pallas kernels, shards(): pl.pallas_call(local_kernel, in_specs=[vmem] * 3 + [pl.BlockSpec(memory_s...  2.35 us
    ppermute x3, waiting for transfers between devices, swap(): return lax.ppermute(value, axis, [(0, 1), (1, 0)])  1.88 us
  transfers between devices with their start and end apart: 6, of which 2 were waited for; matrix products, arithmetic and copies ran while one was open for 0% of the time, Pallas kernels for 3%

profile of v8, /device:TPU:1, one launch (start us, length us, event | category | flops | bytes accessed | tf_op | source)
XLA Modules:
  0.0 83.4 jit_solution(2446310805954657115)
XLA Ops:
  0.0 0.0 copy-start
  0.0 0.0 copy-start.1
  0.0 1.2 %collect_faces.1 = (f32[2,1152,128]{2,1,0:T(8,128)S(1)}, bf16[72,256]{1,0:T(8,128)(2,1)S(1)}, bf16[288,256]{1,0:T(8,128)(2,1)S(1)}, bf16[288,256]{1,0:T(8,128)(2...) custom-call(bf16[1152,2048]{1,0:T(8,128)(2,1)} %bitcast.8), custom_call_target="tpu_custom_call" | custom-call | tf_op jit(solution)/shard_map/collect_faces/pallas_call | solution.py:215
  1.3 16.3 %collective-permute-start.4 = (bf16[72,256]{1,0:T(8,128)(2,1)S(1)}, bf16[72,256]{1,0:T(8,128)(2,1)S(1)}, u32[]{:S(2)}, u32[]{:S(2)}) collective-permute-start(bf16[72,256]{1,0:T(8,128)(2,1)S(1)} %get-tuple-element.24), channel_id=1, source_target_pairs={{0,1},{1,0},{2,3},{3,2},{4,5},{5,4},{6,7},{7,6},{8,9},{9,8},{10,11... | collective-permute-start | bytes 110600 | tf_op jit(solution)/shard_map/ppermute | solution.py:206
  17.5 3.1 %collective-permute-start = (bf16[192,256]{1,0:T(8,128)(2,1)S(1)}, bf16[192,256]{1,0:T(8,128)(2,1)S(1)}, u32[]{:S(2)}, u32[]{:S(2)}) collective-permute-start(bf16[192,256]{1,0:T(8,128)(2,1)S(1)} %get-tuple-element.17), channel_id=1, source_target_pairs={{0,2},{4,6},{8,10},{12,14},{16,18},{20,22},{24,26},{28,30},{2,0},{... | collective-permute-start | bytes 294920 | tf_op jit(solution)/shard_map/ppermute | solution.py:231
  20.7 0.7 collective-permute-start.1
  21.3 3.1 %collective-permute-start.2 = (bf16[288,256]{1,0:T(8,128)(2,1)S(1)}, bf16[288,256]{1,0:T(8,128)(2,1)S(1)}, u32[]{:S(2)}, u32[]{:S(2)}) collective-permute-start(bf16[288,256]{1,0:T(8,128)(2,1)S(1)} %get-tuple-element.19), channel_id=1, source_target_pairs={{0,32},{32,0},{1,33},{33,1},{2,34},{34,2},{3,35},{35,3},{4,36},{36... | collective-permute-start | bytes 442376 | tf_op jit(solution)/shard_map/ppermute | solution.py:206
  24.5 2.5 %collective-permute-start.3 = (bf16[288,256]{1,0:T(8,128)(2,1)S(1)}, bf16[288,256]{1,0:T(8,128)(2,1)S(1)}, u32[]{:S(2)}, u32[]{:S(2)}) collective-permute-start(bf16[288,256]{1,0:T(8,128)(2,1)S(1)} %get-tuple-element.20), channel_id=1, source_target_pairs={{32,64},{96,128},{160,192},{224,256},{288,320},{352,384},{416,448}... | collective-permute-start | bytes 442376 | tf_op jit(solution)/shard_map/ppermute | solution.py:234
  27.0 0.0 copy-done
  27.0 0.0 copy-done.1
  27.0 2.4 %local_stencil.1 = (f32[384,128]{1,0:T(8,128)S(1)}, f32[4,96,1152]{2,1,0:T(8,128)S(1)}, f32[1152,256]{1,0:T(8,128)S(1)}, bf16[1152,2048]{1,0:T(8,128)(2,1)S(1)}) custom-call(s32[6,4,16]{2,1,0:T(4,128)S(1)} %bitcast.7, f32[3,3,8,7]{3,2,1,0:T(8,128)S(1)} %bitcast.6, f32[2,1152,128]{2,1,0:T(8,128)S(1)} %get-tuple-element.21.panel_ref, bf16[1152,2048]{1,0:T(8,128)(2,1)} %bitcast.9), custom_call_target="tpu_custom_call" | custom-call | flops 12386304 | bytes 884736 | tf_op jit(solution)/shard_map/local_stencil/pallas_call | solution.py:235
  29.4 0.0 collective-permute-done.4.zface_ref
  29.4 0.2 edge_terms.1.term_ref
  29.6 0.0 collective-permute-done.yin_ref
  29.6 0.0 collective-permute-done.1.yout_ref
  29.6 0.0 collective-permute-done.2.chip_ref
  29.6 1.3 %collective-permute-done.3.beside_ref = bf16[288,256]{1,0:T(8,128)(2,1)S(1)} collective-permute-done((bf16[288,256]{1,0:T(8,128)(2,1)S(1)}, bf16[288,256]{1,0:T(8,128)(2,1)S(1)}, u32[]{:S(2)}, u32[]{:S(2)}) %collective-permute-start.3) | collective-permute-done | bytes 147488 | tf_op jit(solution)/shard_map/ppermute | solution.py:234
  30.9 1.8 %faces_and_product.1 = (f32[16,128,128]{2,1,0:T(8,128)S(1)}, bf16[16,128,128]{2,1,0:T(8,128)(2,1)S(1)}) custom-call(bf16[192,256]{1,0:T(8,128)(2,1)S(1)} %collective-permute-done.yin_ref, bf16[192,256]{1,0:T(8,128)(2,1)S(1)} %collective-permute-done.1.yout_ref, bf16[288,256]{1,0:T(8,128)(2,1)S(1)} %collective-permute-done.2.chip_ref, ...), custom_call_target="tpu_custom_call" | custom-call | flops 1207959552 | bytes 4718592 | tf_op jit(solution)/shard_map/faces_and_product/pallas_call | solution.py:265
  32.7 1.9 %collective-permute-start.5 = (bf16[16,128,128]{2,1,0:T(8,128)(2,1)S(1)}, bf16[16,128,128]{2,1,0:T(8,128)(2,1)S(1)}, u32[]{:S(2)}, u32[]{:S(2)}) collective-permute-start(bf16[16,128,128]{2,1,0:T(8,128)(2,1)S(1)} %get-tuple-element.28), channel_id=1, source_target_pairs={{0,32},{32,0},{1,33},{33,1},{2,34},{34,2},{3,35},{35,3},{4,36},{36... | collective-permute-start | bytes 1572872 | tf_op jit(solution)/shard_map/ppermute | solution.py:206
  34.7 1.9 %collective-permute-done.5 = bf16[16,128,128]{2,1,0:T(8,128)(2,1)S(1)} collective-permute-done((bf16[16,128,128]{2,1,0:T(8,128)(2,1)S(1)}, bf16[16,128,128]{2,1,0:T(8,128)(2,1)S(1)}, u32[]{:S(2)}, u32[]{:S(2)}) %collective-permute-start.5) | collective-permute-done | bytes 524320 | tf_op jit(solution)/shard_map/ppermute | solution.py:206
  36.5 0.1 add_convert_fusion
  36.7 21.1 %all_to_all.10.parts_ref = bf16[32,64,128]{2,1,0:T(8,128)(2,1)S(1)} all-to-all(bf16[32,64,128]{2,1,0:T(8,128)(2,1)S(1)} %bitcast.10), channel_id=1, replica_groups=mesh['zh'=4,'zl'=2,'core'=2,'y'=4,'x'=4,'gz'=2] {'y','x','zl'}, dimensions={0} | all-to-all | bytes 1048576 | tf_op jit(solution)/shard_map/all_to_all | solution.py:276
  57.7 0.1 near_sum.1
  57.8 16.4 %all_to_all.11.planes_ref = bf16[16,64,128]{2,1,0:T(8,128)(2,1)S(1)} all-to-all(bf16[16,64,128]{2,1,0:T(8,128)(2,1)S(1)} %near_sum.1), channel_id=1, replica_groups=mesh['zh'=4,'zl'=2,'core'=2,'y'=4,'x'=4,'gz'=2] {'gz','zh','zl'}, dimensions={0} | all-to-all | bytes 524288 | tf_op jit(solution)/shard_map/all_to_all | solution.py:285
  74.3 8.3 %all_gather.3.both_ref = f32[256,128]{1,0:T(8,128)S(1)} all-gather(f32[128,128]{1,0:T(8,128)S(1)} %fold.1), channel_id=1, replica_groups=mesh['zh'=4,'zl'=2,'core'=2,'y'=4,'x'=4,'gz'=2] {'core'}, dimensions={0}, use_global_device_ids=true | all-gather | bytes 196608 | tf_op jit(solution)/shard_map/all_gather | solution.py:294
  82.6 0.8 flip.1
  (1 shorter events, 0.0 us)
Async XLA Ops:
  0.0 27.0 %copy-start = (f32[8,7,3,3]{1,0,3,2:T(8,128)S(1)}, f32[8,7,3,3]{1,0,3,2:T(8,128)}, u32[]{:S(2)}) copy-start(f32[8,7,3,3]{1,0,3,2:T(8,128)} %param.4) | copy-start | bytes 6052
  0.0 27.0 %copy-start.1 = (s32[4,6,16]{2,0,1:T(4,128)S(1)}, s32[4,6,16]{2,0,1:T(4,128)}, u32[]{:S(2)}) copy-start(s32[4,6,16]{2,0,1:T(4,128)} %param.5) | copy-start | bytes 4612
  1.3 28.2 %collective-permute-start.4 = (bf16[72,256]{1,0:T(8,128)(2,1)S(1)}, bf16[72,256]{1,0:T(8,128)(2,1)S(1)}, u32[]{:S(2)}, u32[]{:S(2)}) collective-permute-start(bf16[72,256]{1,0:T(8,128)(2,1)S(1)} %get-tuple-element.24), channel_id=1, source_target_pairs={{0,1},{1,0},{2,3},{3,2},{4,5},{5,4},{6,7},{7,6},{8,9},{9,8},{10,11... | collective-permute-start | bytes 110600 | tf_op jit(solution)/shard_map/ppermute | solution.py:206
  17.5 12.1 %collective-permute-start = (bf16[192,256]{1,0:T(8,128)(2,1)S(1)}, bf16[192,256]{1,0:T(8,128)(2,1)S(1)}, u32[]{:S(2)}, u32[]{:S(2)}) collective-permute-start(bf16[192,256]{1,0:T(8,128)(2,1)S(1)} %get-tuple-element.17), channel_id=1, source_target_pairs={{0,2},{4,6},{8,10},{12,14},{16,18},{20,22},{24,26},{28,30},{2,0},{... | collective-permute-start | bytes 294920 | tf_op jit(solution)/shard_map/ppermute | solution.py:231
  20.7 9.0 %collective-permute-start.1 = (bf16[192,256]{1,0:T(8,128)(2,1)S(1)}, bf16[192,256]{1,0:T(8,128)(2,1)S(1)}, u32[]{:S(2)}, u32[]{:S(2)}) collective-permute-start(bf16[192,256]{1,0:T(8,128)(2,1)S(1)} %get-tuple-element.18), channel_id=1, source_target_pairs={{2,4},{6,8},{10,12},{14,16},{18,20},{22,24},{26,28},{4,2},{8,6},{1... | collective-permute-start | bytes 294920 | tf_op jit(solution)/shard_map/ppermute | solution.py:232
  21.3 8.3 %collective-permute-start.2 = (bf16[288,256]{1,0:T(8,128)(2,1)S(1)}, bf16[288,256]{1,0:T(8,128)(2,1)S(1)}, u32[]{:S(2)}, u32[]{:S(2)}) collective-permute-start(bf16[288,256]{1,0:T(8,128)(2,1)S(1)} %get-tuple-element.19), channel_id=1, source_target_pairs={{0,32},{32,0},{1,33},{33,1},{2,34},{34,2},{3,35},{35,3},{4,36},{36... | collective-permute-start | bytes 442376 | tf_op jit(solution)/shard_map/ppermute | solution.py:206
  24.5 6.5 %collective-permute-start.3 = (bf16[288,256]{1,0:T(8,128)(2,1)S(1)}, bf16[288,256]{1,0:T(8,128)(2,1)S(1)}, u32[]{:S(2)}, u32[]{:S(2)}) collective-permute-start(bf16[288,256]{1,0:T(8,128)(2,1)S(1)} %get-tuple-element.20), channel_id=1, source_target_pairs={{32,64},{96,128},{160,192},{224,256},{288,320},{352,384},{416,448}... | collective-permute-start | bytes 442376 | tf_op jit(solution)/shard_map/ppermute | solution.py:234
  32.7 3.8 %collective-permute-start.5 = (bf16[16,128,128]{2,1,0:T(8,128)(2,1)S(1)}, bf16[16,128,128]{2,1,0:T(8,128)(2,1)S(1)}, u32[]{:S(2)}, u32[]{:S(2)}) collective-permute-start(bf16[16,128,128]{2,1,0:T(8,128)(2,1)S(1)} %get-tuple-element.28), channel_id=1, source_target_pairs={{0,32},{32,0},{1,33},{33,1},{2,34},{34,2},{3,35},{35,3},{4,36},{36... | collective-permute-start | bytes 1572872 | tf_op jit(solution)/shard_map/ppermute | solution.py:206

commit v9 on v8

--- a/solution.py
+++ b/solution.py
@@ -143,7 +143,7 @@
         term_ref[i * CELLS : (i + 1) * CELLS, :] = total
 
 
-def product_kernel(yin_ref, yout_ref, chip_ref, beside_ref, wall_ref, part_ref, term_ref, modes_ref,
+def product_kernel(yin_ref, yout_ref, beside_ref, chip_ref, wall_ref, part_ref, term_ref, modes_ref,
                    keep_ref, send_ref, stiff_ref, left_ref):
     core, gz = lax.axis_index("core"), lax.axis_index(GZ)
     level = lax.broadcasted_iota(jnp.int32, (SZ, PANEL), 0)
@@ -230,8 +230,8 @@
 
     yin = lax.ppermute(yinner, COL, pairs(0))
     yout = lax.ppermute(youter, COL, pairs(1))
+    beside = lax.ppermute(xouter, ROW, pairs(1))
     chip = swap(xinner, "core")
-    beside = lax.ppermute(xouter, ROW, pairs(1))
     coef, wall, part, near = pl.pallas_call(
         local_kernel,
         in_specs=[vmem] * 3 + [pl.BlockSpec(memory_space=pl.ANY)],
@@ -271,7 +271,7 @@
         cost_estimate=pl.CostEstimate(flops=2 * ROWS * full * PANEL, bytes_accessed=2 * ROWS * full, transcendentals=0),
         compiler_params=pltpu.CompilerParams(vmem_limit_bytes=32 << 20),
         name="faces_and_product",
-    )(yin, yout, chip, beside, wall, part, term, near)
+    )(yin, yout, beside, chip, wall, part, term, near)
     mine = (keep + swap(send, "core").astype(f32)).astype(bf16)
     parts = lax.all_to_all(mine.reshape(2 * tiles, HALF // 2, HALF), COL + ("zl",), 0, 0, tiled=True)
     copies = pl.pallas_call(

time: 83.7 us -> 82.5 us (0.986)
  waiting for transfers between devices: 3.18 us -> 1.53 us
    ppermute x1, waiting for transfers between devices: 1.29 us -> 0.01 us  [shards(): beside = lax.ppermute(xouter, ROW, pairs(1))]
    ppermute x1, starting transfers between devices: 2.54 us -> 3.77 us  [shards(): beside = lax.ppermute(xouter, ROW, pairs(1))]
  transfers between devices with their start and end apart: 6 -> 6, of which waited for: 2 -> 1; matrix products, arithmetic and copies ran while one was open for 0% -> 0% of each run, Pallas kernels for 3% -> 3%
where the time goes in v9:
time: 82.5 us; the launch traced here: 82.1 us
  blocking collectives  45.7 us (55%)
  starting transfers between devices  28.1 us (34%)
  Pallas kernels  6.45 us (8%)
  waiting for transfers between devices  1.53 us (2%)
    all_to_all x1, blocking collectives, shards(): lax.all_to_all(mine.reshape(2 * tiles, HALF // 2, HALF), COL + ('zl',), 0...  20.9 us
    ppermute x3, starting transfers between devices, swap(): return lax.ppermute(value, axis, [(0, 1), (1, 0)])  20.6 us
    all_to_all x1, blocking collectives, shards(): planes = lax.all_to_all(copies, Z, 0, 0, tiled=True)  16.5 us
    all_gather x1, blocking collectives, shards(): both = lax.all_gather(half, 'core', axis=0, tiled=True)  8.34 us
    ppermute x1, starting transfers between devices, shards(): beside = lax.ppermute(xouter, ROW, pairs(1))  3.77 us
    ppermute x1, starting transfers between devices, shards(): yin = lax.ppermute(yinner, COL, pairs(0))  3.12 us
    pallas_call x1, Pallas kernels, shards(): pl.pallas_call(local_kernel, in_specs=[vmem] * 3 + [pl.BlockSpec(memory_s...  2.35 us
    pallas_call x1, Pallas kernels, shards(): pl.pallas_call(product_kernel, in_specs=[vmem] * 8, out_specs=[vmem] * 2,...  1.79 us
  transfers between devices with their start and end apart: 6, of which 1 were waited for; matrix products, arithmetic and copies ran while one was open for 0% of the time, Pallas kernels for 3%

profile of v9, /device:TPU:1, one launch (start us, length us, event | category | flops | bytes accessed | tf_op | source)
XLA Modules:
  0.0 82.1 jit_solution(7417693939445128549)
XLA Ops:
  0.0 0.0 copy-start
  0.0 0.0 copy-start.1
  0.0 1.2 %collect_faces.1 = (f32[2,1152,128]{2,1,0:T(8,128)S(1)}, bf16[72,256]{1,0:T(8,128)(2,1)S(1)}, bf16[288,256]{1,0:T(8,128)(2,1)S(1)}, bf16[288,256]{1,0:T(8,128)(2...) custom-call(bf16[1152,2048]{1,0:T(8,128)(2,1)} %bitcast.8), custom_call_target="tpu_custom_call" | custom-call | tf_op jit(solution)/shard_map/collect_faces/pallas_call | solution.py:215
  1.3 16.3 %collective-permute-start.4 = (bf16[72,256]{1,0:T(8,128)(2,1)S(1)}, bf16[72,256]{1,0:T(8,128)(2,1)S(1)}, u32[]{:S(2)}, u32[]{:S(2)}) collective-permute-start(bf16[72,256]{1,0:T(8,128)(2,1)S(1)} %get-tuple-element.24), channel_id=1, source_target_pairs={{0,1},{1,0},{2,3},{3,2},{4,5},{5,4},{6,7},{7,6},{8,9},{9,8},{10,11... | collective-permute-start | bytes 110600 | tf_op jit(solution)/shard_map/ppermute | solution.py:206
  17.5 3.1 %collective-permute-start = (bf16[192,256]{1,0:T(8,128)(2,1)S(1)}, bf16[192,256]{1,0:T(8,128)(2,1)S(1)}, u32[]{:S(2)}, u32[]{:S(2)}) collective-permute-start(bf16[192,256]{1,0:T(8,128)(2,1)S(1)} %get-tuple-element.17), channel_id=1, source_target_pairs={{0,2},{4,6},{8,10},{12,14},{16,18},{20,22},{24,26},{28,30},{2,0},{... | collective-permute-start | bytes 294920 | tf_op jit(solution)/shard_map/ppermute | solution.py:231
  20.7 0.7 collective-permute-start.1
  21.3 3.8 %collective-permute-start.2 = (bf16[288,256]{1,0:T(8,128)(2,1)S(1)}, bf16[288,256]{1,0:T(8,128)(2,1)S(1)}, u32[]{:S(2)}, u32[]{:S(2)}) collective-permute-start(bf16[288,256]{1,0:T(8,128)(2,1)S(1)} %get-tuple-element.19), channel_id=1, source_target_pairs={{32,64},{96,128},{160,192},{224,256},{288,320},{352,384},{416,448}... | collective-permute-start | bytes 442376 | tf_op jit(solution)/shard_map/ppermute | solution.py:233
  25.1 1.9 %collective-permute-start.3 = (bf16[288,256]{1,0:T(8,128)(2,1)S(1)}, bf16[288,256]{1,0:T(8,128)(2,1)S(1)}, u32[]{:S(2)}, u32[]{:S(2)}) collective-permute-start(bf16[288,256]{1,0:T(8,128)(2,1)S(1)} %get-tuple-element.20), channel_id=1, source_target_pairs={{0,32},{32,0},{1,33},{33,1},{2,34},{34,2},{3,35},{35,3},{4,36},{36... | collective-permute-start | bytes 442376 | tf_op jit(solution)/shard_map/ppermute | solution.py:206
  27.0 0.0 copy-done
  27.0 0.0 copy-done.1
  27.0 2.4 %local_stencil.1 = (f32[384,128]{1,0:T(8,128)S(1)}, f32[4,96,1152]{2,1,0:T(8,128)S(1)}, f32[1152,256]{1,0:T(8,128)S(1)}, bf16[1152,2048]{1,0:T(8,128)(2,1)S(1)}) custom-call(s32[6,4,16]{2,1,0:T(4,128)S(1)} %bitcast.7, f32[3,3,8,7]{3,2,1,0:T(8,128)S(1)} %bitcast.6, f32[2,1152,128]{2,1,0:T(8,128)S(1)} %get-tuple-element.21.panel_ref, bf16[1152,2048]{1,0:T(8,128)(2,1)} %bitcast.9), custom_call_target="tpu_custom_call" | custom-call | flops 12386304 | bytes 884736 | tf_op jit(solution)/shard_map/local_stencil/pallas_call | solution.py:235
  29.4 0.0 collective-permute-done.4.zface_ref
  29.4 0.2 edge_terms.1.term_ref
  29.6 0.0 collective-permute-done.yin_ref
  29.6 0.0 collective-permute-done.1.yout_ref
  29.6 0.0 collective-permute-done.2.beside_ref
  29.6 0.0 collective-permute-done.3.chip_ref
  29.7 1.8 %faces_and_product.1 = (f32[16,128,128]{2,1,0:T(8,128)S(1)}, bf16[16,128,128]{2,1,0:T(8,128)(2,1)S(1)}) custom-call(bf16[192,256]{1,0:T(8,128)(2,1)S(1)} %collective-permute-done.yin_ref, bf16[192,256]{1,0:T(8,128)(2,1)S(1)} %collective-permute-done.1.yout_ref, bf16[288,256]{1,0:T(8,128)(2,1)S(1)} %collective-permute-done.2.beside_ref, ...), custom_call_target="tpu_custom_call" | custom-call | flops 1207959552 | bytes 4718592 | tf_op jit(solution)/shard_map/faces_and_product/pallas_call | solution.py:265
  31.5 2.4 %collective-permute-start.5 = (bf16[16,128,128]{2,1,0:T(8,128)(2,1)S(1)}, bf16[16,128,128]{2,1,0:T(8,128)(2,1)S(1)}, u32[]{:S(2)}, u32[]{:S(2)}) collective-permute-start(bf16[16,128,128]{2,1,0:T(8,128)(2,1)S(1)} %get-tuple-element.28), channel_id=1, source_target_pairs={{0,32},{32,0},{1,33},{33,1},{2,34},{34,2},{3,35},{35,3},{4,36},{36... | collective-permute-start | bytes 1572872 | tf_op jit(solution)/shard_map/ppermute | solution.py:206
  33.9 1.5 %collective-permute-done.5 = bf16[16,128,128]{2,1,0:T(8,128)(2,1)S(1)} collective-permute-done((bf16[16,128,128]{2,1,0:T(8,128)(2,1)S(1)}, bf16[16,128,128]{2,1,0:T(8,128)(2,1)S(1)}, u32[]{:S(2)}, u32[]{:S(2)}) %collective-permute-start.5) | collective-permute-done | bytes 524320 | tf_op jit(solution)/shard_map/ppermute | solution.py:206
  35.4 0.1 add_convert_fusion
  35.5 20.9 %all_to_all.10.parts_ref = bf16[32,64,128]{2,1,0:T(8,128)(2,1)S(1)} all-to-all(bf16[32,64,128]{2,1,0:T(8,128)(2,1)S(1)} %bitcast.10), channel_id=1, replica_groups=mesh['zh'=4,'zl'=2,'core'=2,'y'=4,'x'=4,'gz'=2] {'y','x','zl'}, dimensions={0} | all-to-all | bytes 1048576 | tf_op jit(solution)/shard_map/all_to_all | solution.py:276
  56.4 0.1 near_sum.1
  56.5 16.5 %all_to_all.11.planes_ref = bf16[16,64,128]{2,1,0:T(8,128)(2,1)S(1)} all-to-all(bf16[16,64,128]{2,1,0:T(8,128)(2,1)S(1)} %near_sum.1), channel_id=1, replica_groups=mesh['zh'=4,'zl'=2,'core'=2,'y'=4,'x'=4,'gz'=2] {'gz','zh','zl'}, dimensions={0} | all-to-all | bytes 524288 | tf_op jit(solution)/shard_map/all_to_all | solution.py:285
  73.0 8.3 %all_gather.3.both_ref = f32[256,128]{1,0:T(8,128)S(1)} all-gather(f32[128,128]{1,0:T(8,128)S(1)} %fold.1), channel_id=1, replica_groups=mesh['zh'=4,'zl'=2,'core'=2,'y'=4,'x'=4,'gz'=2] {'core'}, dimensions={0}, use_global_device_ids=true | all-gather | bytes 196608 | tf_op jit(solution)/shard_map/all_gather | solution.py:294
  81.4 0.8 flip.1
  (1 shorter events, 0.0 us)
Async XLA Ops:
  0.0 27.0 %copy-start = (f32[8,7,3,3]{1,0,3,2:T(8,128)S(1)}, f32[8,7,3,3]{1,0,3,2:T(8,128)}, u32[]{:S(2)}) copy-start(f32[8,7,3,3]{1,0,3,2:T(8,128)} %param.4) | copy-start | bytes 6052
  0.0 27.0 %copy-start.1 = (s32[4,6,16]{2,0,1:T(4,128)S(1)}, s32[4,6,16]{2,0,1:T(4,128)}, u32[]{:S(2)}) copy-start(s32[4,6,16]{2,0,1:T(4,128)} %param.5) | copy-start | bytes 4612
  1.3 28.2 %collective-permute-start.4 = (bf16[72,256]{1,0:T(8,128)(2,1)S(1)}, bf16[72,256]{1,0:T(8,128)(2,1)S(1)}, u32[]{:S(2)}, u32[]{:S(2)}) collective-permute-start(bf16[72,256]{1,0:T(8,128)(2,1)S(1)} %get-tuple-element.24), channel_id=1, source_target_pairs={{0,1},{1,0},{2,3},{3,2},{4,5},{5,4},{6,7},{7,6},{8,9},{9,8},{10,11... | collective-permute-start | bytes 110600 | tf_op jit(solution)/shard_map/ppermute | solution.py:206
  17.5 12.1 %collective-permute-start = (bf16[192,256]{1,0:T(8,128)(2,1)S(1)}, bf16[192,256]{1,0:T(8,128)(2,1)S(1)}, u32[]{:S(2)}, u32[]{:S(2)}) collective-permute-start(bf16[192,256]{1,0:T(8,128)(2,1)S(1)} %get-tuple-element.17), channel_id=1, source_target_pairs={{0,2},{4,6},{8,10},{12,14},{16,18},{20,22},{24,26},{28,30},{2,0},{... | collective-permute-start | bytes 294920 | tf_op jit(solution)/shard_map/ppermute | solution.py:231
  20.7 9.0 %collective-permute-start.1 = (bf16[192,256]{1,0:T(8,128)(2,1)S(1)}, bf16[192,256]{1,0:T(8,128)(2,1)S(1)}, u32[]{:S(2)}, u32[]{:S(2)}) collective-permute-start(bf16[192,256]{1,0:T(8,128)(2,1)S(1)} %get-tuple-element.18), channel_id=1, source_target_pairs={{2,4},{6,8},{10,12},{14,16},{18,20},{22,24},{26,28},{4,2},{8,6},{1... | collective-permute-start | bytes 294920 | tf_op jit(solution)/shard_map/ppermute | solution.py:232
  21.3 8.3 %collective-permute-start.2 = (bf16[288,256]{1,0:T(8,128)(2,1)S(1)}, bf16[288,256]{1,0:T(8,128)(2,1)S(1)}, u32[]{:S(2)}, u32[]{:S(2)}) collective-permute-start(bf16[288,256]{1,0:T(8,128)(2,1)S(1)} %get-tuple-element.19), channel_id=1, source_target_pairs={{32,64},{96,128},{160,192},{224,256},{288,320},{352,384},{416,448}... | collective-permute-start | bytes 442376 | tf_op jit(solution)/shard_map/ppermute | solution.py:233
  25.1 4.5 %collective-permute-start.3 = (bf16[288,256]{1,0:T(8,128)(2,1)S(1)}, bf16[288,256]{1,0:T(8,128)(2,1)S(1)}, u32[]{:S(2)}, u32[]{:S(2)}) collective-permute-start(bf16[288,256]{1,0:T(8,128)(2,1)S(1)} %get-tuple-element.20), channel_id=1, source_target_pairs={{0,32},{32,0},{1,33},{33,1},{2,34},{34,2},{3,35},{35,3},{4,36},{36... | collective-permute-start | bytes 442376 | tf_op jit(solution)/shard_map/ppermute | solution.py:206
  31.5 3.9 %collective-permute-start.5 = (bf16[16,128,128]{2,1,0:T(8,128)(2,1)S(1)}, bf16[16,128,128]{2,1,0:T(8,128)(2,1)S(1)}, u32[]{:S(2)}, u32[]{:S(2)}) collective-permute-start(bf16[16,128,128]{2,1,0:T(8,128)(2,1)S(1)} %get-tuple-element.28), channel_id=1, source_target_pairs={{0,32},{32,0},{1,33},{33,1},{2,34},{34,2},{3,35},{35,3},{4,36},{36... | collective-permute-start | bytes 1572872 | tf_op jit(solution)/shard_map/ppermute | solution.py:206

commit v10 on v9

--- a/solution.py
+++ b/solution.py
@@ -143,7 +143,7 @@
         term_ref[i * CELLS : (i + 1) * CELLS, :] = total
 
 
-def product_kernel(yin_ref, yout_ref, beside_ref, chip_ref, wall_ref, part_ref, term_ref, modes_ref,
+def product_kernel(yout_ref, yin_ref, beside_ref, chip_ref, wall_ref, part_ref, term_ref, modes_ref,
                    keep_ref, send_ref, stiff_ref, left_ref):
     core, gz = lax.axis_index("core"), lax.axis_index(GZ)
     level = lax.broadcasted_iota(jnp.int32, (SZ, PANEL), 0)
@@ -271,7 +271,7 @@
         cost_estimate=pl.CostEstimate(flops=2 * ROWS * full * PANEL, bytes_accessed=2 * ROWS * full, transcendentals=0),
         compiler_params=pltpu.CompilerParams(vmem_limit_bytes=32 << 20),
         name="faces_and_product",
-    )(yin, yout, beside, chip, wall, part, term, near)
+    )(yout, yin, beside, chip, wall, part, term, near)
     mine = (keep + swap(send, "core").astype(f32)).astype(bf16)
     parts = lax.all_to_all(mine.reshape(2 * tiles, HALF // 2, HALF), COL + ("zl",), 0, 0, tiled=True)
     copies = pl.pallas_call(

time: 82.5 us -> 82.4 us (level)
  blocking collectives: 45.7 us -> 42.9 us
  starting transfers between devices: 28.1 us -> 30.9 us
    all_to_all x1, blocking collectives: 20.9 us -> 18.1 us  [shards(): lax.all_to_all(mine.reshape(2 * tiles, HALF // 2, HALF), COL + ('zl',), 0...]
    ppermute x1, starting transfers between devices: 3.12 us -> 5.57 us  [shards(): yin = lax.ppermute(yinner, COL, pairs(0))]
where the time goes in v10:
time: 82.4 us; the launch traced here: 82.1 us
  blocking collectives  42.9 us (52%)
  starting transfers between devices  30.9 us (38%)
  Pallas kernels  6.45 us (8%)
  waiting for transfers between devices  1.53 us (2%)
    ppermute x3, starting transfers between devices, swap(): return lax.ppermute(value, axis, [(0, 1), (1, 0)])  20.6 us
    all_to_all x1, blocking collectives, shards(): lax.all_to_all(mine.reshape(2 * tiles, HALF // 2, HALF), COL + ('zl',), 0...  18.1 us
    all_to_all x1, blocking collectives, shards(): planes = lax.all_to_all(copies, Z, 0, 0, tiled=True)  16.5 us
    all_gather x1, blocking collectives, shards(): both = lax.all_gather(half, 'core', axis=0, tiled=True)  8.34 us
    ppermute x1, starting transfers between devices, shards(): yin = lax.ppermute(yinner, COL, pairs(0))  5.57 us
    ppermute x1, starting transfers between devices, shards(): beside = lax.ppermute(xouter, ROW, pairs(1))  4.05 us
    pallas_call x1, Pallas kernels, shards(): pl.pallas_call(local_kernel, in_specs=[vmem] * 3 + [pl.BlockSpec(memory_s...  2.35 us
    pallas_call x1, Pallas kernels, shards(): pl.pallas_call(product_kernel, in_specs=[vmem] * 8, out_specs=[vmem] * 2,...  1.78 us
  transfers between devices with their start and end apart: 6, of which 1 were waited for; matrix products, arithmetic and copies ran while one was open for 0% of the time, Pallas kernels for 3%

profile of v10, /device:TPU:1, one launch (start us, length us, event | category | flops | bytes accessed | tf_op | source)
XLA Modules:
  0.0 82.1 jit_solution(18342572319752169287)
XLA Ops:
  0.0 0.0 copy-start
  0.0 0.0 copy-start.1
  0.0 1.2 %collect_faces.1 = (f32[2,1152,128]{2,1,0:T(8,128)S(1)}, bf16[72,256]{1,0:T(8,128)(2,1)S(1)}, bf16[288,256]{1,0:T(8,128)(2,1)S(1)}, bf16[288,256]{1,0:T(8,128)(2...) custom-call(bf16[1152,2048]{1,0:T(8,128)(2,1)} %bitcast.8), custom_call_target="tpu_custom_call" | custom-call | tf_op jit(solution)/shard_map/collect_faces/pallas_call | solution.py:215
  1.3 16.3 %collective-permute-start.4 = (bf16[72,256]{1,0:T(8,128)(2,1)S(1)}, bf16[72,256]{1,0:T(8,128)(2,1)S(1)}, u32[]{:S(2)}, u32[]{:S(2)}) collective-permute-start(bf16[72,256]{1,0:T(8,128)(2,1)S(1)} %get-tuple-element.24), channel_id=1, source_target_pairs={{0,1},{1,0},{2,3},{3,2},{4,5},{5,4},{6,7},{7,6},{8,9},{9,8},{10,11... | collective-permute-start | bytes 110600 | tf_op jit(solution)/shard_map/ppermute | solution.py:206
  17.5 0.7 collective-permute-start
  18.2 5.6 %collective-permute-start.1 = (bf16[192,256]{1,0:T(8,128)(2,1)S(1)}, bf16[192,256]{1,0:T(8,128)(2,1)S(1)}, u32[]{:S(2)}, u32[]{:S(2)}) collective-permute-start(bf16[192,256]{1,0:T(8,128)(2,1)S(1)} %get-tuple-element.18), channel_id=1, source_target_pairs={{0,2},{4,6},{8,10},{12,14},{16,18},{20,22},{24,26},{28,30},{2,0},{... | collective-permute-start | bytes 294920 | tf_op jit(solution)/shard_map/ppermute | solution.py:231
  23.8 4.0 %collective-permute-start.2 = (bf16[288,256]{1,0:T(8,128)(2,1)S(1)}, bf16[288,256]{1,0:T(8,128)(2,1)S(1)}, u32[]{:S(2)}, u32[]{:S(2)}) collective-permute-start(bf16[288,256]{1,0:T(8,128)(2,1)S(1)} %get-tuple-element.19), channel_id=1, source_target_pairs={{32,64},{96,128},{160,192},{224,256},{288,320},{352,384},{416,448}... | collective-permute-start | bytes 442376 | tf_op jit(solution)/shard_map/ppermute | solution.py:233
  27.8 1.9 %collective-permute-start.3 = (bf16[288,256]{1,0:T(8,128)(2,1)S(1)}, bf16[288,256]{1,0:T(8,128)(2,1)S(1)}, u32[]{:S(2)}, u32[]{:S(2)}) collective-permute-start(bf16[288,256]{1,0:T(8,128)(2,1)S(1)} %get-tuple-element.20), channel_id=1, source_target_pairs={{0,32},{32,0},{1,33},{33,1},{2,34},{34,2},{3,35},{35,3},{4,36},{36... | collective-permute-start | bytes 442376 | tf_op jit(solution)/shard_map/ppermute | solution.py:206
  29.8 0.0 copy-done
  29.8 0.0 copy-done.1
  29.8 2.4 %local_stencil.1 = (f32[384,128]{1,0:T(8,128)S(1)}, f32[4,96,1152]{2,1,0:T(8,128)S(1)}, f32[1152,256]{1,0:T(8,128)S(1)}, bf16[1152,2048]{1,0:T(8,128)(2,1)S(1)}) custom-call(s32[6,4,16]{2,1,0:T(4,128)S(1)} %bitcast.7, f32[3,3,8,7]{3,2,1,0:T(8,128)S(1)} %bitcast.6, f32[2,1152,128]{2,1,0:T(8,128)S(1)} %get-tuple-element.21.panel_ref, bf16[1152,2048]{1,0:T(8,128)(2,1)} %bitcast.9), custom_call_target="tpu_custom_call" | custom-call | flops 12386304 | bytes 884736 | tf_op jit(solution)/shard_map/local_stencil/pallas_call | solution.py:235
  32.1 0.0 collective-permute-done.4.zface_ref
  32.2 0.2 edge_terms.1.term_ref
  32.3 0.0 collective-permute-done.yout_ref
  32.4 0.0 collective-permute-done.1.yin_ref
  32.4 0.0 collective-permute-done.2.beside_ref
  32.4 0.0 collective-permute-done.3.chip_ref
  32.4 1.8 %faces_and_product.1 = (f32[16,128,128]{2,1,0:T(8,128)S(1)}, bf16[16,128,128]{2,1,0:T(8,128)(2,1)S(1)}) custom-call(bf16[192,256]{1,0:T(8,128)(2,1)S(1)} %collective-permute-done.yout_ref, bf16[192,256]{1,0:T(8,128)(2,1)S(1)} %collective-permute-done.1.yin_ref, bf16[288,256]{1,0:T(8,128)(2,1)S(1)} %collective-permute-done.2.beside_ref, ...), custom_call_target="tpu_custom_call" | custom-call | flops 1207959552 | bytes 4718592 | tf_op jit(solution)/shard_map/faces_and_product/pallas_call | solution.py:265
  34.2 2.4 %collective-permute-start.5 = (bf16[16,128,128]{2,1,0:T(8,128)(2,1)S(1)}, bf16[16,128,128]{2,1,0:T(8,128)(2,1)S(1)}, u32[]{:S(2)}, u32[]{:S(2)}) collective-permute-start(bf16[16,128,128]{2,1,0:T(8,128)(2,1)S(1)} %get-tuple-element.28), channel_id=1, source_target_pairs={{0,32},{32,0},{1,33},{33,1},{2,34},{34,2},{3,35},{35,3},{4,36},{36... | collective-permute-start | bytes 1572872 | tf_op jit(solution)/shard_map/ppermute | solution.py:206
  36.6 1.5 %collective-permute-done.5 = bf16[16,128,128]{2,1,0:T(8,128)(2,1)S(1)} collective-permute-done((bf16[16,128,128]{2,1,0:T(8,128)(2,1)S(1)}, bf16[16,128,128]{2,1,0:T(8,128)(2,1)S(1)}, u32[]{:S(2)}, u32[]{:S(2)}) %collective-permute-start.5) | collective-permute-done | bytes 524320 | tf_op jit(solution)/shard_map/ppermute | solution.py:206
  38.1 0.1 add_convert_fusion
  38.2 18.1 %all_to_all.10.parts_ref = bf16[32,64,128]{2,1,0:T(8,128)(2,1)S(1)} all-to-all(bf16[32,64,128]{2,1,0:T(8,128)(2,1)S(1)} %bitcast.10), channel_id=1, replica_groups=mesh['zh'=4,'zl'=2,'core'=2,'y'=4,'x'=4,'gz'=2] {'y','x','zl'}, dimensions={0} | all-to-all | bytes 1048576 | tf_op jit(solution)/shard_map/all_to_all | solution.py:276
  56.3 0.1 near_sum.1
  56.4 16.5 %all_to_all.11.planes_ref = bf16[16,64,128]{2,1,0:T(8,128)(2,1)S(1)} all-to-all(bf16[16,64,128]{2,1,0:T(8,128)(2,1)S(1)} %near_sum.1), channel_id=1, replica_groups=mesh['zh'=4,'zl'=2,'core'=2,'y'=4,'x'=4,'gz'=2] {'gz','zh','zl'}, dimensions={0} | all-to-all | bytes 524288 | tf_op jit(solution)/shard_map/all_to_all | solution.py:285
  73.0 8.3 %all_gather.3.both_ref = f32[256,128]{1,0:T(8,128)S(1)} all-gather(f32[128,128]{1,0:T(8,128)S(1)} %fold.1), channel_id=1, replica_groups=mesh['zh'=4,'zl'=2,'core'=2,'y'=4,'x'=4,'gz'=2] {'core'}, dimensions={0}, use_global_device_ids=true | all-gather | bytes 196608 | tf_op jit(solution)/shard_map/all_gather | solution.py:294
  81.3 0.8 flip.1
  (1 shorter events, 0.0 us)
Async XLA Ops:
  0.0 29.8 %copy-start = (f32[8,7,3,3]{1,0,3,2:T(8,128)S(1)}, f32[8,7,3,3]{1,0,3,2:T(8,128)}, u32[]{:S(2)}) copy-start(f32[8,7,3,3]{1,0,3,2:T(8,128)} %param.4) | copy-start | bytes 6052
  0.0 29.8 %copy-start.1 = (s32[4,6,16]{2,0,1:T(4,128)S(1)}, s32[4,6,16]{2,0,1:T(4,128)}, u32[]{:S(2)}) copy-start(s32[4,6,16]{2,0,1:T(4,128)} %param.5) | copy-start | bytes 4612
  1.3 30.9 %collective-permute-start.4 = (bf16[72,256]{1,0:T(8,128)(2,1)S(1)}, bf16[72,256]{1,0:T(8,128)(2,1)S(1)}, u32[]{:S(2)}, u32[]{:S(2)}) collective-permute-start(bf16[72,256]{1,0:T(8,128)(2,1)S(1)} %get-tuple-element.24), channel_id=1, source_target_pairs={{0,1},{1,0},{2,3},{3,2},{4,5},{5,4},{6,7},{7,6},{8,9},{9,8},{10,11... | collective-permute-start | bytes 110600 | tf_op jit(solution)/shard_map/ppermute | solution.py:206
  17.5 14.8 %collective-permute-start = (bf16[192,256]{1,0:T(8,128)(2,1)S(1)}, bf16[192,256]{1,0:T(8,128)(2,1)S(1)}, u32[]{:S(2)}, u32[]{:S(2)}) collective-permute-start(bf16[192,256]{1,0:T(8,128)(2,1)S(1)} %get-tuple-element.17), channel_id=1, source_target_pairs={{2,4},{6,8},{10,12},{14,16},{18,20},{22,24},{26,28},{4,2},{8,6},{1... | collective-permute-start | bytes 294920 | tf_op jit(solution)/shard_map/ppermute | solution.py:232
  18.2 14.2 %collective-permute-start.1 = (bf16[192,256]{1,0:T(8,128)(2,1)S(1)}, bf16[192,256]{1,0:T(8,128)(2,1)S(1)}, u32[]{:S(2)}, u32[]{:S(2)}) collective-permute-start(bf16[192,256]{1,0:T(8,128)(2,1)S(1)} %get-tuple-element.18), channel_id=1, source_target_pairs={{0,2},{4,6},{8,10},{12,14},{16,18},{20,22},{24,26},{28,30},{2,0},{... | collective-permute-start | bytes 294920 | tf_op jit(solution)/shard_map/ppermute | solution.py:231
  23.8 8.6 %collective-permute-start.2 = (bf16[288,256]{1,0:T(8,128)(2,1)S(1)}, bf16[288,256]{1,0:T(8,128)(2,1)S(1)}, u32[]{:S(2)}, u32[]{:S(2)}) collective-permute-start(bf16[288,256]{1,0:T(8,128)(2,1)S(1)} %get-tuple-element.19), channel_id=1, source_target_pairs={{32,64},{96,128},{160,192},{224,256},{288,320},{352,384},{416,448}... | collective-permute-start | bytes 442376 | tf_op jit(solution)/shard_map/ppermute | solution.py:233
  27.8 4.5 %collective-permute-start.3 = (bf16[288,256]{1,0:T(8,128)(2,1)S(1)}, bf16[288,256]{1,0:T(8,128)(2,1)S(1)}, u32[]{:S(2)}, u32[]{:S(2)}) collective-permute-start(bf16[288,256]{1,0:T(8,128)(2,1)S(1)} %get-tuple-element.20), channel_id=1, source_target_pairs={{0,32},{32,0},{1,33},{33,1},{2,34},{34,2},{3,35},{35,3},{4,36},{36... | collective-permute-start | bytes 442376 | tf_op jit(solution)/shard_map/ppermute | solution.py:206
  34.2 3.9 %collective-permute-start.5 = (bf16[16,128,128]{2,1,0:T(8,128)(2,1)S(1)}, bf16[16,128,128]{2,1,0:T(8,128)(2,1)S(1)}, u32[]{:S(2)}, u32[]{:S(2)}) collective-permute-start(bf16[16,128,128]{2,1,0:T(8,128)(2,1)S(1)} %get-tuple-element.28), channel_id=1, source_target_pairs={{0,32},{32,0},{1,33},{33,1},{2,34},{34,2},{3,35},{35,3},{4,36},{36... | collective-permute-start | bytes 1572872 | tf_op jit(solution)/shard_map/ppermute | solution.py:206

commit v11 on v10

--- a/solution.py
+++ b/solution.py
@@ -195,11 +195,7 @@
         total = planes_ref[r].astype(f32)
         for q in range(1, 8):
             total = total + planes_ref[2 * q + r].astype(f32)
-        half_ref[64 * r : 64 * (r + 1), :] = total
-
-
-def flip_kernel(both_ref, out_ref):
-    out_ref[...] = both_ref[...].T
+        half_ref[:, 64 * r : 64 * (r + 1)] = total.T
 
 
 def swap(value, axis):
@@ -291,15 +287,9 @@
         compiler_params=pltpu.CompilerParams(vmem_limit_bytes=4 << 20),
         name="fold",
     )(planes)
-    both = lax.all_gather(half, "core", axis=0, tiled=True)
-    return pl.pallas_call(
-        flip_kernel,
-        in_specs=[vmem],
-        out_specs=vmem,
-        out_shape=shape((HALF, PANEL), f32),
-        compiler_params=pltpu.CompilerParams(vmem_limit_bytes=4 << 20),
-        name="flip",
-    )(both)
+    strips = half.reshape(HALF // 8, 1, 8, HALF)
+    both = lax.all_gather(strips, "core", axis=1, tiled=True)
+    return both.transpose(0, 2, 1, 3).reshape(HALF, PANEL)
 
 
 def solution(mesh):

time: 82.4 us -> 82.5 us (level)
  no operation moved by 1% of the time
where the time goes in v11:
time: 82.5 us; the launch traced here: 82.1 us
  blocking collectives  42.9 us (52%)
  starting transfers between devices  30.9 us (37%)
  Pallas kernels  5.83 us (7%)
  waiting for transfers between devices  1.53 us (2%)
    ppermute x3, starting transfers between devices, swap(): return lax.ppermute(value, axis, [(0, 1), (1, 0)])  20.6 us
    all_to_all x1, blocking collectives, shards(): lax.all_to_all(mine.reshape(2 * tiles, HALF // 2, HALF), COL + ('zl',), 0...  18.1 us
    all_to_all x1, blocking collectives, shards(): planes = lax.all_to_all(copies, Z, 0, 0, tiled=True)  16.5 us
    all_gather x1, blocking collectives, shards(): both = lax.all_gather(strips, 'core', axis=1, tiled=True)  8.33 us
    ppermute x1, starting transfers between devices, shards(): yin = lax.ppermute(yinner, COL, pairs(0))  5.57 us
    ppermute x1, starting transfers between devices, shards(): beside = lax.ppermute(xouter, ROW, pairs(1))  4.05 us
    pallas_call x1, Pallas kernels, shards(): pl.pallas_call(local_kernel, in_specs=[vmem] * 3 + [pl.BlockSpec(memory_s...  2.35 us
    pallas_call x1, Pallas kernels, shards(): pl.pallas_call(product_kernel, in_specs=[vmem] * 8, out_specs=[vmem] * 2,...  1.78 us
  transfers between devices with their start and end apart: 6, of which 1 were waited for; matrix products, arithmetic and copies ran while one was open for 0% of the time, Pallas kernels for 3%

profile of v11, /device:TPU:1, one launch (start us, length us, event | category | flops | bytes accessed | tf_op | source)
XLA Modules:
  0.0 82.1 jit_solution(479775174755639906)
XLA Ops:
  0.0 0.0 copy-start
  0.0 0.0 copy-start.1
  0.0 1.2 %collect_faces.1 = (f32[2,1152,128]{2,1,0:T(8,128)S(1)}, bf16[72,256]{1,0:T(8,128)(2,1)S(1)}, bf16[288,256]{1,0:T(8,128)(2,1)S(1)}, bf16[288,256]{1,0:T(8,128)(2...) custom-call(bf16[1152,2048]{1,0:T(8,128)(2,1)} %bitcast.15), custom_call_target="tpu_custom_call" | custom-call | tf_op jit(solution)/shard_map/collect_faces/pallas_call | solution.py:211
  1.3 16.3 %collective-permute-start.4 = (bf16[72,256]{1,0:T(8,128)(2,1)S(1)}, bf16[72,256]{1,0:T(8,128)(2,1)S(1)}, u32[]{:S(2)}, u32[]{:S(2)}) collective-permute-start(bf16[72,256]{1,0:T(8,128)(2,1)S(1)} %get-tuple-element.24), channel_id=1, source_target_pairs={{0,1},{1,0},{2,3},{3,2},{4,5},{5,4},{6,7},{7,6},{8,9},{9,8},{10,11... | collective-permute-start | bytes 110600 | tf_op jit(solution)/shard_map/ppermute | solution.py:202
  17.5 0.7 collective-permute-start
  18.2 5.6 %collective-permute-start.1 = (bf16[192,256]{1,0:T(8,128)(2,1)S(1)}, bf16[192,256]{1,0:T(8,128)(2,1)S(1)}, u32[]{:S(2)}, u32[]{:S(2)}) collective-permute-start(bf16[192,256]{1,0:T(8,128)(2,1)S(1)} %get-tuple-element.18), channel_id=1, source_target_pairs={{0,2},{4,6},{8,10},{12,14},{16,18},{20,22},{24,26},{28,30},{2,0},{... | collective-permute-start | bytes 294920 | tf_op jit(solution)/shard_map/ppermute | solution.py:227
  23.8 4.0 %collective-permute-start.2 = (bf16[288,256]{1,0:T(8,128)(2,1)S(1)}, bf16[288,256]{1,0:T(8,128)(2,1)S(1)}, u32[]{:S(2)}, u32[]{:S(2)}) collective-permute-start(bf16[288,256]{1,0:T(8,128)(2,1)S(1)} %get-tuple-element.19), channel_id=1, source_target_pairs={{32,64},{96,128},{160,192},{224,256},{288,320},{352,384},{416,448}... | collective-permute-start | bytes 442376 | tf_op jit(solution)/shard_map/ppermute | solution.py:229
  27.8 1.9 %collective-permute-start.3 = (bf16[288,256]{1,0:T(8,128)(2,1)S(1)}, bf16[288,256]{1,0:T(8,128)(2,1)S(1)}, u32[]{:S(2)}, u32[]{:S(2)}) collective-permute-start(bf16[288,256]{1,0:T(8,128)(2,1)S(1)} %get-tuple-element.20), channel_id=1, source_target_pairs={{0,32},{32,0},{1,33},{33,1},{2,34},{34,2},{3,35},{35,3},{4,36},{36... | collective-permute-start | bytes 442376 | tf_op jit(solution)/shard_map/ppermute | solution.py:202
  29.8 0.0 copy-done
  29.8 0.0 copy-done.1
  29.8 2.4 %local_stencil.1 = (f32[384,128]{1,0:T(8,128)S(1)}, f32[4,96,1152]{2,1,0:T(8,128)S(1)}, f32[1152,256]{1,0:T(8,128)S(1)}, bf16[1152,2048]{1,0:T(8,128)(2,1)S(1)}) custom-call(s32[6,4,16]{2,1,0:T(4,128)S(1)} %bitcast.14, f32[3,3,8,7]{3,2,1,0:T(8,128)S(1)} %bitcast.13, f32[2,1152,128]{2,1,0:T(8,128)S(1)} %get-tuple-element.21.panel_ref, bf16[1152,2048]{1,0:T(8,128)(2,1)} %bitcast.16), custom_call_target="tpu_custom_call" | custom-call | flops 12386304 | bytes 884736 | tf_op jit(solution)/shard_map/local_stencil/pallas_call | solution.py:231
  32.1 0.0 collective-permute-done.4.zface_ref
  32.2 0.2 edge_terms.1.term_ref
  32.3 0.0 collective-permute-done.yout_ref
  32.4 0.0 collective-permute-done.1.yin_ref
  32.4 0.0 collective-permute-done.2.beside_ref
  32.4 0.0 collective-permute-done.3.chip_ref
  32.4 1.8 %faces_and_product.1 = (f32[16,128,128]{2,1,0:T(8,128)S(1)}, bf16[16,128,128]{2,1,0:T(8,128)(2,1)S(1)}) custom-call(bf16[192,256]{1,0:T(8,128)(2,1)S(1)} %collective-permute-done.yout_ref, bf16[192,256]{1,0:T(8,128)(2,1)S(1)} %collective-permute-done.1.yin_ref, bf16[288,256]{1,0:T(8,128)(2,1)S(1)} %collective-permute-done.2.beside_ref, ...), custom_call_target="tpu_custom_call" | custom-call | flops 1207959552 | bytes 4718592 | tf_op jit(solution)/shard_map/faces_and_product/pallas_call | solution.py:261
  34.2 2.4 %collective-permute-start.5 = (bf16[16,128,128]{2,1,0:T(8,128)(2,1)S(1)}, bf16[16,128,128]{2,1,0:T(8,128)(2,1)S(1)}, u32[]{:S(2)}, u32[]{:S(2)}) collective-permute-start(bf16[16,128,128]{2,1,0:T(8,128)(2,1)S(1)} %get-tuple-element.28), channel_id=1, source_target_pairs={{0,32},{32,0},{1,33},{33,1},{2,34},{34,2},{3,35},{35,3},{4,36},{36... | collective-permute-start | bytes 1572872 | tf_op jit(solution)/shard_map/ppermute | solution.py:202
  36.6 1.5 %collective-permute-done.5 = bf16[16,128,128]{2,1,0:T(8,128)(2,1)S(1)} collective-permute-done((bf16[16,128,128]{2,1,0:T(8,128)(2,1)S(1)}, bf16[16,128,128]{2,1,0:T(8,128)(2,1)S(1)}, u32[]{:S(2)}, u32[]{:S(2)}) %collective-permute-start.5) | collective-permute-done | bytes 524320 | tf_op jit(solution)/shard_map/ppermute | solution.py:202
  38.1 0.1 add_convert_fusion
  38.2 18.1 %all_to_all.10.parts_ref = bf16[32,64,128]{2,1,0:T(8,128)(2,1)S(1)} all-to-all(bf16[32,64,128]{2,1,0:T(8,128)(2,1)S(1)} %bitcast.17), channel_id=1, replica_groups=mesh['zh'=4,'zl'=2,'core'=2,'y'=4,'x'=4,'gz'=2] {'y','x','zl'}, dimensions={0} | all-to-all | bytes 1048576 | tf_op jit(solution)/shard_map/all_to_all | solution.py:272
  56.3 0.1 near_sum.1
  56.4 16.5 %all_to_all.11.planes_ref = bf16[16,64,128]{2,1,0:T(8,128)(2,1)S(1)} all-to-all(bf16[16,64,128]{2,1,0:T(8,128)(2,1)S(1)} %near_sum.1), channel_id=1, replica_groups=mesh['zh'=4,'zl'=2,'core'=2,'y'=4,'x'=4,'gz'=2] {'gz','zh','zl'}, dimensions={0} | all-to-all | bytes 524288 | tf_op jit(solution)/shard_map/all_to_all | solution.py:281
  73.0 0.2 fold.1
  73.1 8.3 %all_gather.3 = f32[16,2,8,128]{3,2,0,1:T(8,128)S(1)} all-gather(f32[16,1,8,128]{3,2,0,1:T(8,128)S(1)} %bitcast.12), channel_id=1, replica_groups=mesh['zh'=4,'zl'=2,'core'=2,'y'=4,'x'=4,'gz'=2] {'core'}, dimensions={1}, use_global_device_ids=true | all-gather | bytes 196608 | tf_op jit(solution)/shard_map/all_gather | solution.py:291
  81.5 0.7 copy.7
Async XLA Ops:
  0.0 29.8 %copy-start = (f32[8,7,3,3]{1,0,3,2:T(8,128)S(1)}, f32[8,7,3,3]{1,0,3,2:T(8,128)}, u32[]{:S(2)}) copy-start(f32[8,7,3,3]{1,0,3,2:T(8,128)} %param.4) | copy-start | bytes 6052
  0.0 29.8 %copy-start.1 = (s32[4,6,16]{2,0,1:T(4,128)S(1)}, s32[4,6,16]{2,0,1:T(4,128)}, u32[]{:S(2)}) copy-start(s32[4,6,16]{2,0,1:T(4,128)} %param.5) | copy-start | bytes 4612
  1.3 30.9 %collective-permute-start.4 = (bf16[72,256]{1,0:T(8,128)(2,1)S(1)}, bf16[72,256]{1,0:T(8,128)(2,1)S(1)}, u32[]{:S(2)}, u32[]{:S(2)}) collective-permute-start(bf16[72,256]{1,0:T(8,128)(2,1)S(1)} %get-tuple-element.24), channel_id=1, source_target_pairs={{0,1},{1,0},{2,3},{3,2},{4,5},{5,4},{6,7},{7,6},{8,9},{9,8},{10,11... | collective-permute-start | bytes 110600 | tf_op jit(solution)/shard_map/ppermute | solution.py:202
  17.5 14.8 %collective-permute-start = (bf16[192,256]{1,0:T(8,128)(2,1)S(1)}, bf16[192,256]{1,0:T(8,128)(2,1)S(1)}, u32[]{:S(2)}, u32[]{:S(2)}) collective-permute-start(bf16[192,256]{1,0:T(8,128)(2,1)S(1)} %get-tuple-element.17), channel_id=1, source_target_pairs={{2,4},{6,8},{10,12},{14,16},{18,20},{22,24},{26,28},{4,2},{8,6},{1... | collective-permute-start | bytes 294920 | tf_op jit(solution)/shard_map/ppermute | solution.py:228
  18.2 14.2 %collective-permute-start.1 = (bf16[192,256]{1,0:T(8,128)(2,1)S(1)}, bf16[192,256]{1,0:T(8,128)(2,1)S(1)}, u32[]{:S(2)}, u32[]{:S(2)}) collective-permute-start(bf16[192,256]{1,0:T(8,128)(2,1)S(1)} %get-tuple-element.18), channel_id=1, source_target_pairs={{0,2},{4,6},{8,10},{12,14},{16,18},{20,22},{24,26},{28,30},{2,0},{... | collective-permute-start | bytes 294920 | tf_op jit(solution)/shard_map/ppermute | solution.py:227
  23.8 8.6 %collective-permute-start.2 = (bf16[288,256]{1,0:T(8,128)(2,1)S(1)}, bf16[288,256]{1,0:T(8,128)(2,1)S(1)}, u32[]{:S(2)}, u32[]{:S(2)}) collective-permute-start(bf16[288,256]{1,0:T(8,128)(2,1)S(1)} %get-tuple-element.19), channel_id=1, source_target_pairs={{32,64},{96,128},{160,192},{224,256},{288,320},{352,384},{416,448}... | collective-permute-start | bytes 442376 | tf_op jit(solution)/shard_map/ppermute | solution.py:229
  27.8 4.5 %collective-permute-start.3 = (bf16[288,256]{1,0:T(8,128)(2,1)S(1)}, bf16[288,256]{1,0:T(8,128)(2,1)S(1)}, u32[]{:S(2)}, u32[]{:S(2)}) collective-permute-start(bf16[288,256]{1,0:T(8,128)(2,1)S(1)} %get-tuple-element.20), channel_id=1, source_target_pairs={{0,32},{32,0},{1,33},{33,1},{2,34},{34,2},{3,35},{35,3},{4,36},{36... | collective-permute-start | bytes 442376 | tf_op jit(solution)/shard_map/ppermute | solution.py:202
  34.2 3.9 %collective-permute-start.5 = (bf16[16,128,128]{2,1,0:T(8,128)(2,1)S(1)}, bf16[16,128,128]{2,1,0:T(8,128)(2,1)S(1)}, u32[]{:S(2)}, u32[]{:S(2)}) collective-permute-start(bf16[16,128,128]{2,1,0:T(8,128)(2,1)S(1)} %get-tuple-element.28), channel_id=1, source_target_pairs={{0,32},{32,0},{1,33},{33,1},{2,34},{34,2},{3,35},{35,3},{4,36},{36... | collective-permute-start | bytes 1572872 | tf_op jit(solution)/shard_map/ppermute | solution.py:202
